TPU v7x, 128 devices: a whole 4x4x4 slice. The times are simulated.
128 devices in a mesh: seq: 8 (over z, core), blk: 4 (over y), tp: 4 (over x).
Axes of the slice: x: 4, y: 4, z: 4, core: 2. Of those that a mesh axis runs over, the one named last changes fastest.
Arguments:
- hidden_in: bfloat16 [16384, 1024], P(('seq', 'blk', 'tp')), may hold values from -24 to 24
- ln1_gain: float32 [1024], replicated, may hold values from 0.1 to 1.9
- ln1_bias: float32 [1024], replicated, may hold values from -3 to 3
- qkv_weight: bfloat16 [1024, 3072], replicated, may hold values from -0.1875 to 0.1875
- qv_bias: float32 [2, 1024], replicated, may hold values from -3 to 3
- out_weight: bfloat16 [1024, 1024], replicated, may hold values from -0.75 to 0.75
- out_bias: float32 [1024], replicated, may hold values from -3 to 3
- ln2_gain: float32 [1024], replicated, may hold values from 0.1 to 1.9
- ln2_bias: float32 [1024], replicated, may hold values from -3 to 3
- fc_weight: bfloat16 [1024, 4096], P(None, 'tp'), may hold values from -0.1875 to 0.1875
- fc_bias: float32 [4096], P('tp'), may hold values from -3 to 3
- proj_weight: bfloat16 [4096, 1024], P('tp'), may hold values from -0.09375 to 0.09375
- proj_bias: float32 [1024], replicated, may hold values from -3 to 3
- cotangent: float32 [16384, 1024], P(('seq', 'blk', 'tp')), may hold values from -3 to 3
Outputs:
- block_out: float32 [16384, 1024], P(('seq', 'blk', 'tp'))
- input_grad: float32 [16384, 1024], P(('seq', 'blk', 'tp'))
- ln1_gain_grad: float32 [1024], P(('seq', 'blk'))
- ln1_bias_grad: float32 [1024], P(('seq', 'blk'))
- qkv_weight_grad: float32 [1024, 3072], P(('seq', 'blk'))
- qv_bias_grad: float32 [2, 1024], P(None, ('seq', 'blk'))
- out_weight_grad: float32 [1024, 1024], P(('seq', 'blk'))
- out_bias_grad: float32 [1024], P(('seq', 'blk'))
- ln2_gain_grad: float32 [1024], P(('seq', 'blk'))
- ln2_bias_grad: float32 [1024], P(('seq', 'blk'))
- fc_weight_grad: float32 [1024, 4096], P(None, 'tp')
- fc_bias_grad: float32 [4096], P('tp')
- proj_weight_grad: float32 [4096, 1024], P('tp')
- proj_bias_grad: float32 [1024], P(('seq', 'blk'))
All inputs are finite; a program needn't handle non-finite values.
Results may differ from a plain program's by a relative error of at most 0.025.
Values may be sent and summed in bfloat16 or wider, within the bound.
A program may use at most 128 MiB of HBM per device.

v0:
```python
import math

import jax
import jax.numpy as jnp
from jax import lax
from jax.sharding import PartitionSpec as P

HEADS = 16
HEAD_DIM = 64


epsilon = 1e-05
gelu_coef = math.sqrt(2.0 / math.pi)
masked_score = -1e30


def normalize(matrix, norm_gain, norm_shift):
    row_mean = jnp.mean(matrix, axis=-1, keepdims=True)
    centered = matrix - row_mean
    variance = jnp.mean(centered * centered, axis=-1, keepdims=True)
    inverse = lax.rsqrt(variance + epsilon)
    scaled = centered * inverse
    return (scaled, inverse, scaled * norm_gain + norm_shift)


def norm_back(upstream_grad, scaled, inverse, norm_gain):
    weighted = upstream_grad * norm_gain
    first_mean = jnp.mean(weighted, axis=-1, keepdims=True)
    second_mean = jnp.mean(weighted * scaled, axis=-1, keepdims=True)
    return inverse * (weighted - first_mean - scaled * second_mean)


def gelu_pair(hidden_pre):
    tanh_arg = gelu_coef * (hidden_pre + 0.044715 * hidden_pre * hidden_pre * hidden_pre)
    tanh_value = jnp.tanh(tanh_arg)
    gelu_value = 0.5 * hidden_pre * (1.0 + tanh_value)
    gelu_slope = 0.5 * (1.0 + tanh_value) + 0.5 * hidden_pre * (
        1.0 - tanh_value * tanh_value
    ) * gelu_coef * (1.0 + 3.0 * 0.044715 * hidden_pre * hidden_pre)
    return (gelu_value, gelu_slope)


def per_device(
    hidden_in,
    ln1_gain,
    ln1_bias,
    qkv_weight,
    qv_bias,
    out_weight,
    out_bias,
    ln2_gain,
    ln2_bias,
    fc_weight,
    fc_bias,
    proj_weight,
    proj_bias,
    cotangent,
):
    local_tokens, model_width = hidden_in.shape
    seq_count = lax.axis_size("seq")
    cycle_size = lax.axis_size(("blk", "tp"))
    local_heads = HEADS // seq_count
    head_dim = HEAD_DIM
    query_rows = seq_count * local_tokens
    head_cols = model_width // seq_count
    score_scale = 1.0 / math.sqrt(head_dim)
    hidden_f = hidden_in.astype(jnp.float32)
    scaled_one, inverse_one, normed_one = normalize(hidden_f, ln1_gain, ln1_bias)
    normed_bf = normed_one.astype(jnp.bfloat16)
    weight_three = qkv_weight.reshape(model_width, 3, model_width)
    bias_three = jnp.stack([qv_bias[0], jnp.zeros_like(qv_bias[0]), qv_bias[1]])
    projected = jnp.einsum(
        "td,dcf->ctf", normed_bf, weight_three, preferred_element_type=jnp.float32
    )
    qkv_tokens = (projected + bias_three[:, None, :]).astype(jnp.bfloat16)
    qkv_heads = lax.all_to_all(qkv_tokens, "seq", split_axis=2, concat_axis=1, tiled=True)
    query_heads = qkv_heads[0]
    key_heads = qkv_heads[1]
    value_heads = qkv_heads[2]
    cycle_index = lax.axis_index(("blk", "tp"))
    local_index = jnp.arange(query_rows, dtype=jnp.int32)
    query_place = (
        local_index // local_tokens * cycle_size + cycle_index
    ) * local_tokens + local_index % local_tokens

    def key_positions(first_key, key_count):
        gathered = first_key + jnp.arange(key_count, dtype=jnp.int32)
        within = gathered % query_rows
        return (
            within // local_tokens * cycle_size + gathered // query_rows
        ) * local_tokens + within % local_tokens

    def split_heads(matrix):
        return matrix.reshape(matrix.shape[0], local_heads, head_dim)

    def block_scores(low_row, key_block):
        return (
            jnp.einsum(
                "qhd,khd->hqk",
                split_heads(query_heads[low_row:]),
                split_heads(key_block),
                preferred_element_type=jnp.float32,
            )
            * score_scale
        )

    def visible_of(low_row, key_block, first_key):
        return (
            query_place[low_row:, None] >= key_positions(first_key, key_block.shape[0])[None, :]
        )[None]

    def forward_update(softmax_state, key_block, value_block, first_key, low_row):
        run_max, run_sum, run_acc = softmax_state
        visible = visible_of(low_row, key_block, first_key)
        scores = jnp.where(visible, block_scores(low_row, key_block), masked_score)
        old_max = run_max[:, low_row:]
        new_max = jnp.maximum(old_max, jnp.max(scores, axis=2))
        rescale = jnp.exp(old_max - new_max)
        attn_prob = jnp.where(visible, jnp.exp(scores - new_max[:, :, None]), 0.0)
        new_sum = run_sum[:, low_row:] * rescale + jnp.sum(attn_prob, axis=2)
        weighted_values = jnp.einsum(
            "hqk,khd->qhd",
            attn_prob.astype(jnp.bfloat16),
            split_heads(value_block),
            preferred_element_type=jnp.float32,
        ).reshape(query_rows - low_row, head_cols)
        new_acc = run_acc[low_row:] * jnp.repeat(rescale.T, head_dim, axis=1) + weighted_values
        return (
            run_max.at[:, low_row:].set(new_max),
            run_sum.at[:, low_row:].set(new_sum),
            run_acc.at[low_row:].set(new_acc),
        )

    def by_segments(update, carry_state, key_shard, value_shard, first_key):
        for segment in range(seq_count):
            low_row = segment * local_tokens
            carry_state = update(
                carry_state,
                key_shard[low_row : low_row + local_tokens],
                value_shard[low_row : low_row + local_tokens],
                first_key + low_row,
                low_row,
            )
        return carry_state

    def fold_with(update, carry_state, shard_pair):
        key_piece, value_piece = shard_pair
        piece_rows = key_piece.shape[0]

        def shard_step(shard_number, inner_state):
            offset = shard_number * query_rows
            key_shard = lax.dynamic_slice_in_dim(key_piece, offset, query_rows, 0)
            value_shard = lax.dynamic_slice_in_dim(value_piece, offset, query_rows, 0)
            return by_segments(update, inner_state, key_shard, value_shard, offset)

        return lax.fori_loop(0, piece_rows // query_rows, shard_step, carry_state)

    initial_state = (
        jnp.full((local_heads, query_rows), masked_score, jnp.float32),
        jnp.zeros((local_heads, query_rows), jnp.float32),
        jnp.zeros((query_rows, head_cols), jnp.float32),
    )
    cycle_init = (initial_state,)
    run_max, run_sum, run_acc = fold_with(
        forward_update,
        cycle_init[0],
        (
            lax.all_gather(key_heads, ("blk", "tp"), axis=0, tiled=True),
            lax.all_gather(value_heads, ("blk", "tp"), axis=0, tiled=True),
        ),
    )
    context_heads = (run_acc / jnp.repeat(run_sum.T, head_dim, axis=1)).astype(jnp.bfloat16)
    log_total = run_max + jnp.log(run_sum)
    context_tokens = lax.all_to_all(context_heads, "seq", split_axis=0, concat_axis=1, tiled=True)
    residual = (
        hidden_f
        + jnp.dot(context_tokens, out_weight, preferred_element_type=jnp.float32)
        + out_bias
    )
    scaled_two, inverse_two, normed_two = normalize(residual, ln2_gain, ln2_bias)
    normed_two_bf = normed_two.astype(jnp.bfloat16)
    gathered_norm = lax.all_gather(normed_two_bf, "tp", axis=0, tiled=True)
    hidden_pre = jnp.dot(gathered_norm, fc_weight, preferred_element_type=jnp.float32) + fc_bias
    gelu_value, gelu_slope = gelu_pair(hidden_pre)
    activation = gelu_value.astype(jnp.bfloat16)
    mlp_out = lax.psum_scatter(
        jnp.dot(activation, proj_weight, preferred_element_type=jnp.float32).astype(jnp.bfloat16),
        "tp",
        scatter_dimension=0,
        tiled=True,
    ).astype(jnp.float32)
    block_out = residual + mlp_out + proj_bias
    cot_bf = cotangent.astype(jnp.bfloat16)
    gathered_cot = lax.all_gather(cot_bf, "tp", axis=0, tiled=True)
    hidden_grad = (
        jnp.dot(gathered_cot, proj_weight.T, preferred_element_type=jnp.float32) * gelu_slope
    )
    hidden_grad_bf = hidden_grad.astype(jnp.bfloat16)
    proj_weight_grad = jnp.einsum(
        "tf,td->fd", activation, gathered_cot, preferred_element_type=jnp.float32
    )
    fc_weight_grad = jnp.einsum(
        "td,tf->df", gathered_norm, hidden_grad_bf, preferred_element_type=jnp.float32
    )
    fc_bias_grad = jnp.sum(hidden_grad, axis=0)
    normed_two_grad = lax.psum_scatter(
        jnp.dot(hidden_grad_bf, fc_weight.T, preferred_element_type=jnp.float32).astype(
            jnp.bfloat16
        ),
        "tp",
        scatter_dimension=0,
        tiled=True,
    ).astype(jnp.float32)
    residual_grad = cotangent + norm_back(normed_two_grad, scaled_two, inverse_two, ln2_gain)
    residual_grad_bf = residual_grad.astype(jnp.bfloat16)
    context_grad = jnp.dot(
        residual_grad_bf, out_weight.T, preferred_element_type=jnp.float32
    ).astype(jnp.bfloat16)
    context_grad_heads = lax.all_to_all(
        context_grad, "seq", split_axis=1, concat_axis=0, tiled=True
    )
    delta_rows = jnp.sum(
        split_heads(context_grad_heads).astype(jnp.float32)
        * split_heads(context_heads).astype(jnp.float32),
        axis=2,
    ).T

    def backward_update(grad_state, key_block, value_block, first_key, low_row):
        query_grad, key_grad, value_grad = grad_state
        visible = visible_of(low_row, key_block, first_key)
        attn_prob = jnp.where(
            visible, jnp.exp(block_scores(low_row, key_block) - log_total[:, low_row:, None]), 0.0
        )
        grad_rows = split_heads(context_grad_heads[low_row:])
        prob_grad = jnp.einsum(
            "qhd,khd->hqk", grad_rows, split_heads(value_block), preferred_element_type=jnp.float32
        )
        score_grad = (attn_prob * (prob_grad - delta_rows[:, low_row:, None]) * score_scale).astype(
            jnp.bfloat16
        )
        query_part = jnp.einsum(
            "hqk,khd->qhd", score_grad, split_heads(key_block), preferred_element_type=jnp.float32
        ).reshape(query_rows - low_row, head_cols)
        key_part = jnp.einsum(
            "hqk,qhd->khd",
            score_grad,
            split_heads(query_heads[low_row:]),
            preferred_element_type=jnp.float32,
        ).reshape(key_block.shape[0], head_cols)
        value_part = jnp.einsum(
            "hqk,qhd->khd",
            attn_prob.astype(jnp.bfloat16),
            grad_rows,
            preferred_element_type=jnp.float32,
        ).reshape(key_block.shape[0], head_cols)
        return (
            query_grad.at[low_row:].add(query_part),
            lax.dynamic_update_slice_in_dim(key_grad, key_part, first_key, 0),
            lax.dynamic_update_slice_in_dim(value_grad, value_part, first_key, 0),
        )

    grad_init = (
        jnp.zeros((query_rows, head_cols), jnp.float32),
        jnp.zeros((cycle_size * query_rows, head_cols), jnp.float32),
        jnp.zeros((cycle_size * query_rows, head_cols), jnp.float32),
    )
    query_grad, key_grad, value_grad = fold_with(
        backward_update,
        grad_init,
        (
            lax.all_gather(key_heads, ("blk", "tp"), axis=0, tiled=True),
            lax.all_gather(value_heads, ("blk", "tp"), axis=0, tiled=True),
        ),
    )
    key_own, value_own = (
        lax.psum_scatter(
            key_grad.astype(jnp.bfloat16), ("blk", "tp"), scatter_dimension=0, tiled=True
        ).astype(jnp.float32),
        lax.psum_scatter(
            value_grad.astype(jnp.bfloat16), ("blk", "tp"), scatter_dimension=0, tiled=True
        ).astype(jnp.float32),
    )
    head_grads = jnp.stack([query_grad, key_own, value_own]).astype(jnp.bfloat16)
    token_grads = lax.all_to_all(head_grads, "seq", split_axis=1, concat_axis=2, tiled=True)
    query_bias_grad = jnp.sum(token_grads[0].astype(jnp.float32), axis=0)
    value_bias_grad = jnp.sum(token_grads[2].astype(jnp.float32), axis=0)
    normed_one_grad = jnp.einsum(
        "ctf,dcf->td", token_grads, weight_three, preferred_element_type=jnp.float32
    )
    input_grad = residual_grad + norm_back(normed_one_grad, scaled_one, inverse_one, ln1_gain)
    vectors = jnp.stack(
        [
            jnp.sum(normed_one_grad * scaled_one, axis=0),
            jnp.sum(normed_one_grad, axis=0),
            query_bias_grad,
            value_bias_grad,
            jnp.sum(residual_grad, axis=0),
            jnp.sum(normed_two_grad * scaled_two, axis=0),
            jnp.sum(normed_two_grad, axis=0),
            jnp.sum(cotangent, axis=0),
        ],
        axis=1,
    )
    qkv_weight_grad = jnp.einsum(
        "td,ctf->dcf", normed_bf, token_grads, preferred_element_type=jnp.float32
    ).reshape(model_width, 3 * model_width)
    out_weight_grad = jnp.einsum(
        "tc,td->cd", context_tokens, residual_grad_bf, preferred_element_type=jnp.float32
    )
    qkv_part, out_part, vector_part = (
        lax.psum_scatter(
            qkv_weight_grad.astype(jnp.bfloat16), ("seq", "blk"), scatter_dimension=0, tiled=True
        ).astype(jnp.float32),
        lax.psum_scatter(
            out_weight_grad.astype(jnp.bfloat16), ("seq", "blk"), scatter_dimension=0, tiled=True
        ).astype(jnp.float32),
        lax.psum_scatter(
            vectors.astype(jnp.bfloat16), ("seq", "blk"), scatter_dimension=0, tiled=True
        ).astype(jnp.float32),
    )
    qkv_part, out_part, vector_part = (
        lax.psum(qkv_part.astype(jnp.bfloat16), "tp").astype(jnp.float32),
        lax.psum(out_part.astype(jnp.bfloat16), "tp").astype(jnp.float32),
        lax.psum(vector_part.astype(jnp.bfloat16), "tp").astype(jnp.float32),
    )
    fc_weight_grad, fc_bias_grad, proj_weight_grad = (
        lax.psum(fc_weight_grad.astype(jnp.bfloat16), ("seq", "blk")).astype(jnp.float32),
        lax.psum(fc_bias_grad.astype(jnp.bfloat16), ("seq", "blk")).astype(jnp.float32),
        lax.psum(proj_weight_grad.astype(jnp.bfloat16), ("seq", "blk")).astype(jnp.float32),
    )
    qv_bias_grad = jnp.stack([vector_part[:, 2], vector_part[:, 3]])
    return (
        block_out,
        input_grad,
        vector_part[:, 0],
        vector_part[:, 1],
        qkv_part,
        qv_bias_grad,
        out_part,
        vector_part[:, 4],
        vector_part[:, 5],
        vector_part[:, 6],
        fc_weight_grad,
        fc_bias_grad,
        proj_weight_grad,
        vector_part[:, 7],
    )


def solution(mesh):
    return jax.shard_map(
        per_device,
        mesh=mesh,
        in_specs=(
            P(("seq", "blk", "tp"), None),
            P(),
            P(),
            P(),
            P(),
            P(),
            P(),
            P(),
            P(),
            P(None, "tp"),
            P("tp"),
            P("tp", None),
            P(),
            P(("seq", "blk", "tp"), None),
        ),
        out_specs=(
            P(("seq", "blk", "tp"), None),
            P(("seq", "blk", "tp"), None),
            P(("seq", "blk")),
            P(("seq", "blk")),
            P(("seq", "blk"), None),
            P(None, ("seq", "blk")),
            P(("seq", "blk"), None),
            P(("seq", "blk")),
            P(("seq", "blk")),
            P(("seq", "blk")),
            P(None, "tp"),
            P("tp"),
            P("tp", None),
            P(("seq", "blk")),
        ),
        check_vma=False,
    )
```

profile of v0, /device:TPU:1, one launch (start us, length us, event | category | flops | bytes accessed | tf_op | source)
XLA Modules:
  0.0 1486.9 jit_solution(16899424603222186177)
XLA Ops:
  10.5 8.7 copy.287
  19.4 5.9 fusion.199
  27.6 21.9 %all_to_all.71 = bf16[3,128,1024]{1,0,2:T(4,128)(2,1)S(1)} all-to-all(bf16[3,128,1024]{1,0,2:T(4,128)(2,1)} %copy.289), channel_id=1, replica_groups=mesh['seq'=8,'blk'=4,'tp'=4] {'seq'}, dimensions={2} | all-to-all | bytes 1572864 | tf_op jit(solution)/shard_map/all_to_all | solution.py:76
  57.9 45.3 %all-gather.7.cloned.1.call-done = bf16[16384,128]{0,1:T(8,128)(2,1)} async-done(((bf16[1024,128]{0,1:T(8,128)(2,1)}), bf16[16384,128]{0,1:T(8,128)(2,1)}) %all-gather.7.cloned.1.call-update) | async-done | bytes 4194320 | tf_op jit(solution)/shard_map/all_gather | solution.py:169
  103.2 53.9 %all-gather.5.cloned.1.call-done = bf16[16384,128]{0,1:T(8,128)(2,1)} async-done(((bf16[1024,128]{0,1:T(8,128)(2,1)}), bf16[16384,128]{0,1:T(8,128)(2,1)}) %all-gather.5.cloned.1.call-update) | async-done | bytes 4194320 | tf_op jit(solution)/shard_map/all_gather | solution.py:168
  157.2 220.2 %while.112 = (s32[]{:T(128)}, f32[2,1024]{1,0:T(2,128)S(1)}, f32[2,1024]{1,0:T(2,128)S(1)}, f32[1024,128]{0,1:T(8,128)S(1)}, s32[1024]{0:T(1024)S(1)}, /*index=5...) while((s32[]{:T(128)}, f32[2,1024]{1,0:T(2,128)S(1)}, ...), condition=%wide.region_26.27_spmd, body=%wide.region_9.26_spmd.sunk | while | flops 314464256 | bytes 33136192 | solution.py:156
  379.3 11.4 all_to_all.72
  397.1 19.1 %all-gather.9.cloned.1.call-done = bf16[512,1024]{1,0:T(8,128)(2,1)} async-done(((bf16[128,1024]{1,0:T(8,128)(2,1)}), bf16[512,1024]{1,0:T(8,128)(2,1)}) %all-gather.9.cloned.1.call-update) | async-done | bytes 1048592 | tf_op jit(solution)/shard_map/all_gather | solution.py:182
  416.2 4.6 fusion.274
  420.8 21.8 %all-gather.11.cloned.1.call-done = bf16[512,1024]{1,0:T(8,128)(2,1)} async-done(((bf16[128,1024]{1,0:T(8,128)(2,1)}), bf16[512,1024]{1,0:T(8,128)(2,1)}) %all-gather.11.cloned.1.call-update) | async-done | bytes 1048592 | tf_op jit(solution)/shard_map/all_gather | solution.py:194
  442.6 4.4 fusion.257
  454.5 19.4 %reduce-scatter.12.cloned.1.call-done = bf16[128,1024]{1,0:T(8,128)(2,1)} async-done(((bf16[512,1024]{1,0:T(8,128)(2,1)}), bf16[128,1024]{1,0:T(8,128)(2,1)}) %reduce-scatter.12.cloned.1.call-update) | async-done | bytes 262160 | tf_op jit(solution)/shard_map/reduce_scatter | solution.py:206
  475.1 25.0 %reduce-scatter.10.cloned.1.call-done = bf16[128,1024]{1,0:T(8,128)(2,1)} async-done(((bf16[512,1024]{1,0:T(8,128)(2,1)}), bf16[128,1024]{1,0:T(8,128)(2,1)}) %reduce-scatter.10.cloned.1.call-update) | async-done | bytes 262160 | tf_op jit(solution)/shard_map/reduce_scatter | solution.py:186
  504.9 6.4 all-to-all-start.2
  511.5 6.3 all-to-all-done.2
  523.5 378.5 %while.113 = (s32[]{:T(128)}, f32[1024,128]{0,1:T(8,128)S(1)}, bf16[16384,128]{0,1:T(8,128)(2,1)}, bf16[16384,128]{0,1:T(8,128)(2,1)}, bf16[16384,128]{0,1:T(8,1...) while((s32[]{:T(128)}, f32[1024,128]{0,1:T(8,128)S(1)}, ...), condition=%wide.region_35.36_spmd, body=%wide.region_34.35_spmd.sunk | while | flops 765635584 | bytes 45661068 | solution.py:156
  902.0 6.4 copy.302
  908.5 6.4 copy.301
  923.3 59.4 %reduce-scatter.16.cloned.1.call-done = bf16[1024,128]{1,0:T(8,128)(2,1)} async-done(((bf16[16384,128]{1,0:T(8,128)(2,1)}), bf16[1024,128]{1,0:T(8,128)(2,1)}) %reduce-scatter.16.cloned.1.call-update) | async-done | bytes 262160 | tf_op jit(solution)/shard_map/reduce_scatter | solution.py:279
  982.6 81.2 %reduce-scatter.14.cloned.1.call-done = bf16[1024,128]{1,0:T(8,128)(2,1)} async-done(((bf16[16384,128]{1,0:T(8,128)(2,1)}), bf16[1024,128]{1,0:T(8,128)(2,1)}) %reduce-scatter.14.cloned.1.call-update) | async-done | bytes 262160 | tf_op jit(solution)/shard_map/reduce_scatter | solution.py:276
  1066.6 6.7 all-to-all-start.3
  1073.5 18.7 %all-to-all-done.3 = bf16[3,1024,128]{2,0,1:T(4,128)(2,1)S(1)} async-done(((bf16[3,1024,128]{2,0,1:T(4,128)(2,1)}), bf16[3,1024,128]{2,0,1:T(4,128)(2,1)S(1)}, u32[]{:S(2)}, u32[]{:S(2)}) %all-to-all-start.3) | async-done | bytes 786464 | tf_op jit(solution)/shard_map/all_to_all | solution.py:284
  1095.6 4.1 fusion.216
  1103.5 4.6 convolution_convert_fusion
  1108.1 61.0 %psum.46 = bf16[1024]{0:T(1024)(128)(2,1)S(1)} all-reduce(bf16[1024]{0:T(1024)(128)(2,1)S(1)} %get-tuple-element.1920), channel_id=1, replica_groups=mesh['seq'=8,'blk'=4,'tp'=4] {'seq','blk'}, use_global_device_ids=true, to_apply=%region_56.57 | all-reduce | flops 1024 | bytes 4096 | tf_op jit(solution)/shard_map/psum | solution.py:328
  1169.7 14.2 all-reduce.5.cloned.1.call-done
  1183.9 4.2 convert_element_type.415
  1191.7 70.7 %reduce-scatter.22.cloned.1.call-done = bf16[32,8]{1,0:T(8,128)(2,1)} async-done(((bf16[1024,8]{1,0:T(8,128)(2,1)}), bf16[32,8]{1,0:T(8,128)(2,1)}) %reduce-scatter.22.cloned.1.call-update) | async-done | bytes 528
  1263.2 8.7 psum.42
  1271.9 72.7 %reduce-scatter.20.cloned.1.call-done = bf16[32,1024]{1,0:T(8,128)(2,1)} async-done(((bf16[1024,1024]{1,0:T(8,128)(2,1)}), bf16[32,1024]{1,0:T(8,128)(2,1)}) %reduce-scatter.20.cloned.1.call-update) | async-done | bytes 65552 | tf_op jit(solution)/shard_map/reduce_scatter | solution.py:314
  1344.6 89.1 %reduce-scatter.18.cloned.1.call-done = bf16[32,3072]{1,0:T(8,128)(2,1)} async-done(((bf16[1024,3072]{1,0:T(8,128)(2,1)}), bf16[32,3072]{1,0:T(8,128)(2,1)}) %reduce-scatter.18.cloned.1.call-update) | async-done | bytes 196624 | tf_op jit(solution)/shard_map/reduce_scatter | solution.py:311
  1434.8 41.9 %all-reduce.7.cloned.1.call-done = (bf16[32,3072]{1,0:T(8,128)(2,1)}, bf16[32,1024]{1,0:T(8,128)(2,1)}) async-done(((bf16[32,3072]{1,0:T(8,128)(2,1)}, bf16[32,1024]{1,0:T(8,128)(2,1)}), (bf16[32,3072]{1,0:T(8,128)(2,1)}, bf16[32,1024]{1,0:T(8,128)(2,1)})) %all-reduce.7.cloned.1.call-update) | async-done | bytes 262160 | tf_op jit(solution)/shard_map/psum | solution.py:322
  (3241 shorter events, 650.0 us)
Async XLA Ops:
  7.2 435.5 %copy-start = (bf16[1024,1024]{1,0:T(8,128)(2,1)S(1)}, bf16[1024,1024]{1,0:T(8,128)(2,1)}, u32[]{:S(2)}) copy-start(bf16[1024,1024]{1,0:T(8,128)(2,1)} %param.101) | copy-start | bytes 6291460
  7.2 96.1 %all-gather.7.cloned.1.call-start = ((), (), s32[]{:S(2)}) async-start(), calls=%async_computation.12 | async-start | bytes 4456448 | tf_op jit(solution)/shard_map/all_gather | solution.py:169
  8.5 10.9 copy-start.16
  9.6 9.7 copy-start.18
  10.4 8.9 copy-start.2
  10.4 8.9 copy-start.11
  10.5 8.9 copy-start.13
  51.8 105.4 %all-gather.5.cloned.1.call-start = ((), (), s32[]{:S(2)}) async-start(), calls=%async_computation.11 | async-start | bytes 4456448 | tf_op jit(solution)/shard_map/all_gather | solution.py:168
  52.9 363.3 %all-gather.9.cloned.1.call-start = ((), (), s32[]{:S(2)}) async-start(), calls=%async_computation.13 | async-start | bytes 1310720 | tf_op jit(solution)/shard_map/all_gather | solution.py:182
  377.4 14.2 copy-start.20
  394.9 47.7 %all-gather.11.cloned.1.call-start = ((), (), s32[]{:S(2)}) async-start(), calls=%async_computation.15 | async-start | bytes 1310720 | tf_op jit(solution)/shard_map/all_gather | solution.py:194
  397.1 45.6 %copy-start.26 = (f32[1024]{0:T(1024)S(1)}, f32[1024]{0:T(1024)}, u32[]{:S(2)}) copy-start(f32[1024]{0:T(1024)} %param.100) | copy-start | bytes 12292
  397.1 76.8 %reduce-scatter.12.cloned.1.call-start = ((), (), s32[]{:S(2)}) async-start(), calls=%async_computation.16 | async-start | bytes 1310720 | tf_op jit(solution)/shard_map/reduce_scatter | solution.py:206
  442.6 5.4 copy-start.23
  450.4 49.8 %copy-start.22 = (f32[1024]{0:T(1024)S(1)}, f32[1024]{0:T(1024)}, u32[]{:S(2)}) copy-start(f32[1024]{0:T(1024)} %param.102) | copy-start | bytes 12292
  450.4 49.8 %reduce-scatter.10.cloned.1.call-start = ((), (), s32[]{:S(2)}) async-start(), calls=%async_computation.14 | async-start | bytes 1310720 | tf_op jit(solution)/shard_map/reduce_scatter | solution.py:186
  454.5 48.7 %copy-start.3 = (bf16[1024,1024]{1,0:T(8,128)(2,1)S(1)}, bf16[1024,1024]{1,0:T(8,128)(2,1)}, u32[]{:S(2)}) copy-start(bf16[1024,1024]{1,0:T(8,128)(2,1)} %param.95) | copy-start | bytes 6291460
  504.9 12.9 all-to-all-start.2
  511.3 7.2 copy-start.8
  511.3 471.3 %reduce-scatter.16.cloned.1.call-start = ((), (), s32[]{:S(2)}) async-start(), calls=%async_computation.18 | async-start | bytes 4456448 | tf_op jit(solution)/shard_map/reduce_scatter | solution.py:279
  908.4 155.4 %reduce-scatter.14.cloned.1.call-start = ((), (), s32[]{:S(2)}) async-start(), calls=%async_computation.17 | async-start | bytes 4456448 | tf_op jit(solution)/shard_map/reduce_scatter | solution.py:276
  914.9 269.1 %all-reduce.5.cloned.1.call-start = ((), (), s32[]{:S(2)}) async-start(), calls=%async_computation.22 | async-start | bytes 8388608 | tf_op jit(solution)/shard_map/psum | solution.py:327
  1064.9 8.4 copy-start.7
  1066.6 25.6 %all-to-all-start.3 = ((bf16[3,1024,128]{2,0,1:T(4,128)(2,1)}), bf16[3,1024,128]{2,0,1:T(4,128)(2,1)S(1)}, u32[]{:S(2)}, u32[]{:S(2)}) async-start(bf16[3,1024,128]{2,0,1:T(4,128)(2,1)} %copy.303), calls=%async_computation.7 | async-start | bytes 2097152 | tf_op jit(solution)/shard_map/all_to_all | solution.py:284
  1073.3 189.1 %reduce-scatter.22.cloned.1.call-start = ((), (), s32[]{:S(2)}) async-start(), calls=%async_computation.21 | async-start | bytes 270336
  1073.3 22.2 %copy-start.12 = (f32[1024]{0:T(1024)S(1)}, f32[1024]{0:T(1024)}, u32[]{:S(2)}) copy-start(f32[1024]{0:T(1024)} %param.91) | copy-start | bytes 12292
  1073.3 22.2 %copy-start.17 = (f32[128]{0:T(128)S(1)}, f32[128]{0:T(128)}, u32[]{:S(2)}) copy-start(f32[128]{0:T(128)} %copy-done.16) | copy-start | bytes 1540
  1073.3 22.2 %copy-start.19 = (f32[128]{0:T(128)S(1)}, f32[128]{0:T(128)}, u32[]{:S(2)}) copy-start(f32[128]{0:T(128)} %copy-done.18) | copy-start | bytes 1540
  1100.7 243.8 %reduce-scatter.20.cloned.1.call-start = ((), (), s32[]{:S(2)}) async-start(), calls=%async_computation.20 | async-start | bytes 2162688 | tf_op jit(solution)/shard_map/reduce_scatter | solution.py:314
  1102.8 330.8 %reduce-scatter.18.cloned.1.call-start = ((), (), s32[]{:S(2)}) async-start(), calls=%async_computation.19 | async-start | bytes 6488064 | tf_op jit(solution)/shard_map/reduce_scatter | solution.py:311
  1108.1 368.6 %all-reduce.7.cloned.1.call-start = ((), (), s32[]{:S(2)}) async-start(), calls=%async_computation.23 | async-start | bytes 524288 | tf_op jit(solution)/shard_map/psum | solution.py:322
  1188.1 291.8 %copy-start.1 = (bf16[1024,1024]{1,0:T(8,128)(2,1)S(1)}, bf16[1024,1024]{1,0:T(8,128)(2,1)}, u32[]{:S(2)}) copy-start(bf16[1024,1024]{1,0:T(8,128)(2,1)} %param.101) | copy-start | bytes 6291460
  (12 other events, 34.0 us)
Sparse Core Ops, SparseCore 0:
  51.9 51.3 all-gather.6
  106.0 51.1 all-gather.4
  395.1 21.1 all-gather.8
  418.3 24.2 all-gather.10
  450.5 23.3 reduce-scatter.11
  476.8 23.2 reduce-scatter.9
  908.5 74.0 reduce-scatter.15
  986.9 76.8 reduce-scatter.13
  1067.8 116.0 all-reduce.4
  1187.8 74.5 reduce-scatter.21
  1266.0 78.5 reduce-scatter.19
  1348.1 85.4 reduce-scatter.17
  1436.3 40.3 all-reduce.6
where the time goes:
time: 1500 us; the launch traced here: 1490 us
  waiting for transfers between devices  639 us (43%)
  matrix products  276 us (18%)
  local copies, waits for them, and re-layouts  249 us (17%)
  other arithmetic  174 us (12%)
  blocking collectives  103 us (7%)
  loops' own time  17.9 us (1%)
    reduce_scatter x1, waiting for transfers between devices, per_device(): lax.psum_scatter(qkv_weight_grad.astype(jnp.bfloat16), ('seq', 'blk'), sc...  89.1 us
    dot_general x256, matrix products, block_scores(): jnp.einsum('qhd,khd->hqk', split_heads(query_heads[low_row:]), split_head...  82.9 us
    reduce_scatter x1, waiting for transfers between devices, per_device(): lax.psum_scatter(key_grad.astype(jnp.bfloat16), ('blk', 'tp'), scatter_di...  81.2 us
    dynamic_update_slice x128, local copies, waits for them, and re-layouts, backward_update(): lax.dynamic_update_slice_in_dim(value_grad, value_part, first_key, 0)  79.2 us
    scatter x112, other arithmetic, forward_update(): run_sum.at[:, low_row:].set(new_sum)  75 us
    reduce_scatter x1, waiting for transfers between devices, per_device(): lax.psum_scatter(out_weight_grad.astype(jnp.bfloat16), ('seq', 'blk'), sc...  72.7 us
    unnamed x14, waiting for transfers between devices  70.9 us
    dynamic_update_slice x112, local copies, waits for them, and re-layouts, backward_update(): lax.dynamic_update_slice_in_dim(key_grad, key_part, first_key, 0)  69 us
  transfers between devices with their start and end apart: 15, of which 15 were waited for; matrix products, arithmetic and copies ran while one was open for 4% of the time, Pallas kernels for 0%

commit v1 on v0

v1 whole, which is shorter than its diff:
```python
import functools
import math

import jax
import jax.numpy as jnp
from jax import lax
from jax.experimental import pallas as pl
from jax.experimental.pallas import tpu as pltpu
from jax.sharding import PartitionSpec as P

HEAD_DIM = 64
TOKENS = 128
SEG = 8
KEY_BLOCKS = 8

epsilon = 1e-05
gelu_coef = math.sqrt(2.0 / math.pi)
masked_score = -1e30
f32, bf16 = jnp.float32, jnp.bfloat16


def normalize(matrix, norm_gain, norm_shift):
    row_mean = jnp.mean(matrix, axis=-1, keepdims=True)
    centered = matrix - row_mean
    variance = jnp.mean(centered * centered, axis=-1, keepdims=True)
    inverse = lax.rsqrt(variance + epsilon)
    scaled = centered * inverse
    return (scaled, inverse, scaled * norm_gain + norm_shift)


def norm_back(upstream_grad, scaled, inverse, norm_gain):
    weighted = upstream_grad * norm_gain
    first_mean = jnp.mean(weighted, axis=-1, keepdims=True)
    second_mean = jnp.mean(weighted * scaled, axis=-1, keepdims=True)
    return inverse * (weighted - first_mean - scaled * second_mean)


def gelu_pair(hidden_pre):
    tanh_arg = gelu_coef * (hidden_pre + 0.044715 * hidden_pre * hidden_pre * hidden_pre)
    tanh_value = jnp.tanh(tanh_arg)
    gelu_value = 0.5 * hidden_pre * (1.0 + tanh_value)
    gelu_slope = 0.5 * (1.0 + tanh_value) + 0.5 * hidden_pre * (
        1.0 - tanh_value * tanh_value
    ) * gelu_coef * (1.0 + 3.0 * 0.044715 * hidden_pre * hidden_pre)
    return (gelu_value, gelu_slope)


def dot(a, b):
    return jnp.dot(a, b, preferred_element_type=f32)


def block_diagonal(rows, scale):
    turned = rows.astype(f32).T * scale
    upper = lax.broadcasted_iota(jnp.int32, turned.shape, 0) < HEAD_DIM
    zero = jnp.zeros_like(turned)
    return jnp.concatenate(
        [jnp.where(upper, turned, zero), jnp.where(upper, zero, turned)], axis=1
    ).astype(bf16)


def heads_back(stacked):
    lower = lax.broadcasted_iota(jnp.int32, (TOKENS, TOKENS), 1) < HEAD_DIM
    return jnp.where(lower, stacked[:, :TOKENS].T, stacked[:, TOKENS:].T).astype(bf16)


def visible_keys(place, step, keys):
    key = lax.broadcasted_iota(jnp.int32, (keys, 2 * TOKENS), 0) + step * keys
    query = lax.broadcasted_iota(jnp.int32, (keys, 2 * TOKENS), 1) % TOKENS + place * TOKENS
    return key <= query


def over_queries(place, key_group, step, update, keys):
    @pl.when(step * KEY_BLOCKS <= place)
    def _():
        update(key_group, visible_keys(place, step, keys))

    later = SEG - 1 - key_group
    odd = later % 2

    @pl.when(odd == 1)
    def _():
        update(key_group + 1, None)

    def pair(index, carry):
        group = key_group + 1 + odd + 2 * index
        update(group, None)
        update(group + 1, None)
        return carry

    lax.fori_loop(0, later // 2, pair, 0)


def forward_kernel(cycle, q_ref, kv_ref, ctx_ref, lse_ref, qb, m_s, l_s, acc):
    place = lax.axis_index("blk") * lax.axis_size("tp") + lax.axis_index("tp")
    keys = KEY_BLOCKS * TOKENS
    steps = cycle // KEY_BLOCKS
    for group in range(SEG):
        qb[group] = block_diagonal(q_ref[group], 1.0 / math.sqrt(HEAD_DIM))
    m_s[...] = jnp.full(m_s.shape, masked_score, f32)
    l_s[...] = jnp.zeros(l_s.shape, f32)
    acc[...] = jnp.zeros(acc.shape, f32)

    def key_step(index, carry):
        key_group, step = index // steps, index % steps
        k = kv_ref[pl.ds(step * KEY_BLOCKS, KEY_BLOCKS), key_group, 0].reshape(keys, TOKENS)
        v_t = kv_ref[pl.ds(step * KEY_BLOCKS, KEY_BLOCKS), key_group, 1].reshape(keys, TOKENS).T

        def update(group, visible):
            s = dot(k, qb[group])
            if visible is not None:
                s = jnp.where(visible, s, masked_score)
            m_old = m_s[group]
            m_new = jnp.maximum(m_old, jnp.max(s, axis=0, keepdims=True))
            p = jnp.exp(s - m_new)
            r = jnp.exp(m_old - m_new)
            l_s[group] = l_s[group] * r + jnp.sum(p, axis=0, keepdims=True)
            acc[group] = acc[group] * r + dot(v_t, p.astype(bf16))
            m_s[group] = m_new

        over_queries(place, key_group, step, update, keys)
        return carry

    lax.fori_loop(0, SEG * steps, key_step, 0)
    for group in range(SEG):
        row_sum = l_s[group]
        ctx_ref[group] = heads_back(acc[group] / row_sum)
        lse_ref[group] = m_s[group] + jnp.log(row_sum)


def backward_kernel(cycle, q_ref, kv_ref, do_ref, ctx_ref, lse_ref, dq_ref, dkv_ref,
                    qb, dob, qb_t, dob_t, delta, dqt, dk_s, dv_s):
    place = lax.axis_index("blk") * lax.axis_size("tp") + lax.axis_index("tp")
    keys = KEY_BLOCKS * TOKENS
    steps = cycle // KEY_BLOCKS
    scale = 1.0 / math.sqrt(HEAD_DIM)
    for group in range(SEG):
        q_cols = block_diagonal(q_ref[group], scale)
        qb[group] = q_cols
        qb_t[group] = q_cols.T
        do_cols = block_diagonal(do_ref[group], 1.0)
        dob[group] = do_cols
        dob_t[group] = do_cols.T
        product = (do_ref[group].astype(f32) * ctx_ref[group].astype(f32)).T
        delta[group] = jnp.concatenate(
            [
                jnp.sum(product[:HEAD_DIM], axis=0, keepdims=True),
                jnp.sum(product[HEAD_DIM:], axis=0, keepdims=True),
            ],
            axis=1,
        )
    dqt[...] = jnp.zeros(dqt.shape, f32)

    def key_step(index, carry):
        key_group, step = index // steps, index % steps
        blocks = pl.ds(step * KEY_BLOCKS, KEY_BLOCKS)
        k = kv_ref[blocks, key_group, 0].reshape(keys, TOKENS)
        v = kv_ref[blocks, key_group, 1].reshape(keys, TOKENS)
        k_t = k.T
        dk_s[...] = jnp.zeros(dk_s.shape, f32)
        dv_s[...] = jnp.zeros(dv_s.shape, f32)

        def update(group, visible):
            p = jnp.exp(dot(k, qb[group]) - lse_ref[group])
            if visible is not None:
                p = jnp.where(visible, p, 0.0)
            dv_s[...] += dot(p.astype(bf16), dob_t[group])
            ds = (p * (dot(v, dob[group]) - delta[group])).astype(bf16)
            dk_s[...] += dot(ds, qb_t[group])
            dqt[group] += dot(k_t, ds)

        over_queries(place, key_group, step, update, keys)
        dkv_ref[blocks, key_group, 0] = dk_s[...].reshape(KEY_BLOCKS, TOKENS, TOKENS).astype(bf16)
        dkv_ref[blocks, key_group, 1] = dv_s[...].reshape(KEY_BLOCKS, TOKENS, TOKENS).astype(bf16)
        return carry

    lax.fori_loop(0, SEG * steps, key_step, 0)
    for group in range(SEG):
        dq_ref[group] = heads_back(dqt[group] * scale)


WHOLE = pl.BlockSpec(memory_space=pltpu.VMEM)


def attention_forward(queries, key_values):
    cycle = key_values.shape[0]
    return pl.pallas_call(
        functools.partial(forward_kernel, cycle),
        out_shape=(
            jax.ShapeDtypeStruct((SEG, TOKENS, TOKENS), bf16),
            jax.ShapeDtypeStruct((SEG, 1, 2 * TOKENS), f32),
        ),
        in_specs=[WHOLE] * 2,
        out_specs=(WHOLE,) * 2,
        scratch_shapes=[
            pltpu.VMEM((SEG, TOKENS, 2 * TOKENS), bf16),
            pltpu.VMEM((SEG, 1, 2 * TOKENS), f32),
            pltpu.VMEM((SEG, 1, 2 * TOKENS), f32),
            pltpu.VMEM((SEG, TOKENS, 2 * TOKENS), f32),
        ],
        compiler_params=pltpu.CompilerParams(vmem_limit_bytes=40 << 20),
        cost_estimate=pl.CostEstimate(
            flops=60_000_000_000, bytes_accessed=9 << 20, transcendentals=0
        ),
    )(queries, key_values)


def attention_backward(queries, key_values, context_grad, context, log_total):
    cycle = key_values.shape[0]
    columns = pltpu.VMEM((SEG, TOKENS, 2 * TOKENS), bf16)
    rows = pltpu.VMEM((SEG, 2 * TOKENS, TOKENS), bf16)
    return pl.pallas_call(
        functools.partial(backward_kernel, cycle),
        out_shape=(
            jax.ShapeDtypeStruct((SEG, TOKENS, TOKENS), bf16),
            jax.ShapeDtypeStruct(key_values.shape, bf16),
        ),
        in_specs=[WHOLE] * 5,
        out_specs=(WHOLE,) * 2,
        scratch_shapes=[
            columns,
            columns,
            rows,
            rows,
            pltpu.VMEM((SEG, 1, 2 * TOKENS), f32),
            pltpu.VMEM((SEG, TOKENS, 2 * TOKENS), f32),
            pltpu.VMEM((KEY_BLOCKS * TOKENS, TOKENS), f32),
            pltpu.VMEM((KEY_BLOCKS * TOKENS, TOKENS), f32),
        ],
        compiler_params=pltpu.CompilerParams(vmem_limit_bytes=48 << 20),
        cost_estimate=pl.CostEstimate(
            flops=80_000_000_000, bytes_accessed=18 << 20, transcendentals=0
        ),
    )(queries, key_values, context_grad, context, log_total)


def per_device(
    hidden_in,
    ln1_gain,
    ln1_bias,
    qkv_weight,
    qv_bias,
    out_weight,
    out_bias,
    ln2_gain,
    ln2_bias,
    fc_weight,
    fc_bias,
    proj_weight,
    proj_bias,
    cotangent,
):
    tokens, width = hidden_in.shape
    seq_count, blk_count, tp_count = (lax.axis_size(name) for name in ("seq", "blk", "tp"))
    head_cols = width // seq_count
    everywhere = ("seq", "blk", "tp")

    def to_heads(matrix):
        kinds = matrix.shape[1] // width
        parts = matrix.reshape(tokens, kinds, seq_count, head_cols).transpose(2, 1, 0, 3)
        return lax.all_to_all(parts, "seq", split_axis=0, concat_axis=0, tiled=True)

    def to_tokens(parts):
        kinds = parts.shape[1]
        moved = lax.all_to_all(parts, "seq", split_axis=0, concat_axis=0, tiled=True)
        return moved.transpose(2, 1, 0, 3).reshape(tokens, kinds * width)

    hidden_f = hidden_in.astype(f32)
    scaled_one, inverse_one, normed_one = normalize(hidden_f, ln1_gain, ln1_bias)
    normed_bf = normed_one.astype(bf16)
    qkv_bias = jnp.concatenate([qv_bias[0], jnp.zeros_like(qv_bias[0]), qv_bias[1]])
    qkv_heads = to_heads((dot(normed_bf, qkv_weight) + qkv_bias).astype(bf16))
    query_heads = qkv_heads[:, 0]
    key_values = lax.all_gather(qkv_heads[:, 1:], ("blk", "tp"), axis=0, tiled=False)
    key_values = key_values.reshape(blk_count * tp_count, SEG, 2, tokens, head_cols)

    cot_bf = cotangent.astype(bf16)
    gathered_cot = lax.all_gather(cot_bf, "tp", axis=0, tiled=True)
    normed_all = lax.all_gather(normed_bf, "seq", axis=0, tiled=True)

    context_heads, log_total = attention_forward(query_heads, key_values)
    context_tokens = to_tokens(context_heads[:, None])

    residual = hidden_f + dot(context_tokens, out_weight) + out_bias
    scaled_two, inverse_two, normed_two = normalize(residual, ln2_gain, ln2_bias)
    normed_two_bf = normed_two.astype(bf16)
    gathered_norm = lax.all_gather(normed_two_bf, "tp", axis=0, tiled=True)
    hidden_pre = dot(gathered_norm, fc_weight) + fc_bias
    gelu_value, gelu_slope = gelu_pair(hidden_pre)
    activation = gelu_value.astype(bf16)
    hidden_grad = dot(gathered_cot, proj_weight.T) * gelu_slope
    hidden_grad_bf = hidden_grad.astype(bf16)
    normed_two_grad = lax.psum_scatter(
        dot(hidden_grad_bf, fc_weight.T).astype(bf16), "tp", scatter_dimension=0, tiled=True
    ).astype(f32)
    residual_grad = cotangent + norm_back(normed_two_grad, scaled_two, inverse_two, ln2_gain)
    residual_grad_bf = residual_grad.astype(bf16)
    context_grad_heads = to_heads(dot(residual_grad_bf, out_weight.T).astype(bf16))[:, 0]

    query_grad, key_value_grad = attention_backward(
        query_heads, key_values, context_grad_heads, context_heads, log_total
    )

    mlp_out = lax.psum_scatter(
        dot(activation, proj_weight).astype(bf16), "tp", scatter_dimension=0, tiled=True
    ).astype(f32)
    block_out = residual + mlp_out + proj_bias
    wide_grads = jnp.concatenate(
        [
            jnp.einsum("td,tf->df", gathered_norm, hidden_grad_bf, preferred_element_type=f32),
            jnp.einsum("tf,td->fd", activation, gathered_cot, preferred_element_type=f32),
        ]
    ).astype(bf16)
    wide_part = lax.psum_scatter(wide_grads, ("seq", "blk"), scatter_dimension=0, tiled=True)
    wide_sum = lax.all_gather(wide_part, ("seq", "blk"), axis=0, tiled=True)
    fc_weight_grad = wide_sum[:width].astype(f32)
    proj_weight_grad = wide_sum[width:].astype(f32)
    fc_bias_grad = lax.psum(jnp.sum(hidden_grad, axis=0), ("seq", "blk"))
    residual_grad_all = lax.all_gather(residual_grad_bf, "seq", axis=0, tiled=True)
    out_part = jnp.einsum(
        "tc,td->cd",
        context_heads.reshape(SEG * tokens, head_cols),
        residual_grad_all,
        preferred_element_type=f32,
    ).astype(bf16)
    early_vectors = lax.psum(
        jnp.stack(
            [
                jnp.sum(residual_grad, axis=0),
                jnp.sum(normed_two_grad * scaled_two, axis=0),
                jnp.sum(normed_two_grad, axis=0),
                jnp.sum(cotangent, axis=0),
            ]
        ),
        everywhere,
    )

    key_value_own = lax.psum_scatter(
        key_value_grad, ("blk", "tp"), scatter_dimension=0, tiled=False
    )
    head_grads = jnp.concatenate([query_grad[:, None], key_value_own], axis=1)
    token_grads = to_tokens(head_grads)
    normed_one_grad = dot(token_grads, qkv_weight.T)
    input_grad = residual_grad + norm_back(normed_one_grad, scaled_one, inverse_one, ln1_gain)
    token_sums = jnp.sum(token_grads.astype(f32), axis=0)
    late_vectors = lax.psum(
        jnp.stack(
            [
                jnp.sum(normed_one_grad * scaled_one, axis=0),
                jnp.sum(normed_one_grad, axis=0),
                token_sums[:width],
                token_sums[2 * width :],
            ]
        ),
        everywhere,
    )
    own_row = lax.axis_index(("seq", "blk")) * (width // (seq_count * blk_count))
    own_rows = width // (seq_count * blk_count)
    early_own = lax.dynamic_slice_in_dim(early_vectors, own_row, own_rows, 1)
    late_own = lax.dynamic_slice_in_dim(late_vectors, own_row, own_rows, 1)

    fine = own_rows // tp_count
    qkv_part = jnp.einsum(
        "gtd,gktf->dkf",
        normed_all.reshape(SEG, tokens, width),
        head_grads,
        preferred_element_type=f32,
    ).astype(bf16)
    qkv_part = qkv_part.reshape(seq_count, blk_count * tp_count, fine * 3 * head_cols)
    qkv_part = qkv_part.transpose(1, 0, 2).reshape(blk_count * tp_count, -1, head_cols)
    out_rows = out_part.reshape(blk_count * tp_count, -1, head_cols)
    weight_part = lax.psum_scatter(
        jnp.concatenate([qkv_part, out_rows], axis=1).reshape(-1, head_cols),
        ("blk", "tp"),
        scatter_dimension=0,
        tiled=True,
    )
    qkv_rows = weight_part[: seq_count * fine * 3].reshape(seq_count, fine * 3, head_cols)
    qkv_rows = lax.all_to_all(qkv_rows, "seq", split_axis=0, concat_axis=0, tiled=True)
    qkv_rows = qkv_rows.reshape(seq_count, fine, 3, head_cols).transpose(1, 2, 0, 3)
    own_weight = jnp.concatenate(
        [
            qkv_rows.reshape(fine, 3 * width),
            weight_part[seq_count * fine * 3 :].reshape(fine, width),
        ],
        axis=1,
    )
    own_weight = lax.all_gather(own_weight, "tp", axis=0, tiled=True).astype(f32)
    return (
        block_out,
        input_grad,
        late_own[0],
        late_own[1],
        own_weight[:, : 3 * width],
        late_own[2:4],
        own_weight[:, 3 * width :],
        early_own[0],
        early_own[1],
        early_own[2],
        fc_weight_grad,
        fc_bias_grad,
        proj_weight_grad,
        early_own[3],
    )


def solution(mesh):
    return jax.shard_map(
        per_device,
        mesh=mesh,
        in_specs=(
            P(("seq", "blk", "tp"), None),
            P(),
            P(),
            P(),
            P(),
            P(),
            P(),
            P(),
            P(),
            P(None, "tp"),
            P("tp"),
            P("tp", None),
            P(),
            P(("seq", "blk", "tp"), None),
        ),
        out_specs=(
            P(("seq", "blk", "tp"), None),
            P(("seq", "blk", "tp"), None),
            P(("seq", "blk")),
            P(("seq", "blk")),
            P(("seq", "blk"), None),
            P(None, ("seq", "blk")),
            P(("seq", "blk"), None),
            P(("seq", "blk")),
            P(("seq", "blk")),
            P(("seq", "blk")),
            P(None, "tp"),
            P("tp"),
            P("tp", None),
            P(("seq", "blk")),
        ),
        check_vma=False,
    )
```

time: 1500 us -> 683 us (0.46)
  waiting for transfers between devices: 639 us -> 270 us
  matrix products: 276 us -> 37.8 us
  local copies, waits for them, and re-layouts: 249 us -> 24.5 us
  other arithmetic: 174 us -> 23 us
  Pallas kernels: 0 us -> 118 us
  blocking collectives: 103 us -> 175 us
  loops' own time: 17.9 us -> 0 us
    reduce_scatter x6 -> x4, waiting for transfers between devices: 347 us -> 36.9 us  [the longest x1 24.7 us: per_device(): lax.psum_scatter(dot(activation, proj_weight).astype(bf16), 'tp', scatter...]
    dot_general x906 -> x10, matrix products: 269 us -> 33.1 us  [the longest x8 28.2 us: dot(): return jnp.dot(a, b, preferred_element_type=f32)]
    dynamic_update_slice x240 -> x0, local copies, waits for them, and re-layouts: 148 us -> none  [the longest x128 79.2 us: backward_update(): lax.dynamic_update_slice_in_dim(value_grad, value_part, first_key, 0)]
    pallas_call x0 -> x2, Pallas kernels: none -> 118 us  [the longest x1 67.3 us: attention_backward(): pl.pallas_call(functools.partial(backward_kernel, cycle), out_shape=(jax....]
    scatter x224 -> x0, other arithmetic: 82.7 us -> none  [the longest x112 75 us: forward_update(): run_sum.at[:, low_row:].set(new_sum)]
    psum x2, blocking collectives: 69.7 us -> 135 us  [the longest x1 69.1 us: per_device(): fc_bias_grad = lax.psum(jnp.sum(hidden_grad, axis=0), ('seq', 'blk'))]
    psum x2 -> x0, waiting for transfers between devices: 56.1 us -> none  [the longest x1 41.9 us: per_device(): lax.psum(qkv_part.astype(jnp.bfloat16), 'tp').astype(jnp.float32)]
    slice x838 -> x8, local copies, waits for them, and re-layouts: 55.9 us -> 5.76 us  [the longest x1 1.42 us: per_device(): weight_part[:seq_count * fine * 3].reshape(seq_count, fine * 3, head_cols)]
  transfers between devices with their start and end apart: 15 -> 14, of which waited for: 15 -> 11; matrix products, arithmetic and copies ran while one was open for 4% -> 8% of each run, Pallas kernels for 0% -> 10%
where the time goes in v1:
time: 683 us; the launch traced here: 680 us
  waiting for transfers between devices  270 us (40%)
  blocking collectives  175 us (26%)
  Pallas kernels  118 us (17%)
  matrix products  37.8 us (6%)
  local copies, waits for them, and re-layouts  24.5 us (4%)
  other arithmetic  23 us (3%)
  starting transfers between devices  17.3 us (3%)
  between operations  14.3 us (2%)
    all_gather x1, waiting for transfers between devices, per_device(): lax.all_gather(qkv_heads[:, 1:], ('blk', 'tp'), axis=0, tiled=False)  69.6 us
    psum x1, blocking collectives, per_device(): fc_bias_grad = lax.psum(jnp.sum(hidden_grad, axis=0), ('seq', 'blk'))  69.1 us
    pallas_call x1, Pallas kernels, attention_backward(): pl.pallas_call(functools.partial(backward_kernel, cycle), out_shape=(jax....  67.3 us
    psum x1, blocking collectives, per_device(): lax.psum(jnp.stack([jnp.sum(normed_one_grad * scaled_one, axis=0), jnp.su...  65.9 us
    pallas_call x1, Pallas kernels, attention_forward(): pl.pallas_call(functools.partial(forward_kernel, cycle), out_shape=(jax.S...  50.6 us
    unnamed x12, waiting for transfers between devices  46.2 us
    all_gather x1, waiting for transfers between devices, per_device(): wide_sum = lax.all_gather(wide_part, ('seq', 'blk'), axis=0, tiled=True)  42.4 us
    dot_general x8, matrix products, dot(): return jnp.dot(a, b, preferred_element_type=f32)  28.2 us
  transfers between devices with their start and end apart: 14, of which 11 were waited for; matrix products, arithmetic and copies ran while one was open for 8% of the time, Pallas kernels for 10%

profile of v1, /device:TPU:1, one launch (start us, length us, event | category | flops | bytes accessed | tf_op | source)
XLA Modules:
  0.0 680.1 jit_solution(1784580960136351477)
XLA Ops:
  11.7 3.8 fusion
  18.2 18.8 %all_to_all.25 = bf16[8,3,128,128]{3,2,1,0:T(8,128)(2,1)S(1)} all-to-all(bf16[8,3,128,128]{3,2,1,0:T(8,128)(2,1)S(1)} %copy.68), channel_id=1, replica_groups=mesh['seq'=8,'blk'=4,'tp'=4] {'seq'}, dimensions={0} | all-to-all | bytes 1572864 | tf_op jit(solution)/shard_map/all_to_all | solution.py:260
  39.8 69.6 %all-gather.18.cloned.1.call-done = bf16[128,2,128,128]{3,2,1,0:T(8,128)(2,1)} async-done(((bf16[8,2,128,128]{3,2,1,0:T(8,128)(2,1)}), bf16[128,2,128,128]{3,2,1,0:T(8,128)(2,1)}) %all-gather.18.cloned.1.call-update) | async-done | bytes 8388624 | tf_op jit(solution)/shard_map/all_gather | solution.py:273
  109.4 3.4 copy-done.2
  112.8 50.6 %shard_map.245 = (bf16[8,128,128]{2,1,0:T(8,128)(2,1)S(1)}, f32[8,1,256]{2,1,0:T(1,128)S(1)}) custom-call(bf16[8,128,128]{2,1,0:T(8,128)(2,1)S(1)} %slice_bitcast_fusion.q_ref, bf16[16,8,2,128,128]{4,3,2,1,0:T(8,128)(2,1)S(1)} %bitcast.98), custom_call_target="tpu_custom_call" | custom-call | flops 60000002048 | bytes 9437184 | tf_op jit(solution)/shard_map/pallas_call | solution.py:186
  163.4 11.4 %all_to_all.26 = bf16[8,1,128,128]{3,2,1,0:T(8,128)(2,1)S(1)} all-to-all(bf16[8,1,128,128]{3,2,1,0:T(8,128)(2,1)S(1)} %bitcast.92), channel_id=1, replica_groups=mesh['seq'=8,'blk'=4,'tp'=4] {'seq'}, dimensions={0} | all-to-all | bytes 524288 | tf_op jit(solution)/shard_map/all_to_all | solution.py:264
  181.2 24.6 %all-gather.8.cloned.1.call-done = bf16[512,1024]{1,0:T(8,128)(2,1)} async-done(((bf16[128,1024]{1,0:T(8,128)(2,1)}), bf16[512,1024]{1,0:T(8,128)(2,1)}) %all-gather.8.cloned.1.call-update) | async-done | bytes 1048592 | tf_op jit(solution)/shard_map/all_gather | solution.py:286
  205.8 4.5 fusion.39
  210.2 22.1 %all-gather.10.cloned.1.call-done = bf16[512,1024]{1,0:T(8,128)(2,1)} async-done(((bf16[128,1024]{1,0:T(8,128)(2,1)}), bf16[512,1024]{1,0:T(8,128)(2,1)}) %all-gather.10.cloned.1.call-update) | async-done | bytes 1048592 | tf_op jit(solution)/shard_map/all_gather | solution.py:277
  232.3 4.4 fusion.38
  237.8 2.3 convolution_convert_fusion.2
  240.1 4.1 convolution_convert_fusion.3
  244.5 3.0 convolution_convert_fusion.1
  249.1 2.5 pad_maximum_fusion
  251.6 11.9 %reduce-scatter.10.cloned.1.call-done = bf16[128,1024]{1,0:T(8,128)(2,1)} async-done(((bf16[512,1024]{1,0:T(8,128)(2,1)}), bf16[128,1024]{1,0:T(8,128)(2,1)}) %reduce-scatter.10.cloned.1.call-update) | async-done | bytes 262160 | tf_op jit(solution)/shard_map/reduce_scatter | solution.py:292
  264.8 24.7 %reduce-scatter.8.cloned.1.call-done = bf16[128,1024]{1,0:T(8,128)(2,1)} async-done(((bf16[512,1024]{1,0:T(8,128)(2,1)}), bf16[128,1024]{1,0:T(8,128)(2,1)}) %reduce-scatter.8.cloned.1.call-update) | async-done | bytes 262160 | tf_op jit(solution)/shard_map/reduce_scatter | solution.py:303
  294.4 6.3 all-to-all-start.2
  301.5 5.7 all-to-all-done.2
  307.2 67.3 %shard_map.246 = (bf16[8,128,128]{2,1,0:T(8,128)(2,1)S(1)}, bf16[16,8,2,128,128]{4,3,2,1,0:T(8,128)(2,1)}) custom-call(bf16[8,128,128]{2,1,0:T(8,128)(2,1)S(1)} %slice_bitcast_fusion.q_ref, bf16[16,8,2,128,128]{4,3,2,1,0:T(8,128)(2,1)} %bitcast.97, bf16[8,128,128]{2,1,0:T(8,128)(2,1)S(1)} %bitcast.94, bf16[8,128,128]{2,1,0:T(8,128)(2,1)S(1)} %get-tuple-element.18.ctx_ref, ...), custom_call_target="tpu_custom_call" | custom-call | flops 80000000000 | bytes 18874368 | tf_op jit(solution)/shard_map/pallas_call | solution.py:211
  375.9 69.1 %psum.23 = f32[1024]{0:T(1024)} all-reduce(f32[1024]{0:T(1024)S(1)} %get-tuple-element.52), channel_id=1, replica_groups=mesh['seq'=8,'blk'=4,'tp'=4] {'seq','blk'}, use_global_device_ids=true, to_apply=%region_23.0 | all-reduce | flops 1024 | bytes 8192 | tf_op jit(solution)/shard_map/psum | solution.py:317
  447.3 44.5 %reduce-scatter.16.cloned.1.call-done = bf16[1,8,2,128,128]{4,3,2,1,0:T(8,128)(2,1)} async-done(((bf16[16,8,2,128,128]{4,3,2,1,0:T(8,128)(2,1)}), bf16[1,8,2,128,128]{4,3,2,1,0:T(8,128)(2,1)}) %reduce-scatter.16.cloned.1.call-update) | async-done | bytes 524304
  493.9 6.2 all-to-all-start.3
  500.2 42.4 %all-gather.16.cloned.1.call-done = bf16[2048,1024]{1,0:T(8,128)(2,1)} async-done(((bf16[64,1024]{1,0:T(8,128)(2,1)}), bf16[2048,1024]{1,0:T(8,128)(2,1)}) %all-gather.16.cloned.1.call-update) | async-done | bytes 4194320 | tf_op jit(solution)/shard_map/all_gather | solution.py:314
  542.6 6.7 slice_convert_fusion
  549.2 19.7 %all-gather.12.cloned.1.call-done = bf16[1024,1024]{1,0:T(8,128)(2,1)} async-done(((bf16[128,1024]{1,0:T(8,128)(2,1)}), bf16[1024,1024]{1,0:T(8,128)(2,1)}) %all-gather.12.cloned.1.call-update) | async-done | bytes 2097168 | tf_op jit(solution)/shard_map/all_gather | solution.py:278
  568.9 2.9 bitcast_convert_fusion
  577.0 6.0 fusion.23
  583.0 65.9 %all-reduce.1 = (f32[4,1024]{1,0:T(4,128)S(1)}, f32[4,1024]{1,0:T(4,128)S(1)}) all-reduce(f32[4,1024]{1,0:T(4,128)S(1)} %pad_maximum_fusion.4, f32[4,1024]{1,0:T(4,128)S(1)} %pad_maximum_fusion.5), channel_id=1, replica_groups=mesh['seq'=8,'blk'=4,'tp'=4] {'seq','blk','tp'}, use_global_device_ids=true, to_apply=%region_14.0 | all-reduce | flops 8192 | bytes 65536 | tf_op jit(solution)/shard_map/psum | solution.py:345
  649.5 2.2 fusion.22
  653.2 4.2 all-to-all-start.4
  659.3 3.0 all-to-all-done.4
  662.3 9.8 %all_gather.30 = bf16[32,4096]{1,0:T(8,128)(2,1)S(1)} all-gather(bf16[8,4096]{1,0:T(8,128)(2,1)S(1)} %pad_maximum_fusion.3), channel_id=1, replica_groups=mesh['seq'=8,'blk'=4,'tp'=4] {'tp'}, dimensions={0}, use_global_device_ids=true | all-gather | bytes 327680 | tf_op jit(solution)/shard_map/all_gather | solution.py:387
  (128 shorter events, 42.2 us)
Async XLA Ops:
  7.2 225.1 %copy-start = (bf16[1024,1024]{1,0:T(8,128)(2,1)S(1)}, bf16[1024,1024]{1,0:T(8,128)(2,1)}, u32[]{:S(2)}) copy-start(bf16[1024,1024]{1,0:T(8,128)(2,1)} %param.25) | copy-start | bytes 6291460
  7.2 102.2 %all-gather.18.cloned.1.call-start = ((), (), s32[]{:S(2)}) async-start(), calls=%async_computation.19 | async-start | bytes 8912896 | tf_op jit(solution)/shard_map/all_gather | solution.py:273
  8.5 3.2 copy-start.11
  9.6 2.0 copy-start.13
  11.7 3.9 copy-start.6
  38.8 167.0 %all-gather.8.cloned.1.call-start = ((), (), s32[]{:S(2)}) async-start(), calls=%async_computation.10 | async-start | bytes 1310720 | tf_op jit(solution)/shard_map/all_gather | solution.py:286
  109.4 3.4 copy-start.2
  112.8 62.9 %copy-start.3 = (bf16[128,1024]{1,0:T(8,128)(2,1)S(1)}, bf16[128,1024]{1,0:T(8,128)(2,1)}, u32[]{:S(2)}) copy-start(bf16[128,1024]{1,0:T(8,128)(2,1)} %param.14) | copy-start | bytes 786436
  112.8 62.9 %copy-start.15 = (f32[1024]{0:T(1024)S(1)}, f32[1024]{0:T(1024)}, u32[]{:S(2)}) copy-start(f32[1024]{0:T(1024)} %param.20) | copy-start | bytes 12292
  174.8 3.3 copy-start.9
  174.8 3.3 copy-start.16
  179.1 53.2 %all-gather.10.cloned.1.call-start = ((), (), s32[]{:S(2)}) async-start(), calls=%async_computation.12 | async-start | bytes 1310720 | tf_op jit(solution)/shard_map/all_gather | solution.py:277
  181.1 51.2 %copy-start.20 = (f32[1024]{0:T(1024)S(1)}, f32[1024]{0:T(1024)}, u32[]{:S(2)}) copy-start(f32[1024]{0:T(1024)} %param.24) | copy-start | bytes 12292
  181.1 82.4 %reduce-scatter.10.cloned.1.call-start = ((), (), s32[]{:S(2)}) async-start(), calls=%async_computation.13 | async-start | bytes 1310720 | tf_op jit(solution)/shard_map/reduce_scatter | solution.py:292
  232.3 5.4 copy-start.18
  240.1 49.4 %reduce-scatter.8.cloned.1.call-start = ((), (), s32[]{:S(2)}) async-start(), calls=%async_computation.11 | async-start | bytes 1310720 | tf_op jit(solution)/shard_map/reduce_scatter | solution.py:303
  244.2 130.7 %reduce-scatter.14.cloned.1.call-start = ((), (), s32[]{:S(2)}) async-start(), calls=%async_computation.17 | async-start | bytes 4325376 | tf_op jit(solution)/shard_map/reduce_scatter | solution.py:313
  244.4 3.0 copy-start.19
  244.4 3.0 copy-start.21
  251.6 37.9 %copy-start.17 = (f32[1024]{0:T(1024)S(1)}, f32[1024]{0:T(1024)}, u32[]{:S(2)}) copy-start(f32[1024]{0:T(1024)} %param.26) | copy-start | bytes 12292
  251.6 40.9 %copy-start.4 = (bf16[1024,1024]{1,0:T(8,128)(2,1)S(1)}, bf16[1024,1024]{1,0:T(8,128)(2,1)}, u32[]{:S(2)}) copy-start(bf16[1024,1024]{1,0:T(8,128)(2,1)} %param.19) | copy-start | bytes 6291460
  292.5 1.9 copy-start.8
  294.4 12.8 %all-to-all-start.2 = ((bf16[8,1,128,128]{3,2,1,0:T(8,128)(2,1)}), bf16[8,1,128,128]{3,2,1,0:T(8,128)(2,1)S(1)}, u32[]{:S(2)}, u32[]{:S(2)}) async-start(bf16[8,1,128,128]{3,2,1,0:T(8,128)(2,1)} %copy.73), calls=%async_computation.4 | async-start | bytes 524288 | tf_op jit(solution)/shard_map/all_to_all | solution.py:260
  300.7 144.3 %all-gather.14.cloned.1.call-start = ((), (), s32[]{:S(2)}) async-start(), calls=%async_computation.15 | async-start | bytes 2359296 | tf_op jit(solution)/shard_map/all_gather | solution.py:318
  301.4 190.4 %reduce-scatter.16.cloned.1.call-start = ((), (), s32[]{:S(2)}) async-start(), calls=%async_computation.20 | async-start | bytes 8912896
  374.6 168.0 %all-gather.16.cloned.1.call-start = ((), (), s32[]{:S(2)}) async-start(), calls=%async_computation.18 | async-start | bytes 4325376 | tf_op jit(solution)/shard_map/all_gather | solution.py:314
  375.3 193.6 %all-gather.12.cloned.1.call-start = ((), (), s32[]{:S(2)}) async-start(), calls=%async_computation.14 | async-start | bytes 2359296 | tf_op jit(solution)/shard_map/all_gather | solution.py:278
  493.9 81.2 %all-to-all-start.3 = ((bf16[8,3,128,128]{3,2,1,0:T(8,128)(2,1)}), bf16[8,3,128,128]{3,2,1,0:T(8,128)(2,1)}, u32[]{:S(2)}, u32[]{:S(2)}) async-start(bf16[8,3,128,128]{3,2,1,0:T(8,128)(2,1)} %copy.75), calls=%async_computation.5 | async-start | bytes 1572864 | tf_op jit(solution)/shard_map/all_to_all | solution.py:264
  500.2 151.6 %reduce-scatter.12.cloned.1.call-start = ((), (), s32[]{:S(2)}) async-start(), calls=%async_computation.16 | async-start | bytes 1114112 | tf_op jit(solution)/shard_map/reduce_scatter | solution.py:371
  575.1 1.9 copy-start.14
  576.9 96.6 %copy-start.1 = (bf16[1024,1024]{1,0:T(8,128)(2,1)S(1)}, bf16[1024,1024]{1,0:T(8,128)(2,1)}, u32[]{:S(2)}) copy-start(bf16[1024,1024]{1,0:T(8,128)(2,1)} %param.25) | copy-start | bytes 6291460
  653.2 9.0 %all-to-all-start.4 = ((bf16[8,24,128]{2,1,0:T(8,128)(2,1)}), bf16[8,24,128]{2,1,0:T(8,128)(2,1)S(1)}, u32[]{:S(2)}, u32[]{:S(2)}) async-start(bf16[8,24,128]{2,1,0:T(8,128)(2,1)} %bitcast.30), calls=%async_computation.7 | async-start | bytes 98304 | tf_op jit(solution)/shard_map/all_to_all | solution.py:378
  (5 other events, 6.4 us)
Sparse Core Ops, SparseCore 0:
  38.9 70.4 all-gather.17
  179.2 26.5 all-gather.7
  208.0 24.2 all-gather.9
  240.2 23.3 reduce-scatter.9
  265.9 23.4 reduce-scatter.7
  293.5 81.3 reduce-scatter.13
  377.4 26.5 all-gather.13
  407.8 83.9 reduce-scatter.15
  494.3 48.2 all-gather.15
  544.3 24.6 all-gather.11
  575.2 71.0 reduce-scatter.11

commit v2 on v1

v2 whole, which is shorter than its diff:
```python
import functools
import math

import jax
import jax.numpy as jnp
from jax import lax
from jax.experimental import pallas as pl
from jax.experimental.pallas import tpu as pltpu
from jax.sharding import Mesh
from jax.sharding import PartitionSpec as P

D = 64
T = 128
SEG = 16
CYC = 8
N = CYC * T
PAIRS = SEG // 2
HEAD_AXES = ("seq", "bh")
KEY_AXES = ("bl", "tp")
ROW_AXES = ("seq", "bh", "bl")

epsilon = 1e-05
gelu_coef = math.sqrt(2.0 / math.pi)
masked_score = -1e30
score_scale = 1.0 / math.sqrt(D)
f32, bf16 = jnp.float32, jnp.bfloat16
WHOLE = pl.BlockSpec(memory_space=pltpu.VMEM)


def normalize(matrix, norm_gain, norm_shift):
    row_mean = jnp.mean(matrix, axis=-1, keepdims=True)
    centered = matrix - row_mean
    variance = jnp.mean(centered * centered, axis=-1, keepdims=True)
    inverse = lax.rsqrt(variance + epsilon)
    scaled = centered * inverse
    return (scaled, inverse, scaled * norm_gain + norm_shift)


def norm_back(upstream_grad, scaled, inverse, norm_gain):
    weighted = upstream_grad * norm_gain
    first_mean = jnp.mean(weighted, axis=-1, keepdims=True)
    second_mean = jnp.mean(weighted * scaled, axis=-1, keepdims=True)
    return inverse * (weighted - first_mean - scaled * second_mean)


def gelu_pair(hidden_pre):
    tanh_arg = gelu_coef * (hidden_pre + 0.044715 * hidden_pre * hidden_pre * hidden_pre)
    tanh_value = jnp.tanh(tanh_arg)
    gelu_value = 0.5 * hidden_pre * (1.0 + tanh_value)
    gelu_slope = 0.5 * (1.0 + tanh_value) + 0.5 * hidden_pre * (
        1.0 - tanh_value * tanh_value
    ) * gelu_coef * (1.0 + 3.0 * 0.044715 * hidden_pre * hidden_pre)
    return (gelu_value, gelu_slope)


def dot(a, b):
    return jnp.dot(a, b, preferred_element_type=f32)


def product(spec, a, b):
    return jnp.einsum(spec, a, b, preferred_element_type=f32)


def pair_of(ref, pair):
    return jnp.concatenate([ref[2 * pair], ref[2 * pair + 1]], axis=1)


def key_place():
    return lax.axis_index("bl") * lax.axis_size("tp") + lax.axis_index("tp")


def visible_keys(group):
    key = lax.broadcasted_iota(jnp.int32, (N, 2 * T), 0) + group * N
    lane = lax.broadcasted_iota(jnp.int32, (N, 2 * T), 1)
    query = (group // 2 * 2 + lane // T) * N + key_place() * T + lane % T
    return key <= query


def over_pairs(group, update):
    own = group // 2
    update(own, visible_keys(group))

    def full(pair, carry):
        update(pair, None)
        return carry

    lax.fori_loop(own + 1, PAIRS, full, 0)


def forward_kernel(q_ref, kv_ref, ctx_ref, lse_ref, qb, m_s, l_s, acc):
    for pair in range(PAIRS):
        q = pair_of(q_ref, pair).astype(f32) * score_scale
        qb[pair] = jnp.concatenate([q, jnp.zeros_like(q)], axis=0).astype(bf16)
    m_s[...] = jnp.full(m_s.shape, masked_score, f32)
    l_s[...] = jnp.zeros(l_s.shape, f32)
    acc[...] = jnp.zeros(acc.shape, f32)

    def key_step(group, carry):
        kv = kv_ref[:, group].reshape(N, T)
        v_t = kv.T[D:]

        def update(pair, visible):
            s = dot(kv, qb[pair])
            if visible is not None:
                s = jnp.where(visible, s, masked_score)
            m_old = m_s[pair]
            m_new = jnp.maximum(m_old, jnp.max(s, axis=0, keepdims=True))
            e = jnp.exp(s - m_new)
            r = jnp.exp(m_old - m_new)
            l_s[pair] = l_s[pair] * r + jnp.sum(e, axis=0, keepdims=True)
            acc[pair] = acc[pair] * r + dot(v_t, e.astype(bf16))
            m_s[pair] = m_new

        over_pairs(group, update)
        return carry

    lax.fori_loop(0, SEG, key_step, 0)
    for pair in range(PAIRS):
        row_sum = l_s[pair]
        o = (acc[pair] / row_sum).astype(bf16)
        ctx_ref[2 * pair] = o[:, :T]
        ctx_ref[2 * pair + 1] = o[:, T:]
        lse_ref[pair] = m_s[pair] + jnp.log(row_sum)


def attention_forward(queries, key_values):
    return pl.pallas_call(
        forward_kernel,
        out_shape=(
            jax.ShapeDtypeStruct((SEG, D, T), bf16),
            jax.ShapeDtypeStruct((PAIRS, 1, 2 * T), f32),
        ),
        in_specs=[WHOLE] * 2,
        out_specs=(WHOLE,) * 2,
        scratch_shapes=[
            pltpu.VMEM((PAIRS, 2 * D, 2 * T), bf16),
            pltpu.VMEM((PAIRS, 1, 2 * T), f32),
            pltpu.VMEM((PAIRS, 1, 2 * T), f32),
            pltpu.VMEM((PAIRS, D, 2 * T), f32),
        ],
        compiler_params=pltpu.CompilerParams(vmem_limit_bytes=40 << 20),
        cost_estimate=pl.CostEstimate(
            flops=60_000_000_000, bytes_accessed=5 << 20, transcendentals=0
        ),
    )(queries, key_values)


def backward_kernel(q_ref, kv_ref, do_ref, ctx_ref, lse_ref, dq_ref, dkv_ref,
                    w, w_t, delta, dqt, dkv_s):
    for pair in range(PAIRS):
        q = pair_of(q_ref, pair).astype(f32) * score_scale
        do = pair_of(do_ref, pair).astype(f32)
        zero = jnp.zeros_like(q)
        both = jnp.concatenate(
            [jnp.concatenate([q, zero], axis=1), jnp.concatenate([zero, do], axis=1)], axis=0
        )
        w[pair] = both.astype(bf16)
        w_t[pair] = both.T.astype(bf16)
        delta[pair] = jnp.sum(do * pair_of(ctx_ref, pair).astype(f32), axis=0, keepdims=True)
    dqt[...] = jnp.zeros(dqt.shape, f32)

    def key_step(step, carry):
        group = SEG - 1 - step
        kv = kv_ref[:, group].reshape(N, T)
        k_t = kv.T[:D]
        dkv_s[...] = jnp.zeros(dkv_s.shape, f32)

        def update(pair, visible):
            e = jnp.exp(dot(kv, w[pair][:, : 2 * T]) - lse_ref[pair])
            if visible is not None:
                e = jnp.where(visible, e, 0.0)
            ds = (e * (dot(kv, w[pair][:, 2 * T :]) - delta[pair])).astype(bf16)
            dkv_s[...] += dot(jnp.concatenate([ds, e.astype(bf16)], axis=1), w_t[pair])
            dqt[pair] += dot(k_t, ds)

        over_pairs(group, update)
        dkv_ref[:, group] = dkv_s[...].reshape(CYC, T, T).astype(bf16)
        return carry

    lax.fori_loop(0, SEG, key_step, 0)
    for pair in range(PAIRS):
        d = (dqt[pair] * score_scale).astype(bf16)
        dq_ref[2 * pair] = d[:, :T]
        dq_ref[2 * pair + 1] = d[:, T:]


def attention_backward(queries, key_values, context_grad, context, log_total):
    return pl.pallas_call(
        backward_kernel,
        out_shape=(
            jax.ShapeDtypeStruct((SEG, D, T), bf16),
            jax.ShapeDtypeStruct(key_values.shape, bf16),
        ),
        in_specs=[WHOLE] * 5,
        out_specs=(WHOLE,) * 2,
        scratch_shapes=[
            pltpu.VMEM((PAIRS, T, 4 * T), bf16),
            pltpu.VMEM((PAIRS, 4 * T, T), bf16),
            pltpu.VMEM((PAIRS, 1, 2 * T), f32),
            pltpu.VMEM((PAIRS, D, 2 * T), f32),
            pltpu.VMEM((N, T), f32),
        ],
        compiler_params=pltpu.CompilerParams(vmem_limit_bytes=48 << 20),
        cost_estimate=pl.CostEstimate(
            flops=75_000_000_000, bytes_accessed=10 << 20, transcendentals=0
        ),
    )(queries, key_values, context_grad, context, log_total)


def per_device(
    hidden_in,
    ln1_gain,
    ln1_bias,
    qkv_weight,
    qv_bias,
    out_weight,
    out_bias,
    ln2_gain,
    ln2_bias,
    fc_weight,
    fc_bias,
    proj_weight,
    proj_bias,
    cotangent,
):
    tokens, width = hidden_in.shape

    def swap_heads(parts):
        return lax.all_to_all(parts, HEAD_AXES, split_axis=0, concat_axis=0, tiled=True)

    cot_bf = cotangent.astype(bf16)
    gathered_cot = lax.all_gather(cot_bf, "tp", axis=0, tiled=True)

    hidden_f = hidden_in.astype(f32)
    scaled_one, inverse_one, normed_one = normalize(hidden_f, ln1_gain, ln1_bias)
    normed_bf = normed_one.astype(bf16)
    q_t = product("td,dc->ct", normed_bf, qkv_weight[:, :width]) + qv_bias[0][:, None]
    kv = dot(normed_bf, qkv_weight[:, width:]) + jnp.concatenate(
        [jnp.zeros_like(qv_bias[1]), qv_bias[1]]
    )
    kv = kv.astype(bf16).reshape(tokens, 2, SEG, D).transpose(2, 0, 1, 3)
    sent = jnp.concatenate(
        [q_t.astype(bf16).reshape(SEG, D, tokens), kv.reshape(SEG, tokens, 2 * D)], axis=1
    )
    arrived = swap_heads(sent)
    query_t, own_kv = arrived[:, :D], arrived[:, D:]
    own_kv, gathered_cot = lax.optimization_barrier((own_kv, gathered_cot))
    key_values = lax.all_gather(own_kv, KEY_AXES, axis=0, tiled=False)
    key_values = key_values.reshape(CYC, SEG, tokens, 2 * D)
    normed_all = lax.all_gather(normed_bf, HEAD_AXES, axis=0, tiled=False)
    normed_all = normed_all.reshape(SEG, tokens, width)
    context_heads, log_total = attention_forward(query_t, key_values)
    context_heads, normed_all = lax.optimization_barrier((context_heads, normed_all))

    context_t = swap_heads(context_heads).reshape(width, tokens)
    residual = hidden_f + product("ct,cd->td", context_t, out_weight) + out_bias
    scaled_two, inverse_two, normed_two = normalize(residual, ln2_gain, ln2_bias)
    gathered_norm = lax.all_gather(normed_two.astype(bf16), "tp", axis=0, tiled=True)
    hidden_pre = dot(gathered_norm, fc_weight) + fc_bias
    gelu_value, gelu_slope = gelu_pair(hidden_pre)
    activation = gelu_value.astype(bf16)
    hidden_grad = dot(gathered_cot, proj_weight.T) * gelu_slope
    hidden_grad_bf = hidden_grad.astype(bf16)
    normed_two_grad = lax.psum_scatter(
        dot(hidden_grad_bf, fc_weight.T).astype(bf16), "tp", scatter_dimension=0, tiled=True
    ).astype(f32)
    residual_grad = cotangent + norm_back(normed_two_grad, scaled_two, inverse_two, ln2_gain)
    residual_grad_bf = residual_grad.astype(bf16)
    context_grad = product("td,cd->ct", residual_grad_bf, out_weight).astype(bf16)
    context_grad_heads = swap_heads(context_grad.reshape(SEG, D, tokens))

    wide_grads = jnp.concatenate(
        [
            product("td,tf->df", gathered_norm, hidden_grad_bf),
            product("tf,td->fd", activation, gathered_cot),
        ]
    ).astype(bf16)
    wide_part = lax.psum_scatter(wide_grads, ROW_AXES, scatter_dimension=0, tiled=True)
    wide_sum = lax.all_gather(wide_part, ROW_AXES, axis=0, tiled=True)
    fc_weight_grad = wide_sum[:width].astype(f32)
    proj_weight_grad = wide_sum[width:].astype(f32)
    mlp_out = lax.psum_scatter(
        dot(activation, proj_weight).astype(bf16), "tp", scatter_dimension=0, tiled=True
    ).astype(f32)
    block_out = residual + mlp_out + proj_bias
    bias_parts = lax.all_gather(jnp.sum(hidden_grad, axis=0).astype(bf16)[None], ROW_AXES, axis=0, tiled=True)
    fc_bias_grad = jnp.sum(bias_parts.astype(f32), axis=0)
    residual_grad_all = lax.all_gather(residual_grad_bf, HEAD_AXES, axis=0, tiled=False)
    residual_grad_all = residual_grad_all.reshape(SEG, tokens, width)

    query_grad, key_value_grad = attention_backward(
        query_t, key_values, context_grad_heads, context_heads, log_total
    )
    key_value_own = lax.psum_scatter(
        key_value_grad, KEY_AXES, scatter_dimension=0, tiled=False
    )
    head_grads = jnp.concatenate([query_grad, key_value_own.transpose(0, 2, 1)], axis=1)
    token_grads = swap_heads(head_grads).reshape(SEG, 3, D, tokens)
    token_grads = token_grads.transpose(1, 0, 2, 3).reshape(3 * width, tokens)
    normed_one_grad = product("ft,df->td", token_grads, qkv_weight)
    input_grad = residual_grad + norm_back(normed_one_grad, scaled_one, inverse_one, ln1_gain)

    fine = D // CYC
    vectors = jnp.stack(
        [
            jnp.sum(residual_grad, axis=0),
            jnp.sum(normed_two_grad * scaled_two, axis=0),
            jnp.sum(normed_two_grad, axis=0),
            jnp.sum(cotangent, axis=0),
            jnp.sum(normed_one_grad * scaled_one, axis=0),
            jnp.sum(normed_one_grad, axis=0),
        ]
    ).astype(bf16)
    count = vectors.shape[0]
    vectors = vectors.reshape(count, SEG, CYC, fine).transpose(2, 1, 0, 3)
    head_sums = jnp.sum(head_grads.astype(f32), axis=(0, 2)).astype(bf16).reshape(3, CYC, fine)
    qkv_part = product("gtd,gft->df", normed_all, head_grads).astype(bf16)
    qkv_part = qkv_part.reshape(SEG, CYC, fine * 3 * D).transpose(1, 0, 2)
    out_part = product("gct,gtd->cd", context_heads, residual_grad_all).astype(bf16)
    packed = jnp.concatenate(
        [
            qkv_part.reshape(CYC, -1),
            vectors.reshape(CYC, -1),
            out_part.reshape(CYC, -1),
            head_sums.transpose(1, 0, 2).reshape(CYC, -1),
        ],
        axis=1,
    )
    length = packed.shape[1]
    padded = -length % (16 * T)
    packed = jnp.pad(packed, ((0, 0), (0, padded)))
    summed = lax.psum_scatter(
        packed.reshape(-1, T), KEY_AXES, scatter_dimension=0, tiled=True
    ).reshape(-1)
    qkv_size, vector_size = SEG * fine * 3 * D, SEG * count * fine
    to_rows = jnp.concatenate(
        [
            summed[:qkv_size].reshape(SEG, -1),
            summed[qkv_size : qkv_size + vector_size].reshape(SEG, -1),
        ],
        axis=1,
    )
    moved = swap_heads(to_rows)
    qkv_rows = moved[:, : fine * 3 * D].reshape(SEG, fine, 3, D).transpose(1, 2, 0, 3)
    vector_rows = jnp.sum(
        moved[:, fine * 3 * D :].astype(f32).reshape(SEG, count, fine), axis=0
    ).astype(bf16)
    rest = summed[qkv_size + vector_size :]
    out_rows = rest[: fine * width].reshape(fine, width)
    bias_rows = rest[fine * width : fine * width + 3 * fine].reshape(3, fine)
    narrow = jnp.concatenate([vector_rows, bias_rows]).T
    own_rows = jnp.concatenate(
        [
            qkv_rows.reshape(fine, 3 * width),
            out_rows,
            jnp.pad(narrow, ((0, 0), (0, T - count - 3))),
        ],
        axis=1,
    )
    own_rows = lax.all_gather(own_rows, "tp", axis=0, tiled=True).astype(f32)
    narrow = own_rows[:, 4 * width :]
    return (
        block_out,
        input_grad,
        narrow[:, 4],
        narrow[:, 5],
        own_rows[:, : 3 * width],
        jnp.stack([narrow[:, count], narrow[:, count + 2]]),
        own_rows[:, 3 * width : 4 * width],
        narrow[:, 0],
        narrow[:, 1],
        narrow[:, 2],
        fc_weight_grad,
        fc_bias_grad,
        proj_weight_grad,
        narrow[:, 3],
    )


def solution(mesh):
    shape = mesh.devices.shape
    split = Mesh(
        mesh.devices.reshape(shape[0], shape[1] // 2, 2, shape[2]), ("seq", "bh", "bl", "tp")
    )
    every = P(("seq", "bh", "bl", "tp"), None)
    rows = ("seq", "bh", "bl")
    return jax.shard_map(
        per_device,
        mesh=split,
        in_specs=(
            every,
            P(),
            P(),
            P(),
            P(),
            P(),
            P(),
            P(),
            P(),
            P(None, "tp"),
            P("tp"),
            P("tp", None),
            P(),
            every,
        ),
        out_specs=(
            every,
            every,
            P(rows),
            P(rows),
            P(rows, None),
            P(None, rows),
            P(rows, None),
            P(rows),
            P(rows),
            P(rows),
            P(None, "tp"),
            P("tp"),
            P("tp", None),
            P(rows),
        ),
        check_vma=False,
    )
```

time: 683 us -> 628 us (0.919)
  blocking collectives: 175 us -> 106 us
  waiting for transfers between devices: 270 us -> 297 us
  Pallas kernels: 118 us -> 111 us
    psum x2 -> x0, blocking collectives: 135 us -> none  [the longest x1 69.1 us: per_device(): fc_bias_grad = lax.psum(jnp.sum(hidden_grad, axis=0), ('seq', 'blk'))]
    reduce_scatter x2 -> x3, waiting for transfers between devices: 0.34 us -> 107 us  [the longest x1 67.2 us: per_device(): lax.psum_scatter(wide_grads, ROW_AXES, scatter_dimension=0, tiled=True)]
    unnamed x12 -> x11, waiting for transfers between devices: 46.2 us -> 1.52 us
    all_gather x1 -> x2, blocking collectives: 9.84 us -> 53.4 us  [the longest x1 43.5 us: per_device(): lax.all_gather(jnp.sum(hidden_grad, axis=0).astype(bf16)[None], ROW_AXES,...]
    all_to_all x2 -> x3, blocking collectives: 30.2 us -> 52.8 us  [swap_heads(): lax.all_to_all(parts, HEAD_AXES, split_axis=0, concat_axis=0, tiled=True)]
    all_gather x1, waiting for transfers between devices: 22.1 us -> 0.01 us  [per_device(): gathered_cot = lax.all_gather(cot_bf, 'tp', axis=0, tiled=True)]
    all_gather x5, waiting for transfers between devices: 156 us -> 139 us  [the longest x1 50.3 us: per_device(): lax.all_gather(residual_grad_bf, HEAD_AXES, axis=0, tiled=False)]
    dot_general x8 -> x5, matrix products: 28.2 us -> 14.9 us  [dot(): return jnp.dot(a, b, preferred_element_type=f32)]
  transfers between devices with their start and end apart: 14 -> 13, of which waited for: 11 -> 10; matrix products, arithmetic and copies ran while one was open for 8% -> 8% of each run, Pallas kernels for 10% -> 8%
where the time goes in v2:
time: 628 us; the launch traced here: 627 us
  waiting for transfers between devices  297 us (47%)
  Pallas kernels  111 us (18%)
  blocking collectives  106 us (17%)
  matrix products  36.5 us (6%)
  other arithmetic  24.8 us (4%)
  local copies, waits for them, and re-layouts  23.1 us (4%)
  between operations  14.6 us (2%)
  starting transfers between devices  13.4 us (2%)
    reduce_scatter x1, waiting for transfers between devices, per_device(): lax.psum_scatter(wide_grads, ROW_AXES, scatter_dimension=0, tiled=True)  67.2 us
    pallas_call x1, Pallas kernels, attention_backward(): pl.pallas_call(backward_kernel, out_shape=(jax.ShapeDtypeStruct((SEG, D,...  59.5 us
    all_to_all x3, blocking collectives, swap_heads(): lax.all_to_all(parts, HEAD_AXES, split_axis=0, concat_axis=0, tiled=True)  52.8 us
    pallas_call x1, Pallas kernels, attention_forward(): pl.pallas_call(forward_kernel, out_shape=(jax.ShapeDtypeStruct((SEG, D, T...  51.9 us
    all_gather x1, waiting for transfers between devices, per_device(): lax.all_gather(residual_grad_bf, HEAD_AXES, axis=0, tiled=False)  50.3 us
    all_gather x1, waiting for transfers between devices, per_device(): key_values = lax.all_gather(own_kv, KEY_AXES, axis=0, tiled=False)  48.3 us
    all_gather x1, blocking collectives, per_device(): lax.all_gather(jnp.sum(hidden_grad, axis=0).astype(bf16)[None], ROW_AXES,...  43.5 us
    reduce_scatter x1, waiting for transfers between devices, per_device(): lax.psum_scatter(key_value_grad, KEY_AXES, scatter_dimension=0, tiled=False)  39.6 us
  transfers between devices with their start and end apart: 13, of which 10 were waited for; matrix products, arithmetic and copies ran while one was open for 8% of the time, Pallas kernels for 8%

profile of v2, /device:TPU:1, one launch (start us, length us, event | category | flops | bytes accessed | tf_op | source)
XLA Modules:
  0.0 627.0 jit_solution(1479253573811527121)
XLA Ops:
  7.3 2.7 fusion.65
  17.0 2.9 fusion.5
  21.2 23.6 %all_to_all.32 = bf16[16,192,128]{2,1,0:T(8,128)(2,1)S(1)} all-to-all(bf16[16,192,128]{2,1,0:T(8,128)(2,1)S(1)} %pad_maximum_fusion.2), channel_id=1, replica_groups=mesh['seq'=8,'bh'=2,'bl'=2,'tp'=4] {'seq','bh'}, dimensions={0} | all-to-all | bytes 1572864 | tf_op jit(solution)/shard_map/all_to_all | solution.py:229
  48.3 48.3 %all-gather.17.cloned.1.call-done = bf16[128,128,128]{2,1,0:T(8,128)(2,1)} async-done(((bf16[16,128,128]{2,1,0:T(8,128)(2,1)}), bf16[128,128,128]{2,1,0:T(8,128)(2,1)}) %all-gather.17.cloned.1.call-update) | async-done | bytes 4194320 | tf_op jit(solution)/shard_map/all_gather | solution.py:248
  98.8 51.9 %shard_map.245 = (bf16[16,64,128]{2,1,0:T(8,128)(2,1)S(1)}, f32[8,1,256]{2,1,0:T(1,128)S(1)}) custom-call(bf16[16,64,128]{2,1,0:T(8,128)(2,1)S(1)} %slice.118.q_ref, bf16[8,16,128,128]{3,2,1,0:T(8,128)(2,1)S(1)} %bitcast.70), custom_call_target="tpu_custom_call" | custom-call | flops 60000002048 | bytes 5242880 | tf_op jit(solution)/shard_map/pallas_call | solution.py:127
  150.7 4.0 all-gather.19.cloned.1.call-done
  154.7 11.8 %all_to_all.33 = bf16[16,64,128]{2,1,0:T(8,128)(2,1)S(1)} all-to-all(bf16[16,64,128]{2,1,0:T(8,128)(2,1)S(1)} %get-tuple-element.24.ctx_ref), channel_id=1, replica_groups=mesh['seq'=8,'bh'=2,'bl'=2,'tp'=4] {'seq','bh'}, dimensions={0} | all-to-all | bytes 524288 | tf_op jit(solution)/shard_map/all_to_all | solution.py:229
  169.8 20.9 %all-gather.13.cloned.1.call-done = bf16[512,1024]{1,0:T(8,128)(2,1)} async-done(((bf16[128,1024]{1,0:T(8,128)(2,1)}), bf16[512,1024]{1,0:T(8,128)(2,1)}) %all-gather.13.cloned.1.call-update) | async-done | bytes 1048592 | tf_op jit(solution)/shard_map/all_gather | solution.py:258
  190.7 3.2 fusion.69
  194.0 2.4 fusion.68
  197.4 2.3 convolution_convert_fusion.2
  199.8 4.1 convolution_convert_fusion.3
  203.9 19.3 %reduce-scatter.8.cloned.1.call-done = bf16[128,1024]{1,0:T(8,128)(2,1)} async-done(((bf16[512,1024]{1,0:T(8,128)(2,1)}), bf16[128,1024]{1,0:T(8,128)(2,1)}) %reduce-scatter.8.cloned.1.call-update) | async-done | bytes 262160 | tf_op jit(solution)/shard_map/reduce_scatter | solution.py:264
  224.5 24.6 %reduce-scatter.6.cloned.1.call-done = bf16[128,1024]{1,0:T(8,128)(2,1)} async-done(((bf16[512,1024]{1,0:T(8,128)(2,1)}), bf16[128,1024]{1,0:T(8,128)(2,1)}) %reduce-scatter.6.cloned.1.call-update) | async-done | bytes 262160 | tf_op jit(solution)/shard_map/reduce_scatter | solution.py:282
  249.1 2.2 fusion.63
  253.2 17.5 %all_to_all.34.do_ref = bf16[16,64,128]{2,1,0:T(8,128)(2,1)S(1)} all-to-all(bf16[16,64,128]{2,1,0:T(8,128)(2,1)S(1)} %bitcast.77), channel_id=1, replica_groups=mesh['seq'=8,'bh'=2,'bl'=2,'tp'=4] {'seq','bh'}, dimensions={0} | all-to-all | bytes 524288 | tf_op jit(solution)/shard_map/all_to_all | solution.py:229
  270.6 59.5 %shard_map.246 = (bf16[16,64,128]{2,1,0:T(8,128)(2,1)S(1)}, bf16[8,16,128,128]{3,2,1,0:T(8,128)(2,1)S(1)}) custom-call(bf16[16,64,128]{2,1,0:T(8,128)(2,1)S(1)} %slice.118.q_ref, bf16[8,16,128,128]{3,2,1,0:T(8,128)(2,1)} %bitcast.69, bf16[16,64,128]{2,1,0:T(8,128)(2,1)S(1)} %all_to_all.34.do_ref, bf16[16,64,128]{2,1,0:T(8,128)(2,1)S(1)} %get-tuple-element.24.ctx_ref, ...), custom_call_target="tpu_custom_call" | custom-call | flops 74999996416 | bytes 10485760 | tf_op jit(solution)/shard_map/pallas_call | solution.py:188
  333.0 3.0 convolution_convert_fusion.1
  337.6 2.5 pad_maximum_fusion
  341.6 39.6 %reduce-scatter.10.cloned.1.call-done = bf16[1,16,128,128]{3,2,1,0:T(8,128)(2,1)} async-done(((bf16[8,16,128,128]{3,2,1,0:T(8,128)(2,1)}), bf16[1,16,128,128]{3,2,1,0:T(8,128)(2,1)}) %reduce-scatter.10.cloned.1.call-update) | async-done | bytes 524304 | tf_op jit(solution)/shard_map/reduce_scatter | solution.py:294
  384.0 7.2 %all-to-all-start.3 = ((bf16[16,192,128]{2,1,0:T(8,128)(2,1)}), bf16[16,192,128]{2,1,0:T(8,128)(2,1)S(1)}, u32[]{:S(2)}, u32[]{:S(2)}) async-start(bf16[16,192,128]{2,1,0:T(8,128)(2,1)} %copy.99), calls=%async_computation.6 | async-start | bytes 1572864 | tf_op jit(solution)/shard_map/all_to_all | solution.py:229
  391.3 50.3 %all-gather.21.cloned.1.call-done = bf16[2048,1024]{1,0:T(8,128)(2,1)} async-done(((bf16[128,1024]{1,0:T(8,128)(2,1)}), bf16[2048,1024]{1,0:T(8,128)(2,1)}) %all-gather.21.cloned.1.call-update) | async-done | bytes 4194320 | tf_op jit(solution)/shard_map/all_gather | solution.py:288
  441.6 3.1 fusion.28
  445.0 3.6 fusion.16
  449.4 5.2 fusion.51
  456.4 67.2 %reduce-scatter.14.cloned.1.call-done = bf16[64,1024]{1,0:T(8,128)(2,1)} async-done(((bf16[2048,1024]{1,0:T(8,128)(2,1)}), bf16[64,1024]{1,0:T(8,128)(2,1)}) %reduce-scatter.14.cloned.1.call-update) | async-done | bytes 131088 | tf_op jit(solution)/shard_map/reduce_scatter | solution.py:278
  523.6 43.5 %all-gather.3 = bf16[32768]{0:T(1024)(128)(2,1)S(1)} all-gather(bf16[1024]{0:T(1024)(128)(2,1)S(1)} %get-tuple-element.59), channel_id=5, replica_groups=mesh['seq'=8,'bh'=2,'bl'=2,'tp'=4] {'seq','bh','bl'}, dimensions={0}, use_global_device_ids=true | all-gather | bytes 67584 | tf_op jit(solution)/shard_map/all_gather | solution.py:286
  571.5 5.7 all-to-all-start.4
  578.8 5.9 all-to-all-done.4
  585.5 9.9 %all_gather.41 = bf16[32,4224]{1,0:T(8,128)(2,1)S(1)} all-gather(bf16[8,4224]{1,0:T(8,128)(2,1)S(1)} %fusion.61), channel_id=1, replica_groups=mesh['seq'=8,'bh'=2,'bl'=2,'tp'=4] {'tp'}, dimensions={0}, use_global_device_ids=true | all-gather | bytes 337920 | tf_op jit(solution)/shard_map/all_gather | solution.py:360
  598.3 15.4 %all-gather.15.cloned.1.call-done = bf16[2048,1024]{1,0:T(8,128)(2,1)} async-done(((bf16[64,1024]{1,0:T(8,128)(2,1)}), bf16[2048,1024]{1,0:T(8,128)(2,1)}) %all-gather.15.cloned.1.call-update) | async-done | bytes 4194320 | tf_op jit(solution)/shard_map/all_gather | solution.py:279
  613.7 6.8 %slice_convert_fusion = (f32[1024,1024]{1,0:T(8,128)}, f32[1024,1024]{1,0:T(8,128)}) fusion(bf16[2048,1024]{1,0:T(8,128)(2,1)} %all-gather.15.cloned.1.call-done), kind=kLoop, calls=%fused_computation.13 | loop fusion | flops 2097152 | bytes 12582912 | tf_op jit(solution)/shard_map/convert_element_type | solution.py:281
  (179 shorter events, 42.5 us)
Async XLA Ops:
  7.2 186.8 %copy-start = (bf16[1024,1024]{1,0:T(8,128)(2,1)S(1)}, bf16[1024,1024]{1,0:T(8,128)(2,1)}, u32[]{:S(2)}) copy-start(bf16[1024,1024]{1,0:T(8,128)(2,1)} %param.25) | copy-start | bytes 6291460
  7.2 6.8 %copy-start.18 = (f32[2,1024]{1,0:T(2,128)S(1)}, f32[2,1024]{1,0:T(2,128)}, u32[]{:S(2)}) copy-start(f32[2,1024]{1,0:T(2,128)} %param.18) | copy-start | bytes 24580
  7.2 39.3 %all-gather.11.cloned.1.call-start = ((), (), s32[]{:S(2)}) async-start(), calls=%async_computation.10 | async-start | bytes 1310720 | tf_op jit(solution)/shard_map/all_gather | solution.py:232
  10.0 86.6 %all-gather.17.cloned.1.call-start = ((), (), s32[]{:S(2)}) async-start(), calls=%async_computation.18 | async-start | bytes 4718592 | tf_op jit(solution)/shard_map/all_gather | solution.py:248
  14.0 5.9 copy-start.11
  46.5 108.2 %all-gather.19.cloned.1.call-start = ((), (), s32[]{:S(2)}) async-start(), calls=%async_computation.19 | async-start | bytes 4456448 | tf_op jit(solution)/shard_map/all_gather | solution.py:250
  47.3 143.5 %all-gather.13.cloned.1.call-start = ((), (), s32[]{:S(2)}) async-start(), calls=%async_computation.11 | async-start | bytes 1310720 | tf_op jit(solution)/shard_map/all_gather | solution.py:258
  98.8 67.7 %copy-start.4 = (bf16[128,1024]{1,0:T(8,128)(2,1)S(1)}, bf16[128,1024]{1,0:T(8,128)(2,1)}, u32[]{:S(2)}) copy-start(bf16[128,1024]{1,0:T(8,128)(2,1)} %param.14) | copy-start | bytes 786436
  98.8 67.7 %copy-start.23 = (f32[1024]{0:T(1024)S(1)}, f32[1024]{0:T(1024)}, u32[]{:S(2)}) copy-start(f32[1024]{0:T(1024)} %param.20) | copy-start | bytes 12292
  154.7 14.2 %copy-start.16 = (f32[1024]{0:T(1024)S(1)}, f32[1024]{0:T(1024)}, u32[]{:S(2)}) copy-start(f32[1024]{0:T(1024)} %param.21) | copy-start | bytes 12292
  154.7 14.2 %copy-start.24 = (f32[1024]{0:T(1024)S(1)}, f32[1024]{0:T(1024)}, u32[]{:S(2)}) copy-start(f32[1024]{0:T(1024)} %param.22) | copy-start | bytes 12292
  169.8 24.2 %copy-start.29 = (f32[1024]{0:T(1024)S(1)}, f32[1024]{0:T(1024)}, u32[]{:S(2)}) copy-start(f32[1024]{0:T(1024)} %param.24) | copy-start | bytes 12292
  169.8 53.5 %reduce-scatter.8.cloned.1.call-start = ((), (), s32[]{:S(2)}) async-start(), calls=%async_computation.13 | async-start | bytes 1310720 | tf_op jit(solution)/shard_map/reduce_scatter | solution.py:264
  190.7 3.3 copy-start.27
  194.0 3.4 copy-start.26
  199.7 49.4 %copy-start.25 = (f32[1024]{0:T(1024)S(1)}, f32[1024]{0:T(1024)}, u32[]{:S(2)}) copy-start(f32[1024]{0:T(1024)} %param.26) | copy-start | bytes 12292
  199.7 49.3 %reduce-scatter.6.cloned.1.call-start = ((), (), s32[]{:S(2)}) async-start(), calls=%async_computation.12 | async-start | bytes 1310720 | tf_op jit(solution)/shard_map/reduce_scatter | solution.py:282
  203.9 48.3 %copy-start.5 = (bf16[1024,1024]{1,0:T(8,128)(2,1)S(1)}, bf16[1024,1024]{1,0:T(8,128)(2,1)}, u32[]{:S(2)}) copy-start(bf16[1024,1024]{1,0:T(8,128)(2,1)} %param.19) | copy-start | bytes 6291460
  203.9 177.3 %reduce-scatter.10.cloned.1.call-start = ((), (), s32[]{:S(2)}) async-start(), calls=%async_computation.14 | async-start | bytes 4718592 | tf_op jit(solution)/shard_map/reduce_scatter | solution.py:294
  252.1 78.0 %copy-start.10 = (bf16[128,1024]{1,0:T(8,128)(2,1)}, bf16[128,1024]{1,0:T(8,128)(2,1)S(1)}, u32[]{:S(2)}) copy-start(bf16[128,1024]{1,0:T(8,128)(2,1)S(1)} %convert_element_type.106) | copy-start | bytes 786436
  332.1 109.5 %all-gather.21.cloned.1.call-start = ((), (), s32[]{:S(2)}) async-start(), calls=%async_computation.20 | async-start | bytes 4456448 | tf_op jit(solution)/shard_map/all_gather | solution.py:288
  332.9 3.1 copy-start.28
  332.9 190.7 %reduce-scatter.14.cloned.1.call-start = ((), (), s32[]{:S(2)}) async-start(), calls=%async_computation.16 | async-start | bytes 4325376 | tf_op jit(solution)/shard_map/reduce_scatter | solution.py:278
  332.9 3.0 copy-start.31
  384.0 65.2 %all-to-all-start.3 = ((bf16[16,192,128]{2,1,0:T(8,128)(2,1)}), bf16[16,192,128]{2,1,0:T(8,128)(2,1)S(1)}, u32[]{:S(2)}, u32[]{:S(2)}) async-start(bf16[16,192,128]{2,1,0:T(8,128)(2,1)} %copy.99), calls=%async_computation.6 | async-start | bytes 1572864 | tf_op jit(solution)/shard_map/all_to_all | solution.py:229
  391.3 176.5 %reduce-scatter.12.cloned.1.call-start = ((), (), s32[]{:S(2)}) async-start(), calls=%async_computation.15 | async-start | bytes 626688 | tf_op jit(solution)/shard_map/reduce_scatter | solution.py:332
  441.6 3.4 copy-start.13
  455.0 122.2 %copy-start.7 = (f32[128,1024]{1,0:T(8,128)S(1)}, f32[128,1024]{1,0:T(8,128)}, u32[]{:S(2)}) copy-start(f32[128,1024]{1,0:T(8,128)} %copy-done.6) | copy-start | bytes 1572868
  456.4 157.3 %all-gather.15.cloned.1.call-start = ((), (), s32[]{:S(2)}) async-start(), calls=%async_computation.17 | async-start | bytes 4325376 | tf_op jit(solution)/shard_map/all_gather | solution.py:279
  567.8 10.4 %copy-start.14 = (bf16[272,128]{1,0:T(8,128)(2,1)S(1)}, bf16[272,128]{1,0:T(8,128)(2,1)}, u32[]{:S(2)}) copy-start(bf16[272,128]{1,0:T(8,128)(2,1)} %reduce-scatter.12.cloned.1.call-done) | copy-start | bytes 208900
  571.5 13.2 %all-to-all-start.4 = ((bf16[16,2,792]{2,1,0:T(2,128)(2,1)}), bf16[16,2,792]{2,1,0:T(2,128)(2,1)S(1)}, u32[]{:S(2)}, u32[]{:S(2)}) async-start(bf16[16,2,792]{2,1,0:T(2,128)(2,1)} %reshape.211), calls=%async_computation.8 | async-start | bytes 114688 | tf_op jit(solution)/shard_map/all_to_all | solution.py:229
  613.7 6.8 %copy-start.1 = (bf16[1024,1024]{1,0:T(8,128)(2,1)S(1)}, bf16[1024,1024]{1,0:T(8,128)(2,1)}, u32[]{:S(2)}) copy-start(bf16[1024,1024]{1,0:T(8,128)(2,1)} %param.25) | copy-start | bytes 6291460
  (14 other events, 15.8 us)
Sparse Core Ops, SparseCore 0:
  10.3 26.2 all-gather.10
  46.6 49.8 all-gather.16
  99.6 55.0 all-gather.18
  169.9 20.7 all-gather.12
  199.8 23.3 reduce-scatter.7
  225.6 23.3 reduce-scatter.5
  332.3 48.8 reduce-scatter.9
  384.2 57.4 all-gather.20
  445.9 77.7 reduce-scatter.13
  526.5 33.6 reduce-scatter.11
  562.8 50.8 all-gather.14

commit v3 on v2

--- a/solution.py
+++ b/solution.py
@@ -87,7 +87,114 @@
     lax.fori_loop(own + 1, PAIRS, full, 0)
 
 
-def forward_kernel(q_ref, kv_ref, ctx_ref, lse_ref, qb, m_s, l_s, acc):
+def group_index(axes):
+    index = 0
+    for name in axes:
+        index = index * lax.axis_size(name) + lax.axis_index(name)
+    return index
+
+
+def group_device(axes, index):
+    device = {}
+    for name in reversed(axes):
+        device[name] = index % lax.axis_size(name)
+        index = index // lax.axis_size(name)
+    return device
+
+
+def greet(axes, count):
+    me = group_index(axes)
+    barrier = pltpu.get_barrier_semaphore()
+    for hop in range(1, count):
+        pl.semaphore_signal(
+            barrier,
+            inc=1,
+            device_id=group_device(axes, (me + hop) % count),
+            device_id_type=pl.DeviceIdType.MESH,
+        )
+    pl.semaphore_wait(barrier, count - 1)
+    return me
+
+
+def push(source, target, sems, index, axes, peer):
+    send_sem, recv_sem = sems
+    return pltpu.make_async_remote_copy(
+        src_ref=source,
+        dst_ref=target,
+        send_sem=send_sem.at[index],
+        recv_sem=recv_sem.at[index],
+        device_id=group_device(axes, peer),
+        device_id_type=pl.DeviceIdType.MESH,
+    )
+
+
+def exchange_kernel(axes, count, kind, x_ref, o_ref, *scratch):
+    sems = scratch[-2:]
+    landing = scratch[0] if kind == "reduce" else o_ref
+    me = greet(axes, count)
+
+    def block(place):
+        return x_ref if kind == "gather" else x_ref.at[place]
+
+    for hop in range(1, count):
+        peer = (me + hop) % count
+        push(block(peer), landing.at[me], sems, hop - 1, axes, peer).start()
+    if kind != "reduce":
+        landing[me] = block(me)[...]
+    for hop in range(1, count):
+        origin = (me - hop + count) % count
+        push(block(me), landing.at[origin], sems, hop - 1, axes, origin).wait_recv()
+    if kind == "reduce":
+        total = block(me)[...].astype(f32)
+        for hop in range(1, count):
+            total += landing[(me - hop + count) % count].astype(f32)
+        o_ref[...] = total.astype(o_ref.dtype)
+    for hop in range(1, count):
+        peer = (me + hop) % count
+        push(block(peer), landing.at[me], sems, hop - 1, axes, peer).wait_send()
+
+
+def exchange(x, axes, kind, collective_id, out_dtype=bf16):
+    count = 1
+    for name in axes:
+        count *= lax.axis_size(name)
+    block = x.shape if kind == "gather" else x.shape[1:]
+    landing = (count,) + block
+    scratch = [pltpu.SemaphoreType.DMA((count - 1,))] * 2
+    if kind == "reduce":
+        scratch = [pltpu.VMEM(landing, x.dtype)] + scratch
+    return pl.pallas_call(
+        functools.partial(exchange_kernel, axes, count, kind),
+        out_shape=jax.ShapeDtypeStruct(block if kind == "reduce" else landing, out_dtype),
+        in_specs=[WHOLE],
+        out_specs=WHOLE,
+        scratch_shapes=scratch,
+        compiler_params=pltpu.CompilerParams(
+            collective_id=collective_id, has_side_effects=True, vmem_limit_bytes=24 << 20
+        ),
+        cost_estimate=pl.CostEstimate(
+            flops=12_000_000_000, bytes_accessed=4 << 20, transcendentals=0
+        ),
+    )(x)
+
+
+FWD_CHUNK = 4
+BWD_CHUNK = 2
+
+
+def forward_kernel(q_ref, own_ref, ctx_ref, lse_ref, kv_ref, qb, m_s, l_s, acc, *sems):
+    me = greet(KEY_AXES, CYC)
+
+    def send(chunk, hop, place, peer):
+        rows = pl.ds(chunk * FWD_CHUNK, FWD_CHUNK)
+        return push(
+            own_ref.at[rows], kv_ref.at[place, rows], sems, (chunk, hop - 1), KEY_AXES, peer
+        )
+
+    for chunk in range(SEG // FWD_CHUNK):
+        for hop in range(1, CYC):
+            send(chunk, hop, me, (me + hop) % CYC).start()
+    kv_ref[me] = own_ref[...]
     for pair in range(PAIRS):
         q = pair_of(q_ref, pair).astype(f32) * score_scale
         qb[pair] = jnp.concatenate([q, jnp.zeros_like(q)], axis=0).astype(bf16)
@@ -114,39 +221,60 @@
         over_pairs(group, update)
         return carry
 
-    lax.fori_loop(0, SEG, key_step, 0)
+    def chunk_step(chunk, carry):
+        for hop in range(1, CYC):
+            origin = (me - hop + CYC) % CYC
+            send(chunk, hop, origin, origin).wait_recv()
+        return lax.fori_loop(chunk * FWD_CHUNK, (chunk + 1) * FWD_CHUNK, key_step, carry)
+
+    lax.fori_loop(0, SEG // FWD_CHUNK, chunk_step, 0)
     for pair in range(PAIRS):
         row_sum = l_s[pair]
         o = (acc[pair] / row_sum).astype(bf16)
         ctx_ref[2 * pair] = o[:, :T]
         ctx_ref[2 * pair + 1] = o[:, T:]
         lse_ref[pair] = m_s[pair] + jnp.log(row_sum)
-
-
-def attention_forward(queries, key_values):
+    for chunk in range(SEG // FWD_CHUNK):
+        for hop in range(1, CYC):
+            send(chunk, hop, me, (me + hop) % CYC).wait_send()
+
+
+def attention_forward(queries, own_kv):
     return pl.pallas_call(
         forward_kernel,
         out_shape=(
             jax.ShapeDtypeStruct((SEG, D, T), bf16),
             jax.ShapeDtypeStruct((PAIRS, 1, 2 * T), f32),
+            jax.ShapeDtypeStruct((CYC, SEG, T, 2 * D), bf16),
         ),
         in_specs=[WHOLE] * 2,
-        out_specs=(WHOLE,) * 2,
+        out_specs=(WHOLE,) * 3,
         scratch_shapes=[
             pltpu.VMEM((PAIRS, 2 * D, 2 * T), bf16),
             pltpu.VMEM((PAIRS, 1, 2 * T), f32),
             pltpu.VMEM((PAIRS, 1, 2 * T), f32),
             pltpu.VMEM((PAIRS, D, 2 * T), f32),
-        ],
-        compiler_params=pltpu.CompilerParams(vmem_limit_bytes=40 << 20),
+        ]
+        + [pltpu.SemaphoreType.DMA((SEG // FWD_CHUNK, CYC - 1))] * 2,
+        compiler_params=pltpu.CompilerParams(
+            collective_id=0, has_side_effects=True, vmem_limit_bytes=40 << 20
+        ),
         cost_estimate=pl.CostEstimate(
-            flops=60_000_000_000, bytes_accessed=5 << 20, transcendentals=0
-        ),
-    )(queries, key_values)
-
-
-def backward_kernel(q_ref, kv_ref, do_ref, ctx_ref, lse_ref, dq_ref, dkv_ref,
-                    w, w_t, delta, dqt, dkv_s):
+            flops=70_000_000_000, bytes_accessed=5 << 20, transcendentals=0
+        ),
+    )(queries, own_kv)
+
+
+def backward_kernel(q_ref, kv_ref, do_ref, ctx_ref, lse_ref, grad_ref,
+                    w, w_t, delta, dqt, dkv_s, staged, landed, *sems):
+    me = greet(KEY_AXES, CYC)
+
+    def send(chunk, hop, place, source, peer):
+        rows = pl.ds(chunk * BWD_CHUNK, BWD_CHUNK)
+        return push(
+            staged.at[source, rows], landed.at[place, rows], sems, (chunk, hop - 1), KEY_AXES, peer
+        )
+
     for pair in range(PAIRS):
         q = pair_of(q_ref, pair).astype(f32) * score_scale
         do = pair_of(do_ref, pair).astype(f32)
@@ -174,35 +302,65 @@
             dqt[pair] += dot(k_t, ds)
 
         over_pairs(group, update)
-        dkv_ref[:, group] = dkv_s[...].reshape(CYC, T, T).astype(bf16)
+        staged[:, group] = dkv_s[...].reshape(CYC, T, T).astype(bf16)
         return carry
 
-    lax.fori_loop(0, SEG, key_step, 0)
+    chunks = SEG // BWD_CHUNK
+
+    def chunk_step(step, carry):
+        carry = lax.fori_loop(step * BWD_CHUNK, (step + 1) * BWD_CHUNK, key_step, carry)
+        for hop in range(1, CYC):
+            peer = (me + hop) % CYC
+            send(chunks - 1 - step, hop, me, peer, peer).start()
+        return carry
+
+    lax.fori_loop(0, chunks, chunk_step, 0)
     for pair in range(PAIRS):
         d = (dqt[pair] * score_scale).astype(bf16)
-        dq_ref[2 * pair] = d[:, :T]
-        dq_ref[2 * pair + 1] = d[:, T:]
+        grad_ref[2 * pair, :D] = d[:, :T]
+        grad_ref[2 * pair + 1, :D] = d[:, T:]
+
+    def finish(step, carry):
+        chunk = chunks - 1 - step
+        for hop in range(1, CYC):
+            origin = (me - hop + CYC) % CYC
+            send(chunk, hop, origin, me, origin).wait_recv()
+        for part in range(BWD_CHUNK):
+            group = chunk * BWD_CHUNK + part
+            total = staged[me, group].astype(f32)
+            for hop in range(1, CYC):
+                total += landed[(me - hop + CYC) % CYC, group].astype(f32)
+            grad_ref[group, D:] = total.T.astype(bf16)
+        return carry
+
+    lax.fori_loop(0, chunks, finish, 0)
+    for chunk in range(chunks):
+        for hop in range(1, CYC):
+            peer = (me + hop) % CYC
+            send(chunk, hop, me, peer, peer).wait_send()
 
 
 def attention_backward(queries, key_values, context_grad, context, log_total):
     return pl.pallas_call(
         backward_kernel,
-        out_shape=(
-            jax.ShapeDtypeStruct((SEG, D, T), bf16),
-            jax.ShapeDtypeStruct(key_values.shape, bf16),
-        ),
+        out_shape=jax.ShapeDtypeStruct((SEG, 3 * D, T), bf16),
         in_specs=[WHOLE] * 5,
-        out_specs=(WHOLE,) * 2,
+        out_specs=WHOLE,
         scratch_shapes=[
             pltpu.VMEM((PAIRS, T, 4 * T), bf16),
             pltpu.VMEM((PAIRS, 4 * T, T), bf16),
             pltpu.VMEM((PAIRS, 1, 2 * T), f32),
             pltpu.VMEM((PAIRS, D, 2 * T), f32),
             pltpu.VMEM((N, T), f32),
-        ],
-        compiler_params=pltpu.CompilerParams(vmem_limit_bytes=48 << 20),
+            pltpu.VMEM((CYC, SEG, T, T), bf16),
+            pltpu.VMEM((CYC, SEG, T, T), bf16),
+        ]
+        + [pltpu.SemaphoreType.DMA((SEG // BWD_CHUNK, CYC - 1))] * 2,
+        compiler_params=pltpu.CompilerParams(
+            collective_id=1, has_side_effects=True, vmem_limit_bytes=48 << 20
+        ),
         cost_estimate=pl.CostEstimate(
-            flops=75_000_000_000, bytes_accessed=10 << 20, transcendentals=0
+            flops=80_000_000_000, bytes_accessed=10 << 20, transcendentals=0
         ),
     )(queries, key_values, context_grad, context, log_total)
 
@@ -245,25 +403,24 @@
     arrived = swap_heads(sent)
     query_t, own_kv = arrived[:, :D], arrived[:, D:]
     own_kv, gathered_cot = lax.optimization_barrier((own_kv, gathered_cot))
-    key_values = lax.all_gather(own_kv, KEY_AXES, axis=0, tiled=False)
-    key_values = key_values.reshape(CYC, SEG, tokens, 2 * D)
     normed_all = lax.all_gather(normed_bf, HEAD_AXES, axis=0, tiled=False)
     normed_all = normed_all.reshape(SEG, tokens, width)
-    context_heads, log_total = attention_forward(query_t, key_values)
+    context_heads, log_total, key_values = attention_forward(query_t, own_kv)
     context_heads, normed_all = lax.optimization_barrier((context_heads, normed_all))
 
     context_t = swap_heads(context_heads).reshape(width, tokens)
     residual = hidden_f + product("ct,cd->td", context_t, out_weight) + out_bias
     scaled_two, inverse_two, normed_two = normalize(residual, ln2_gain, ln2_bias)
-    gathered_norm = lax.all_gather(normed_two.astype(bf16), "tp", axis=0, tiled=True)
+    gathered_norm = exchange(normed_two.astype(bf16), ("tp",), "gather", 2)
+    gathered_norm = gathered_norm.reshape(-1, width)
     hidden_pre = dot(gathered_norm, fc_weight) + fc_bias
     gelu_value, gelu_slope = gelu_pair(hidden_pre)
     activation = gelu_value.astype(bf16)
     hidden_grad = dot(gathered_cot, proj_weight.T) * gelu_slope
     hidden_grad_bf = hidden_grad.astype(bf16)
-    normed_two_grad = lax.psum_scatter(
-        dot(hidden_grad_bf, fc_weight.T).astype(bf16), "tp", scatter_dimension=0, tiled=True
-    ).astype(f32)
+    normed_two_grad = exchange(
+        dot(hidden_grad_bf, fc_weight.T).astype(bf16).reshape(-1, tokens, width), ("tp",), "reduce", 3, f32
+    )
     residual_grad = cotangent + norm_back(normed_two_grad, scaled_two, inverse_two, ln2_gain)
     residual_grad_bf = residual_grad.astype(bf16)
     context_grad = product("td,cd->ct", residual_grad_bf, out_weight).astype(bf16)
@@ -275,26 +432,29 @@
             product("tf,td->fd", activation, gathered_cot),
         ]
     ).astype(bf16)
+    context_grad_heads, wide_grads = lax.optimization_barrier((context_grad_heads, wide_grads))
     wide_part = lax.psum_scatter(wide_grads, ROW_AXES, scatter_dimension=0, tiled=True)
+    head_grads = attention_backward(
+        query_t, key_values, context_grad_heads, context_heads, log_total
+    )
+    head_grads, wide_part, activation = lax.optimization_barrier((head_grads, wide_part, activation))
+
+    bias_sum = jnp.sum(hidden_grad, axis=0).astype(bf16)
+    bias_sum += lax.ppermute(bias_sum, "bl", [(0, 1), (1, 0)])
+    riding = jnp.concatenate([residual_grad_bf, jnp.pad(bias_sum[None], ((0, 15), (0, 0)))])
+    riding = lax.all_gather(riding, HEAD_AXES, axis=0, tiled=False)
+    riding = riding.reshape(SEG, tokens + 16, width)
+    residual_grad_all = riding[:, :tokens]
+    fc_bias_grad = jnp.sum(riding[:, tokens].astype(f32), axis=0)
+    wide_part, riding = lax.optimization_barrier((wide_part, riding))
     wide_sum = lax.all_gather(wide_part, ROW_AXES, axis=0, tiled=True)
     fc_weight_grad = wide_sum[:width].astype(f32)
     proj_weight_grad = wide_sum[width:].astype(f32)
-    mlp_out = lax.psum_scatter(
-        dot(activation, proj_weight).astype(bf16), "tp", scatter_dimension=0, tiled=True
-    ).astype(f32)
+    mlp_out = exchange(
+        dot(activation, proj_weight).astype(bf16).reshape(-1, tokens, width), ("tp",), "reduce", 4, f32
+    )
     block_out = residual + mlp_out + proj_bias
-    bias_parts = lax.all_gather(jnp.sum(hidden_grad, axis=0).astype(bf16)[None], ROW_AXES, axis=0, tiled=True)
-    fc_bias_grad = jnp.sum(bias_parts.astype(f32), axis=0)
-    residual_grad_all = lax.all_gather(residual_grad_bf, HEAD_AXES, axis=0, tiled=False)
-    residual_grad_all = residual_grad_all.reshape(SEG, tokens, width)
-
-    query_grad, key_value_grad = attention_backward(
-        query_t, key_values, context_grad_heads, context_heads, log_total
-    )
-    key_value_own = lax.psum_scatter(
-        key_value_grad, KEY_AXES, scatter_dimension=0, tiled=False
-    )
-    head_grads = jnp.concatenate([query_grad, key_value_own.transpose(0, 2, 1)], axis=1)
+
     token_grads = swap_heads(head_grads).reshape(SEG, 3, D, tokens)
     token_grads = token_grads.transpose(1, 0, 2, 3).reshape(3 * width, tokens)
     normed_one_grad = product("ft,df->td", token_grads, qkv_weight)
@@ -329,9 +489,7 @@
     length = packed.shape[1]
     padded = -length % (16 * T)
     packed = jnp.pad(packed, ((0, 0), (0, padded)))
-    summed = lax.psum_scatter(
-        packed.reshape(-1, T), KEY_AXES, scatter_dimension=0, tiled=True
-    ).reshape(-1)
+    summed = exchange(packed.reshape(CYC, -1, T), KEY_AXES, "reduce", 5).reshape(-1)
     qkv_size, vector_size = SEG * fine * 3 * D, SEG * count * fine
     to_rows = jnp.concatenate(
         [

time: 628 us -> 448 us (0.71)
  waiting for transfers between devices: 297 us -> 82.9 us
  Pallas kernels: 111 us -> 195 us
  blocking collectives: 106 us -> 56.4 us
  local copies, waits for them, and re-layouts: 23.1 us -> 16.8 us
  starting transfers between devices: 13.4 us -> 19.7 us
    reduce_scatter x4 -> x0, waiting for transfers between devices: 83.5 us -> none  [the longest x1 39.6 us: per_device(): lax.psum_scatter(key_value_grad, KEY_AXES, scatter_dimension=0, tiled=False)]
    pallas_call x1 -> x5, Pallas kernels: 59.5 us -> 125 us  [the longest x1 68.1 us: attention_backward(): pl.pallas_call(backward_kernel, out_shape=jax.ShapeDtypeStruct((SEG, 3 *...]
    reduce_scatter x1, waiting for transfers between devices: 67.2 us -> 9.34 us  [per_device(): lax.psum_scatter(wide_grads, ROW_AXES, scatter_dimension=0, tiled=True)]
    all_gather x3 -> x1, waiting for transfers between devices: 119 us -> 62.2 us  [per_device(): riding = lax.all_gather(riding, HEAD_AXES, axis=0, tiled=False)]
    all_gather x1 -> x0, blocking collectives: 43.5 us -> none  [per_device(): lax.all_gather(jnp.sum(hidden_grad, axis=0).astype(bf16)[None], ROW_AXES,...]
    pallas_call x1, Pallas kernels: 51.9 us -> 69.9 us  [attention_forward(): pl.pallas_call(forward_kernel, out_shape=(jax.ShapeDtypeStruct((SEG, D, T...]
    all_gather x1, waiting for transfers between devices: 15.4 us -> 0.01 us  [per_device(): wide_sum = lax.all_gather(wide_part, ROW_AXES, axis=0, tiled=True)]
    all_to_all x3 -> x2, blocking collectives: 52.8 us -> 46.4 us  [swap_heads(): lax.all_to_all(parts, HEAD_AXES, split_axis=0, concat_axis=0, tiled=True)]
  transfers between devices with their start and end apart: 13 -> 9, of which waited for: 10 -> 6; matrix products, arithmetic and copies ran while one was open for 8% -> 10% of each run, Pallas kernels for 8% -> 37%
where the time goes in v3:
time: 448 us; the launch traced here: 445 us
  Pallas kernels  195 us (44%)
  waiting for transfers between devices  82.9 us (19%)
  blocking collectives  56.4 us (13%)
  matrix products  35.8 us (8%)
  other arithmetic  24.1 us (5%)
  starting transfers between devices  19.7 us (4%)
  local copies, waits for them, and re-layouts  16.8 us (4%)
  between operations  14.5 us (3%)
    pallas_call x1, Pallas kernels, attention_forward(): pl.pallas_call(forward_kernel, out_shape=(jax.ShapeDtypeStruct((SEG, D, T...  69.9 us
    pallas_call x1, Pallas kernels, attention_backward(): pl.pallas_call(backward_kernel, out_shape=jax.ShapeDtypeStruct((SEG, 3 *...  68.1 us
    all_gather x1, waiting for transfers between devices, per_device(): riding = lax.all_gather(riding, HEAD_AXES, axis=0, tiled=False)  62.2 us
    pallas_call x4, Pallas kernels, exchange(): pl.pallas_call(functools.partial(exchange_kernel, axes, count, kind), out...  57.3 us
    all_to_all x2, blocking collectives, swap_heads(): lax.all_to_all(parts, HEAD_AXES, split_axis=0, concat_axis=0, tiled=True)  46.4 us
    dot_general x8, matrix products, product(): return jnp.einsum(spec, a, b, preferred_element_type=f32)  23.2 us
    all_to_all x3, starting transfers between devices, swap_heads(): lax.all_to_all(parts, HEAD_AXES, split_axis=0, concat_axis=0, tiled=True)  18.7 us
    dot_general x5, matrix products, dot(): return jnp.dot(a, b, preferred_element_type=f32)  12.6 us
  transfers between devices with their start and end apart: 9, of which 6 were waited for; matrix products, arithmetic and copies ran while one was open for 10% of the time, Pallas kernels for 37%

profile of v3, /device:TPU:1, one launch (start us, length us, event | category | flops | bytes accessed | tf_op | source)
XLA Modules:
  0.0 445.5 jit_solution(2230183045189637472)
XLA Ops:
  7.3 2.7 fusion.66
  14.3 3.0 fusion.7
  18.2 2.0 fusion.26
  20.5 23.6 %all_to_all.32 = bf16[16,192,128]{2,1,0:T(8,128)(2,1)S(1)} all-to-all(bf16[16,192,128]{2,1,0:T(8,128)(2,1)S(1)} %pad_maximum_fusion.1), channel_id=1, replica_groups=mesh['seq'=8,'bh'=2,'bl'=2,'tp'=4] {'seq','bh'}, dimensions={0} | all-to-all | bytes 1572864 | tf_op jit(solution)/shard_map/all_to_all | solution.py:387
  44.2 69.9 %shard_map.245 = (bf16[16,64,128]{2,1,0:T(8,128)(2,1)S(1)}, f32[8,1,256]{2,1,0:T(1,128)S(1)}, bf16[8,16,128,128]{3,2,1,0:T(8,128)(2,1)S(1)}) custom-call(bf16[16,64,128]{2,1,0:T(8,128)(2,1)S(1)} %slice.126.q_ref, bf16[16,128,128]{2,1,0:T(8,128)(2,1)S(1)} %slice.127.own_ref), custom_call_target="tpu_custom_call" | custom-call | flops 70000001024 | bytes 5242880 | tf_op jit(solution)/shard_map/pallas_call | solution.py:243
  114.1 2.0 copy-done.2
  116.9 22.8 %all_to_all.33 = bf16[16,64,128]{2,1,0:T(8,128)(2,1)S(1)} all-to-all(bf16[16,64,128]{2,1,0:T(8,128)(2,1)S(1)} %get-tuple-element.29.ctx_ref), channel_id=1, replica_groups=mesh['seq'=8,'bh'=2,'bl'=2,'tp'=4] {'seq','bh'}, dimensions={0} | all-to-all | bytes 524288 | tf_op jit(solution)/shard_map/all_to_all | solution.py:387
  139.7 2.1 fusion.68
  142.2 17.4 %shard_map.246 = bf16[4,128,1024]{2,1,0:T(8,128)(2,1)S(1)} custom-call(bf16[128,1024]{1,0:T(8,128)(2,1)S(1)} %add_convert_fusion.x_ref), custom_call_target="tpu_custom_call" | custom-call | flops 12000000000 | bytes 4194304 | tf_op jit(solution)/shard_map/pallas_call | solution.py:166
  159.7 2.7 multiply_convert_fusion
  162.4 2.4 fusion.69
  166.1 2.6 convolution_convert_fusion.1
  168.8 13.3 %shard_map.247 = f32[128,1024]{1,0:T(8,128)S(1)} custom-call(bf16[4,128,1024]{2,1,0:T(8,128)(2,1)S(1)} %bitcast.78), custom_call_target="tpu_custom_call" | custom-call | flops 12000000000 | bytes 4194304 | tf_op jit(solution)/shard_map/pallas_call | solution.py:166
  187.5 6.0 %all-to-all-start.2 = ((bf16[16,64,128]{2,1,0:T(8,128)(2,1)}), bf16[16,64,128]{2,1,0:T(8,128)(2,1)S(1)}, u32[]{:S(2)}, u32[]{:S(2)}) async-start(bf16[16,64,128]{2,1,0:T(8,128)(2,1)} %bitcast.12), calls=%async_computation.2 | async-start | bytes 524288 | tf_op jit(solution)/shard_map/all_to_all | solution.py:387
  193.6 3.0 convolution_convert_fusion
  196.6 2.5 pad_maximum_fusion
  199.0 3.2 all-to-all-done.2.do_ref
  205.9 2.3 copy-done.3
  208.2 68.1 %shard_map.248 = bf16[16,192,128]{2,1,0:T(8,128)(2,1)} custom-call(bf16[16,64,128]{2,1,0:T(8,128)(2,1)S(1)} %slice.126.q_ref, bf16[8,16,128,128]{3,2,1,0:T(8,128)(2,1)S(1)} %copy-done.3, bf16[16,64,128]{2,1,0:T(8,128)(2,1)S(1)} %all-to-all-done.2.do_ref, bf16[16,64,128]{2,1,0:T(8,128)(2,1)S(1)} %get-tuple-element.29.ctx_ref, ...), custom_call_target="tpu_custom_call" | custom-call | flops 80000000000 | bytes 10485760 | tf_op jit(solution)/shard_map/pallas_call | solution.py:344
  276.2 9.3 %reduce-scatter.2.cloned.1.call-done = bf16[64,1024]{1,0:T(8,128)(2,1)} async-done(((bf16[2048,1024]{1,0:T(8,128)(2,1)}), bf16[64,1024]{1,0:T(8,128)(2,1)}) %reduce-scatter.2.cloned.1.call-update) | async-done | bytes 131088 | tf_op jit(solution)/shard_map/reduce_scatter | solution.py:436
  285.6 62.2 %all-gather.13.cloned.1.call-done = bf16[2304,1024]{1,0:T(8,128)(2,1)} async-done(((bf16[144,1024]{1,0:T(8,128)(2,1)}), bf16[2304,1024]{1,0:T(8,128)(2,1)}) %all-gather.13.cloned.1.call-update) | async-done | bytes 4718608 | tf_op jit(solution)/shard_map/all_gather | solution.py:445
  348.3 4.3 all-to-all-start.3
  352.6 3.2 convolution_convert_fusion.2
  355.7 15.7 %shard_map.249 = f32[128,1024]{1,0:T(8,128)S(1)} custom-call(bf16[4,128,1024]{2,1,0:T(8,128)(2,1)S(1)} %bitcast.79), custom_call_target="tpu_custom_call" | custom-call | flops 12000000000 | bytes 4194304 | tf_op jit(solution)/shard_map/pallas_call | solution.py:166
  372.9 3.4 fusion.18
  379.2 5.4 %fusion.57 = (bf16[1024]{0:T(1024)(128)(2,1)S(1)}, f32[128]{0:T(128)S(1)}, f32[128]{0:T(128)S(1)}, bf16[1024]{0:T(1024)(128)(2,1)S(1)}, f32[128,1024]{1,0:T(8,128)S(1)}) fusion(bf16[128,1024]{1,0:T(8,128)(2,1)S(1)} %copy-done.4, f32[128]{0:T(128)S(1)} %copy-done.20, f32[128]{0:T(128)S(1)} %copy-done.18, f32[1024]{0:T(1024)S(1)} %copy-done.13, ...), kind=kOutput, calls=%fused_computation.62 | convolution fusion | flops 806614784 | bytes 7874560 | tf_op jit(solution)/shard_map/ft,df->td/dot_general | solution.py:61
  386.2 3.1 fusion.33
  389.5 10.9 %shard_map.250 = bf16[272,128]{1,0:T(8,128)(2,1)S(1)} custom-call(bf16[8,272,128]{2,1,0:T(8,128)(2,1)S(1)} %bitcast.75), custom_call_target="tpu_custom_call" | custom-call | flops 12000000000 | bytes 4194304 | tf_op jit(solution)/shard_map/pallas_call | solution.py:166
  402.6 8.4 %all-to-all-start.4 = ((bf16[16,2,792]{2,1,0:T(2,128)(2,1)}), bf16[16,2,792]{2,1,0:T(2,128)(2,1)S(1)}, u32[]{:S(2)}, u32[]{:S(2)}) async-start(bf16[16,2,792]{2,1,0:T(2,128)(2,1)} %reshape.213), calls=%async_computation.5 | async-start | bytes 114688 | tf_op jit(solution)/shard_map/all_to_all | solution.py:387
  413.2 5.3 %all-to-all-done.4 = bf16[16,2,792]{2,1,0:T(2,128)(2,1)S(1)} async-done(((bf16[16,2,792]{2,1,0:T(2,128)(2,1)}), bf16[16,2,792]{2,1,0:T(2,128)(2,1)S(1)}, u32[]{:S(2)}, u32[]{:S(2)}) %all-to-all-start.4) | async-done | bytes 50720 | tf_op jit(solution)/shard_map/all_to_all | solution.py:387
  419.3 10.0 %all_gather.26 = bf16[32,4224]{1,0:T(8,128)(2,1)S(1)} all-gather(bf16[8,4224]{1,0:T(8,128)(2,1)S(1)} %fusion.63), channel_id=1, replica_groups=mesh['seq'=8,'bh'=2,'bl'=2,'tp'=4] {'tp'}, dimensions={0}, use_global_device_ids=true | all-gather | bytes 337920 | tf_op jit(solution)/shard_map/all_gather | solution.py:518
  432.1 6.8 %slice_convert_fusion = (f32[1024,1024]{1,0:T(8,128)}, f32[1024,1024]{1,0:T(8,128)}) fusion(bf16[2048,1024]{1,0:T(8,128)(2,1)} %all-gather.9.cloned.1.call-done), kind=kLoop, calls=%fused_computation.15 | loop fusion | flops 2097152 | bytes 12582912 | tf_op jit(solution)/shard_map/convert_element_type | solution.py:452
  (155 shorter events, 31.4 us)
Async XLA Ops:
  7.2 152.5 %copy-start = (bf16[1024,1024]{1,0:T(8,128)(2,1)S(1)}, bf16[1024,1024]{1,0:T(8,128)(2,1)}, u32[]{:S(2)}) copy-start(bf16[1024,1024]{1,0:T(8,128)(2,1)} %param.23) | copy-start | bytes 6291460
  7.2 7.0 %copy-start.16 = (f32[2,1024]{1,0:T(2,128)S(1)}, f32[2,1024]{1,0:T(2,128)}, u32[]{:S(2)}) copy-start(f32[2,1024]{1,0:T(2,128)} %param.18) | copy-start | bytes 24580
  7.2 37.0 %all-gather.7.cloned.1.call-start = ((), (), s32[]{:S(2)}) async-start(), calls=%async_computation.6 | async-start | bytes 1310720 | tf_op jit(solution)/shard_map/all_gather | solution.py:390
  10.0 106.9 %all-gather.11.cloned.1.call-start = ((), (), s32[]{:S(2)}) async-start(), calls=%async_computation.9 | async-start | bytes 4456448 | tf_op jit(solution)/shard_map/all_gather | solution.py:406
  11.1 3.1 copy-start.17
  44.1 95.5 %copy-start.4 = (bf16[128,1024]{1,0:T(8,128)(2,1)S(1)}, bf16[128,1024]{1,0:T(8,128)(2,1)}, u32[]{:S(2)}) copy-start(bf16[128,1024]{1,0:T(8,128)(2,1)} %param.14) | copy-start | bytes 786436
  44.1 95.5 %copy-start.21 = (f32[1024]{0:T(1024)S(1)}, f32[1024]{0:T(1024)}, u32[]{:S(2)}) copy-start(f32[1024]{0:T(1024)} %param.20) | copy-start | bytes 12292
  114.1 2.0 copy-start.2
  116.8 25.2 %copy-start.14 = (f32[1024]{0:T(1024)S(1)}, f32[1024]{0:T(1024)}, u32[]{:S(2)}) copy-start(f32[1024]{0:T(1024)} %param.21) | copy-start | bytes 12292
  116.9 25.2 %copy-start.22 = (f32[1024]{0:T(1024)S(1)}, f32[1024]{0:T(1024)}, u32[]{:S(2)}) copy-start(f32[1024]{0:T(1024)} %param.22) | copy-start | bytes 12292
  142.2 17.4 %copy-start.26 = (f32[1024]{0:T(1024)S(1)}, f32[1024]{0:T(1024)}, u32[]{:S(2)}) copy-start(f32[1024]{0:T(1024)} %param.24) | copy-start | bytes 12292
  159.6 2.7 copy-start.24
  159.7 2.7 copy-start.25
  168.8 13.6 %copy-start.10 = (f32[128,1024]{1,0:T(8,128)S(1)}, f32[128,1024]{1,0:T(8,128)}, u32[]{:S(2)}) copy-start(f32[128,1024]{1,0:T(8,128)} %param.27) | copy-start | bytes 1572868
  182.1 2.1 copy-start.5
  187.5 14.7 %all-to-all-start.2 = ((bf16[16,64,128]{2,1,0:T(8,128)(2,1)}), bf16[16,64,128]{2,1,0:T(8,128)(2,1)S(1)}, u32[]{:S(2)}, u32[]{:S(2)}) async-start(bf16[16,64,128]{2,1,0:T(8,128)(2,1)} %bitcast.12), calls=%async_computation.2 | async-start | bytes 524288 | tf_op jit(solution)/shard_map/all_to_all | solution.py:387
  193.5 92.1 %reduce-scatter.2.cloned.1.call-start = ((), (), s32[]{:S(2)}) async-start(), calls=%async_computation.7 | async-start | bytes 4325376 | tf_op jit(solution)/shard_map/reduce_scatter | solution.py:436
  193.6 3.0 copy-start.11
  199.0 5.8 %copy-start.9 = (bf16[128,1024]{1,0:T(8,128)(2,1)S(1)}, bf16[128,1024]{1,0:T(8,128)(2,1)}, u32[]{:S(2)}) copy-start(bf16[128,1024]{1,0:T(8,128)(2,1)} %copy-done.8) | copy-start | bytes 786436
  202.3 145.5 %all-gather.13.cloned.1.call-start = ((), (), s32[]{:S(2)}) async-start(), calls=%async_computation.10 | async-start | bytes 5013504 | tf_op jit(solution)/shard_map/all_gather | solution.py:445
  202.3 2.5 collective-permute-start
  205.6 226.5 %all-gather.9.cloned.1.call-start = ((), (), s32[]{:S(2)}) async-start(), calls=%async_computation.8 | async-start | bytes 4325376 | tf_op jit(solution)/shard_map/all_gather | solution.py:450
  205.9 2.3 copy-start.3
  208.2 139.7 %copy-start.15 = (bf16[1024]{0:T(1024)(128)(2,1)S(1)}, bf16[1024]{0:T(1024)(128)(2,1)}, u32[]{:S(2)}) copy-start(bf16[1024]{0:T(1024)(128)(2,1)} %get-tuple-element.60) | copy-start | bytes 6148
  348.3 29.7 %all-to-all-start.3 = ((bf16[16,192,128]{2,1,0:T(8,128)(2,1)}), bf16[16,192,128]{2,1,0:T(8,128)(2,1)}, u32[]{:S(2)}, u32[]{:S(2)}) async-start(bf16[16,192,128]{2,1,0:T(8,128)(2,1)} %shard_map.248), calls=%async_computation.4 | async-start | bytes 1572864 | tf_op jit(solution)/shard_map/all_to_all | solution.py:387
  372.9 4.1 copy-start.23
  376.6 2.5 copy-start.13
  376.6 2.5 copy-start.18
  376.6 2.5 copy-start.20
  379.2 6.0 %copy-start.7 = (f32[128,1024]{1,0:T(8,128)S(1)}, f32[128,1024]{1,0:T(8,128)}, u32[]{:S(2)}) copy-start(f32[128,1024]{1,0:T(8,128)} %copy-done.6) | copy-start | bytes 1572868
  402.6 15.9 %all-to-all-start.4 = ((bf16[16,2,792]{2,1,0:T(2,128)(2,1)}), bf16[16,2,792]{2,1,0:T(2,128)(2,1)S(1)}, u32[]{:S(2)}, u32[]{:S(2)}) async-start(bf16[16,2,792]{2,1,0:T(2,128)(2,1)} %reshape.213), calls=%async_computation.5 | async-start | bytes 114688 | tf_op jit(solution)/shard_map/all_to_all | solution.py:387
  432.1 6.8 %copy-start.1 = (bf16[1024,1024]{1,0:T(8,128)(2,1)S(1)}, bf16[1024,1024]{1,0:T(8,128)(2,1)}, u32[]{:S(2)}) copy-start(bf16[1024,1024]{1,0:T(8,128)(2,1)} %param.23) | copy-start | bytes 6291460
  (4 other events, 4.5 us)
Sparse Core Ops, SparseCore 0:
  10.3 26.3 all-gather.6
  39.7 77.1 all-gather.10
  202.4 83.1 reduce-scatter.1
  288.8 58.9 all-gather.12
  350.2 46.1 all-gather.8

commit v4 on v3

--- a/solution.py
+++ b/solution.py
@@ -102,18 +102,25 @@
     return device
 
 
-def greet(axes, count):
-    me = group_index(axes)
+def size_of(axes):
+    count = 1
+    for name in axes:
+        count *= lax.axis_size(name)
+    return count
+
+
+def greet(*groups):
     barrier = pltpu.get_barrier_semaphore()
-    for hop in range(1, count):
-        pl.semaphore_signal(
-            barrier,
-            inc=1,
-            device_id=group_device(axes, (me + hop) % count),
-            device_id_type=pl.DeviceIdType.MESH,
-        )
-    pl.semaphore_wait(barrier, count - 1)
-    return me
+    for axes in groups:
+        me, count = group_index(axes), size_of(axes)
+        for hop in range(1, count):
+            pl.semaphore_signal(
+                barrier,
+                inc=1,
+                device_id=group_device(axes, (me + hop) % count),
+                device_id_type=pl.DeviceIdType.MESH,
+            )
+    pl.semaphore_wait(barrier, sum(size_of(axes) - 1 for axes in groups))
 
 
 def push(source, target, sems, index, axes, peer):
@@ -128,54 +135,84 @@
     )
 
 
-def exchange_kernel(axes, count, kind, x_ref, o_ref, *scratch):
-    sems = scratch[-2:]
-    landing = scratch[0] if kind == "reduce" else o_ref
-    me = greet(axes, count)
-
-    def block(place):
-        return x_ref if kind == "gather" else x_ref.at[place]
-
-    for hop in range(1, count):
-        peer = (me + hop) % count
-        push(block(peer), landing.at[me], sems, hop - 1, axes, peer).start()
-    if kind != "reduce":
-        landing[me] = block(me)[...]
-    for hop in range(1, count):
-        origin = (me - hop + count) % count
-        push(block(me), landing.at[origin], sems, hop - 1, axes, origin).wait_recv()
-    if kind == "reduce":
-        total = block(me)[...].astype(f32)
-        for hop in range(1, count):
-            total += landing[(me - hop + count) % count].astype(f32)
-        o_ref[...] = total.astype(o_ref.dtype)
-    for hop in range(1, count):
-        peer = (me + hop) % count
-        push(block(peer), landing.at[me], sems, hop - 1, axes, peer).wait_send()
-
-
-def exchange(x, axes, kind, collective_id, out_dtype=bf16):
-    count = 1
-    for name in axes:
-        count *= lax.axis_size(name)
-    block = x.shape if kind == "gather" else x.shape[1:]
-    landing = (count,) + block
-    scratch = [pltpu.SemaphoreType.DMA((count - 1,))] * 2
-    if kind == "reduce":
-        scratch = [pltpu.VMEM(landing, x.dtype)] + scratch
-    return pl.pallas_call(
-        functools.partial(exchange_kernel, axes, count, kind),
-        out_shape=jax.ShapeDtypeStruct(block if kind == "reduce" else landing, out_dtype),
-        in_specs=[WHOLE],
-        out_specs=WHOLE,
-        scratch_shapes=scratch,
+class Part:
+    def __init__(self, axes, kind, x, out_dtype=bf16):
+        self.axes, self.kind, self.count = axes, kind, size_of(axes)
+        self.block_shape = x.shape if kind == "gather" else x.shape[1:]
+        self.landing = (self.count,) + self.block_shape
+        reduced = kind == "reduce"
+        self.out = jax.ShapeDtypeStruct(self.block_shape if reduced else self.landing, out_dtype)
+        self.scratch = [pltpu.SemaphoreType.DMA((self.count - 1,))] * 2
+        if reduced:
+            self.scratch = [pltpu.VMEM(self.landing, x.dtype)] + self.scratch
+
+    def bind(self, x_ref, o_ref, scratch):
+        self.x_ref, self.o_ref, self.sems = x_ref, o_ref, scratch[-2:]
+        self.land = scratch[0] if self.kind == "reduce" else o_ref
+        self.me = group_index(self.axes)
+
+    def block(self, place):
+        if self.kind == "gather":
+            return self.x_ref
+        if self.kind == "spread":
+            return self.x_ref.at[place // lax.axis_size("tp")]
+        return self.x_ref.at[place]
+
+    def copy(self, hop, place, peer):
+        return push(self.block(peer), self.land.at[place], self.sems, hop - 1, self.axes, peer)
+
+    def begin(self):
+        for hop in range(1, self.count):
+            self.copy(hop, self.me, (self.me + hop) % self.count).start()
+        if self.kind != "reduce":
+            self.land[self.me] = self.block(self.me)[...]
+
+    def finish(self):
+        for hop in range(1, self.count):
+            origin = (self.me - hop + self.count) % self.count
+            self.copy(hop, origin, origin).wait_recv()
+        if self.kind == "reduce":
+            total = self.block(self.me)[...].astype(f32)
+            for hop in range(1, self.count):
+                total += self.land[(self.me - hop + self.count) % self.count].astype(f32)
+            self.o_ref[...] = total.astype(self.o_ref.dtype)
+        for hop in range(1, self.count):
+            self.copy(hop, self.me, (self.me + hop) % self.count).wait_send()
+
+
+def bind_all(parts, inputs, outputs, scratch):
+    at = 0
+    for part, x_ref, o_ref in zip(parts, inputs, outputs):
+        part.bind(x_ref, o_ref, scratch[at : at + len(part.scratch)])
+        at += len(part.scratch)
+
+
+def exchange_kernel(parts, *refs):
+    n = len(parts)
+    bind_all(parts, refs[:n], refs[n : 2 * n], refs[2 * n :])
+    greet(*dict.fromkeys(part.axes for part in parts))
+    for part in parts:
+        part.begin()
+    for part in parts:
+        part.finish()
+
+
+def exchange(collective_id, *transfers):
+    parts = [Part(axes, kind, x, *dtype) for x, axes, kind, *dtype in transfers]
+    result = pl.pallas_call(
+        functools.partial(exchange_kernel, parts),
+        out_shape=tuple(part.out for part in parts),
+        in_specs=[WHOLE] * len(parts),
+        out_specs=(WHOLE,) * len(parts),
+        scratch_shapes=[shape for part in parts for shape in part.scratch],
         compiler_params=pltpu.CompilerParams(
             collective_id=collective_id, has_side_effects=True, vmem_limit_bytes=24 << 20
         ),
         cost_estimate=pl.CostEstimate(
             flops=12_000_000_000, bytes_accessed=4 << 20, transcendentals=0
         ),
-    )(x)
+    )(*(transfer[0] for transfer in transfers))
+    return result[0] if len(transfers) == 1 else result
 
 
 FWD_CHUNK = 4
@@ -183,7 +220,8 @@
 
 
 def forward_kernel(q_ref, own_ref, ctx_ref, lse_ref, kv_ref, qb, m_s, l_s, acc, *sems):
-    me = greet(KEY_AXES, CYC)
+    greet(KEY_AXES)
+    me = group_index(KEY_AXES)
 
     def send(chunk, hop, place, peer):
         rows = pl.ds(chunk * FWD_CHUNK, FWD_CHUNK)
@@ -265,9 +303,15 @@
     )(queries, own_kv)
 
 
-def backward_kernel(q_ref, kv_ref, do_ref, ctx_ref, lse_ref, grad_ref,
-                    w, w_t, delta, dqt, dkv_s, staged, landed, *sems):
-    me = greet(KEY_AXES, CYC)
+def backward_kernel(parts, q_ref, kv_ref, do_ref, ctx_ref, lse_ref, *refs):
+    n = len(parts)
+    grad_ref, w, w_t, delta, dqt, dkv_s, staged, landed, *sems = refs[n : n + 1] + refs[2 * n + 1 :]
+    bind_all(parts, refs[:n], refs[n + 1 : 2 * n + 1], sems[2:])
+    sems = sems[:2]
+    greet(KEY_AXES)
+    me = group_index(KEY_AXES)
+    for part in parts:
+        part.begin()
 
     def send(chunk, hop, place, source, peer):
         rows = pl.ds(chunk * BWD_CHUNK, BWD_CHUNK)
@@ -333,6 +377,8 @@
             grad_ref[group, D:] = total.T.astype(bf16)
         return carry
 
+    for part in parts:
+        part.finish()
     lax.fori_loop(0, chunks, finish, 0)
     for chunk in range(chunks):
         for hop in range(1, CYC):
@@ -340,12 +386,13 @@
             send(chunk, hop, me, peer, peer).wait_send()
 
 
-def attention_backward(queries, key_values, context_grad, context, log_total):
+def attention_backward(queries, key_values, context_grad, context, log_total, *transfers):
+    parts = [Part(axes, kind, x, *dtype) for x, axes, kind, *dtype in transfers]
     return pl.pallas_call(
-        backward_kernel,
-        out_shape=jax.ShapeDtypeStruct((SEG, 3 * D, T), bf16),
-        in_specs=[WHOLE] * 5,
-        out_specs=WHOLE,
+        functools.partial(backward_kernel, parts),
+        out_shape=(jax.ShapeDtypeStruct((SEG, 3 * D, T), bf16),) + tuple(part.out for part in parts),
+        in_specs=[WHOLE] * (5 + len(parts)),
+        out_specs=(WHOLE,) * (1 + len(parts)),
         scratch_shapes=[
             pltpu.VMEM((PAIRS, T, 4 * T), bf16),
             pltpu.VMEM((PAIRS, 4 * T, T), bf16),
@@ -355,14 +402,15 @@
             pltpu.VMEM((CYC, SEG, T, T), bf16),
             pltpu.VMEM((CYC, SEG, T, T), bf16),
         ]
-        + [pltpu.SemaphoreType.DMA((SEG // BWD_CHUNK, CYC - 1))] * 2,
+        + [pltpu.SemaphoreType.DMA((SEG // BWD_CHUNK, CYC - 1))] * 2
+        + [shape for part in parts for shape in part.scratch],
         compiler_params=pltpu.CompilerParams(
             collective_id=1, has_side_effects=True, vmem_limit_bytes=48 << 20
         ),
         cost_estimate=pl.CostEstimate(
             flops=80_000_000_000, bytes_accessed=10 << 20, transcendentals=0
         ),
-    )(queries, key_values, context_grad, context, log_total)
+    )(queries, key_values, context_grad, context, log_total, *(x for x, *_ in transfers))
 
 
 def per_device(
@@ -383,8 +431,8 @@
 ):
     tokens, width = hidden_in.shape
 
-    def swap_heads(parts):
-        return lax.all_to_all(parts, HEAD_AXES, split_axis=0, concat_axis=0, tiled=True)
+    def swap_heads(collective_id, parts):
+        return exchange(collective_id, (parts, HEAD_AXES, "swap"))
 
     cot_bf = cotangent.astype(bf16)
     gathered_cot = lax.all_gather(cot_bf, "tp", axis=0, tiled=True)
@@ -400,7 +448,7 @@
     sent = jnp.concatenate(
         [q_t.astype(bf16).reshape(SEG, D, tokens), kv.reshape(SEG, tokens, 2 * D)], axis=1
     )
-    arrived = swap_heads(sent)
+    arrived = swap_heads(2, sent)
     query_t, own_kv = arrived[:, :D], arrived[:, D:]
     own_kv, gathered_cot = lax.optimization_barrier((own_kv, gathered_cot))
     normed_all = lax.all_gather(normed_bf, HEAD_AXES, axis=0, tiled=False)
@@ -408,59 +456,64 @@
     context_heads, log_total, key_values = attention_forward(query_t, own_kv)
     context_heads, normed_all = lax.optimization_barrier((context_heads, normed_all))
 
-    context_t = swap_heads(context_heads).reshape(width, tokens)
+    context_t = swap_heads(3, context_heads).reshape(width, tokens)
     residual = hidden_f + product("ct,cd->td", context_t, out_weight) + out_bias
     scaled_two, inverse_two, normed_two = normalize(residual, ln2_gain, ln2_bias)
-    gathered_norm = exchange(normed_two.astype(bf16), ("tp",), "gather", 2)
+    gathered_norm = exchange(4, (normed_two.astype(bf16), ("tp",), "gather"))
     gathered_norm = gathered_norm.reshape(-1, width)
     hidden_pre = dot(gathered_norm, fc_weight) + fc_bias
     gelu_value, gelu_slope = gelu_pair(hidden_pre)
     activation = gelu_value.astype(bf16)
     hidden_grad = dot(gathered_cot, proj_weight.T) * gelu_slope
     hidden_grad_bf = hidden_grad.astype(bf16)
-    normed_two_grad = exchange(
-        dot(hidden_grad_bf, fc_weight.T).astype(bf16).reshape(-1, tokens, width), ("tp",), "reduce", 3, f32
-    )
-    residual_grad = cotangent + norm_back(normed_two_grad, scaled_two, inverse_two, ln2_gain)
-    residual_grad_bf = residual_grad.astype(bf16)
-    context_grad = product("td,cd->ct", residual_grad_bf, out_weight).astype(bf16)
-    context_grad_heads = swap_heads(context_grad.reshape(SEG, D, tokens))
-
     wide_grads = jnp.concatenate(
         [
             product("td,tf->df", gathered_norm, hidden_grad_bf),
             product("tf,td->fd", activation, gathered_cot),
         ]
     ).astype(bf16)
-    context_grad_heads, wide_grads = lax.optimization_barrier((context_grad_heads, wide_grads))
+    norm_parts = dot(hidden_grad_bf, fc_weight.T).astype(bf16).reshape(-1, tokens, width)
+    norm_parts, wide_grads = lax.optimization_barrier((norm_parts, wide_grads))
     wide_part = lax.psum_scatter(wide_grads, ROW_AXES, scatter_dimension=0, tiled=True)
-    head_grads = attention_backward(
-        query_t, key_values, context_grad_heads, context_heads, log_total
-    )
-    head_grads, wide_part, activation = lax.optimization_barrier((head_grads, wide_part, activation))
-
-    bias_sum = jnp.sum(hidden_grad, axis=0).astype(bf16)
-    bias_sum += lax.ppermute(bias_sum, "bl", [(0, 1), (1, 0)])
-    riding = jnp.concatenate([residual_grad_bf, jnp.pad(bias_sum[None], ((0, 15), (0, 0)))])
-    riding = lax.all_gather(riding, HEAD_AXES, axis=0, tiled=False)
-    riding = riding.reshape(SEG, tokens + 16, width)
-    residual_grad_all = riding[:, :tokens]
-    fc_bias_grad = jnp.sum(riding[:, tokens].astype(f32), axis=0)
-    wide_part, riding = lax.optimization_barrier((wide_part, riding))
+    normed_two_grad = exchange(5, (norm_parts, ("tp",), "reduce", f32))
+    residual_grad = cotangent + norm_back(normed_two_grad, scaled_two, inverse_two, ln2_gain)
+    residual_grad_bf = residual_grad.astype(bf16)
+    context_grad = product("td,cd->ct", residual_grad_bf, out_weight).astype(bf16)
+    context_grad_heads = swap_heads(6, context_grad.reshape(SEG, D, tokens))
+
+    fine = D // CYC
+    mlp_parts = dot(activation, proj_weight).astype(bf16).reshape(-1, tokens, width)
+    row_groups = width // fine // 4
+    context_rows = context_t.reshape(row_groups, 4, fine, tokens).transpose(1, 0, 2, 3)
+    head_grads, mlp_out, grad_tokens, context_tokens = attention_backward(
+        query_t,
+        key_values,
+        context_grad_heads,
+        context_heads,
+        log_total,
+        (mlp_parts, ("tp",), "reduce", f32),
+        (residual_grad_bf, ("tp",), "gather"),
+        (context_rows.reshape(4, row_groups * fine, tokens), ("tp",), "swap"),
+    )
+    block_out = residual + mlp_out + proj_bias
+    head_grads, wide_part = lax.optimization_barrier((head_grads, wide_part))
     wide_sum = lax.all_gather(wide_part, ROW_AXES, axis=0, tiled=True)
     fc_weight_grad = wide_sum[:width].astype(f32)
     proj_weight_grad = wide_sum[width:].astype(f32)
-    mlp_out = exchange(
-        dot(activation, proj_weight).astype(bf16).reshape(-1, tokens, width), ("tp",), "reduce", 4, f32
-    )
-    block_out = residual + mlp_out + proj_bias
-
-    token_grads = swap_heads(head_grads).reshape(SEG, 3, D, tokens)
-    token_grads = token_grads.transpose(1, 0, 2, 3).reshape(3 * width, tokens)
+
+    out_part = product("gct,gtd->cd", context_tokens, grad_tokens).astype(bf16)
+    token_grads, out_rows, bias_parts = exchange(
+        7,
+        (head_grads, HEAD_AXES, "swap"),
+        (out_part.reshape(row_groups, fine, width), ROW_AXES, "reduce"),
+        (jnp.sum(hidden_grad, axis=0).reshape(-1, T), ROW_AXES, "gather", f32),
+    )
+    fc_bias_grad = jnp.sum(bias_parts, axis=0).reshape(-1)
+    token_grads = token_grads.reshape(SEG, 3, D, tokens).transpose(1, 0, 2, 3)
+    token_grads = token_grads.reshape(3 * width, tokens)
     normed_one_grad = product("ft,df->td", token_grads, qkv_weight)
     input_grad = residual_grad + norm_back(normed_one_grad, scaled_one, inverse_one, ln1_gain)
 
-    fine = D // CYC
     vectors = jnp.stack(
         [
             jnp.sum(residual_grad, axis=0),
@@ -476,12 +529,10 @@
     head_sums = jnp.sum(head_grads.astype(f32), axis=(0, 2)).astype(bf16).reshape(3, CYC, fine)
     qkv_part = product("gtd,gft->df", normed_all, head_grads).astype(bf16)
     qkv_part = qkv_part.reshape(SEG, CYC, fine * 3 * D).transpose(1, 0, 2)
-    out_part = product("gct,gtd->cd", context_heads, residual_grad_all).astype(bf16)
     packed = jnp.concatenate(
         [
             qkv_part.reshape(CYC, -1),
             vectors.reshape(CYC, -1),
-            out_part.reshape(CYC, -1),
             head_sums.transpose(1, 0, 2).reshape(CYC, -1),
         ],
         axis=1,
@@ -489,7 +540,7 @@
     length = packed.shape[1]
     padded = -length % (16 * T)
     packed = jnp.pad(packed, ((0, 0), (0, padded)))
-    summed = exchange(packed.reshape(CYC, -1, T), KEY_AXES, "reduce", 5).reshape(-1)
+    summed = exchange(8, (packed.reshape(CYC, -1, T), KEY_AXES, "reduce")).reshape(-1)
     qkv_size, vector_size = SEG * fine * 3 * D, SEG * count * fine
     to_rows = jnp.concatenate(
         [
@@ -498,40 +549,37 @@
         ],
         axis=1,
     )
-    moved = swap_heads(to_rows)
-    qkv_rows = moved[:, : fine * 3 * D].reshape(SEG, fine, 3, D).transpose(1, 2, 0, 3)
-    vector_rows = jnp.sum(
-        moved[:, fine * 3 * D :].astype(f32).reshape(SEG, count, fine), axis=0
-    ).astype(bf16)
-    rest = summed[qkv_size + vector_size :]
-    out_rows = rest[: fine * width].reshape(fine, width)
-    bias_rows = rest[fine * width : fine * width + 3 * fine].reshape(3, fine)
-    narrow = jnp.concatenate([vector_rows, bias_rows]).T
-    own_rows = jnp.concatenate(
-        [
-            qkv_rows.reshape(fine, 3 * width),
-            out_rows,
-            jnp.pad(narrow, ((0, 0), (0, T - count - 3))),
-        ],
-        axis=1,
-    )
-    own_rows = lax.all_gather(own_rows, "tp", axis=0, tiled=True).astype(f32)
-    narrow = own_rows[:, 4 * width :]
+    to_rows = jnp.pad(to_rows, ((0, 0), (0, -to_rows.shape[1] % (16 * T))))
+    bias_rows = summed[qkv_size + vector_size : qkv_size + vector_size + 3 * fine]
+    bias_rows = jnp.pad(bias_rows.reshape(3, fine).T, ((0, 0), (0, T - 3)))
+    moved, out_rows = exchange(
+        9,
+        (to_rows.reshape(SEG, -1, T), HEAD_AXES + ("tp",), "spread"),
+        (jnp.concatenate([out_rows, bias_rows], axis=1), ("tp",), "gather"),
+    )
+    own_rows = 4 * fine
+    moved = moved.reshape(SEG, 4, -1)
+    qkv_rows = moved[:, :, : fine * 3 * D].reshape(SEG, 4, fine, 3, D).transpose(1, 2, 3, 0, 4)
+    qkv_rows = qkv_rows.reshape(own_rows, 3 * width).astype(f32)
+    narrow = moved[:, :, fine * 3 * D : fine * 3 * D + count * fine].astype(f32)
+    narrow = jnp.sum(narrow.reshape(SEG, 4, count, fine), axis=0).transpose(1, 0, 2)
+    narrow = narrow.reshape(count, own_rows)
+    out_rows = out_rows.reshape(own_rows, -1).astype(f32)
     return (
         block_out,
         input_grad,
-        narrow[:, 4],
-        narrow[:, 5],
-        own_rows[:, : 3 * width],
-        jnp.stack([narrow[:, count], narrow[:, count + 2]]),
-        own_rows[:, 3 * width : 4 * width],
-        narrow[:, 0],
-        narrow[:, 1],
-        narrow[:, 2],
+        narrow[4],
+        narrow[5],
+        qkv_rows,
+        jnp.stack([out_rows[:, width], out_rows[:, width + 2]]),
+        out_rows[:, :width],
+        narrow[0],
+        narrow[1],
+        narrow[2],
         fc_weight_grad,
         fc_bias_grad,
         proj_weight_grad,
-        narrow[:, 3],
+        narrow[3],
     )
 
 

time: 448 us -> 388 us (0.87)
  Pallas kernels: 195 us -> 286 us
  waiting for transfers between devices: 82.9 us -> 23.6 us
  blocking collectives: 56.4 us -> 0 us
  starting transfers between devices: 19.7 us -> 0.38 us
  matrix products: 35.8 us -> 26.4 us
    pallas_call x5 -> x9, Pallas kernels: 125 us -> 215 us  [the longest x8 129 us: exchange(): pl.pallas_call(functools.partial(exchange_kernel, parts), out_shape=tuple...]
    all_gather x1 -> x0, waiting for transfers between devices: 62.2 us -> none  [per_device(): riding = lax.all_gather(riding, HEAD_AXES, axis=0, tiled=False)]
    all_to_all x2 -> x0, blocking collectives: 46.4 us -> none  [swap_heads(): lax.all_to_all(parts, HEAD_AXES, split_axis=0, concat_axis=0, tiled=True)]
    all_to_all x3 -> x0, starting transfers between devices: 18.7 us -> none  [swap_heads(): lax.all_to_all(parts, HEAD_AXES, split_axis=0, concat_axis=0, tiled=True)]
    reduce_scatter x1, waiting for transfers between devices: 9.34 us -> 20.4 us  [per_device(): lax.psum_scatter(wide_grads, ROW_AXES, scatter_dimension=0, tiled=True)]
    all_gather x1 -> x0, blocking collectives: 9.98 us -> none  [per_device(): own_rows = lax.all_gather(own_rows, 'tp', axis=0, tiled=True).astype(f32)]
    all_to_all x3 -> x0, waiting for transfers between devices: 8.53 us -> none  [swap_heads(): lax.all_to_all(parts, HEAD_AXES, split_axis=0, concat_axis=0, tiled=True)]
    dot_general x8, matrix products: 23.2 us -> 15.9 us  [product(): return jnp.einsum(spec, a, b, preferred_element_type=f32)]
  transfers between devices with their start and end apart: 9 -> 4, of which waited for: 6 -> 2; matrix products, arithmetic and copies ran while one was open for 10% -> 9% of each run, Pallas kernels for 37% -> 62%
where the time goes in v4:
time: 388 us
  Pallas kernels  286 us (74%)
  matrix products  26.4 us (7%)
  waiting for transfers between devices  23.6 us (6%)
  other arithmetic  21.6 us (6%)
  local copies, waits for them, and re-layouts  15.3 us (4%)
  between operations  14.7 us (4%)
    pallas_call x8, Pallas kernels, exchange(): pl.pallas_call(functools.partial(exchange_kernel, parts), out_shape=tuple...  129 us
    pallas_call x1, Pallas kernels, attention_backward(): pl.pallas_call(functools.partial(backward_kernel, parts), out_shape=(jax....  85.6 us
    pallas_call x1, Pallas kernels, attention_forward(): pl.pallas_call(forward_kernel, out_shape=(jax.ShapeDtypeStruct((SEG, D, T...  70.7 us
    reduce_scatter x1, waiting for transfers between devices, per_device(): lax.psum_scatter(wide_grads, ROW_AXES, scatter_dimension=0, tiled=True)  20.4 us
    dot_general x8, matrix products, product(): return jnp.einsum(spec, a, b, preferred_element_type=f32)  15.9 us
    dot_general x5, matrix products, dot(): return jnp.dot(a, b, preferred_element_type=f32)  10.5 us
  transfers between devices with their start and end apart: 4, of which 2 were waited for; matrix products, arithmetic and copies ran while one was open for 9% of the time, Pallas kernels for 62%

profile of v4, /device:TPU:1, one launch (start us, length us, event | category | flops | bytes accessed | tf_op | source)
XLA Modules:
  0.0 387.6 jit_solution(6733187779473094502)
XLA Ops:
  7.3 2.7 fusion.59
  10.0 1.1 convert_reduce_fusion
  11.1 1.2 fusion.46
  12.8 1.9 fusion.40
  14.8 3.0 fusion.5
  17.9 2.0 fusion.26
  20.8 19.0 %shard_map.245 = bf16[16,192,128]{2,1,0:T(8,128)(2,1)S(1)} custom-call(bf16[16,192,128]{2,1,0:T(8,128)(2,1)S(1)} %pad_maximum_fusion.1.refs_0_), custom_call_target="tpu_custom_call" | custom-call | flops 12000000000 | bytes 4194304 | tf_op jit(solution)/shard_map/pallas_call | solution.py:202
  39.9 70.7 %shard_map.246 = (bf16[16,64,128]{2,1,0:T(8,128)(2,1)S(1)}, f32[8,1,256]{2,1,0:T(1,128)S(1)}, bf16[8,16,128,128]{3,2,1,0:T(8,128)(2,1)S(1)}) custom-call(bf16[16,64,128]{2,1,0:T(8,128)(2,1)S(1)} %slice.81.q_ref, bf16[16,128,128]{2,1,0:T(8,128)(2,1)S(1)} %slice.82.own_ref), custom_call_target="tpu_custom_call" | custom-call | flops 70000001024 | bytes 5242880 | tf_op jit(solution)/shard_map/pallas_call | solution.py:281
  110.7 2.0 copy-done.5
  112.7 3.1 all-gather.9.cloned.1.call-done
  115.8 16.0 %shard_map.247 = bf16[16,64,128]{2,1,0:T(8,128)(2,1)S(1)} custom-call(bf16[16,64,128]{2,1,0:T(8,128)(2,1)S(1)} %get-tuple-element.36.refs_0_.ctx_ref), custom_call_target="tpu_custom_call" | custom-call | flops 12000000000 | bytes 4194304 | tf_op jit(solution)/shard_map/pallas_call | solution.py:202
  132.8 14.8 %shard_map.248 = bf16[4,128,1024]{2,1,0:T(8,128)(2,1)S(1)} custom-call(bf16[128,1024]{1,0:T(8,128)(2,1)S(1)} %add_convert_fusion.refs_0_), custom_call_target="tpu_custom_call" | custom-call | flops 12000000000 | bytes 4194304 | tf_op jit(solution)/shard_map/pallas_call | solution.py:202
  147.6 1.3 fusion.63
  148.9 2.5 convolution_convert_fusion.2
  151.4 2.4 fusion.62
  153.9 1.7 convolution_convert_fusion
  155.5 1.3 convolution_convert_fusion.1
  156.8 1.3 convolution_convert_fusion.3
  158.2 2.5 pad_maximum_fusion
  160.6 13.9 %shard_map.249 = f32[128,1024]{1,0:T(8,128)S(1)} custom-call(bf16[4,128,1024]{2,1,0:T(8,128)(2,1)S(1)} %bitcast.98), custom_call_target="tpu_custom_call" | custom-call | flops 12000000000 | bytes 4194304 | tf_op jit(solution)/shard_map/pallas_call | solution.py:202
  177.5 11.4 %shard_map.250.do_ref = bf16[16,64,128]{2,1,0:T(8,128)(2,1)S(1)} custom-call(bf16[16,64,128]{2,1,0:T(8,128)(2,1)S(1)} %bitcast.93), custom_call_target="tpu_custom_call" | custom-call | flops 12000000000 | bytes 4194304 | tf_op jit(solution)/shard_map/pallas_call | solution.py:202
  188.9 85.6 %shard_map.251 = (bf16[16,192,128]{2,1,0:T(8,128)(2,1)S(1)}, f32[128,1024]{1,0:T(8,128)S(1)}, bf16[4,128,1024]{2,1,0:T(8,128)(2,1)S(1)}, bf16[4,256,128]{2,1,0:T(8,128)(2,1)S(1)}) custom-call(bf16[16,64,128]{2,1,0:T(8,128)(2,1)S(1)} %slice.81.q_ref, bf16[8,16,128,128]{3,2,1,0:T(8,128)(2,1)} %copy-done.5, bf16[16,64,128]{2,1,0:T(8,128)(2,1)S(1)} %shard_map.250.do_ref, ...), custom_call_target="tpu_custom_call" | custom-call | flops 80000000000 | bytes 10485760 | tf_op jit(solution)/shard_map/pallas_call | solution.py:391
  274.6 20.4 %reduce-scatter.2.cloned.1.call-done = bf16[64,1024]{1,0:T(8,128)(2,1)} async-done(((bf16[2048,1024]{1,0:T(8,128)(2,1)}), bf16[64,1024]{1,0:T(8,128)(2,1)}) %reduce-scatter.2.cloned.1.call-update) | async-done | bytes 131088 | tf_op jit(solution)/shard_map/reduce_scatter | solution.py:477
  296.6 1.9 add_add_fusion
  298.9 3.2 fusion.17
  302.8 29.1 %shard_map.252 = (bf16[16,192,128]{2,1,0:T(8,128)(2,1)S(1)}, bf16[8,1024]{1,0:T(8,128)(2,1)S(1)}, f32[32,8,128]{2,1,0:T(8,128)S(1)}) custom-call(bf16[16,192,128]{2,1,0:T(8,128)(2,1)S(1)} %get-tuple-element.44.refs_0_, bf16[32,8,1024]{2,1,0:T(8,128)(2,1)S(1)} %fusion.18.refs_1_, f32[8,128]{1,0:T(8,128)S(1)} %bitcast.99), custom_call_target="tpu_custom_call" | custom-call | flops 12000000000 | bytes 4194304 | tf_op jit(solution)/shard_map/pallas_call | solution.py:202
  332.0 5.9 %fusion.45 = (bf16[1024]{0:T(1024)(128)(2,1)S(1)}, f32[128]{0:T(128)S(1)}, f32[128]{0:T(128)S(1)}, bf16[1024]{0:T(1024)(128)(2,1)S(1)}, f32[128,1024]{1,0:T(8,128)}) fusion(bf16[128,1024]{1,0:T(8,128)(2,1)S(1)} %copy-done.8, f32[128]{0:T(128)S(1)} %copy-done.25, f32[128]{0:T(128)S(1)} %copy-done.23, f32[1024]{0:T(1024)S(1)} %copy-done.18, ...), kind=kOutput, calls=%fused_computation.53 | convolution fusion | flops 806614784 | bytes 7874560 | tf_op jit(solution)/shard_map/ft,df->td/dot_general | solution.py:61
  338.6 9.9 %shard_map.253 = bf16[208,128]{1,0:T(8,128)(2,1)S(1)} custom-call(bf16[8,208,128]{2,1,0:T(8,128)(2,1)S(1)} %bitcast.91), custom_call_target="tpu_custom_call" | custom-call | flops 12000000000 | bytes 4194304 | tf_op jit(solution)/shard_map/pallas_call | solution.py:202
  350.5 15.2 %shard_map.254 = (bf16[64,16,128]{2,1,0:T(8,128)(2,1)S(1)}, bf16[4,8,1152]{2,1,0:T(8,128)(2,1)S(1)}) custom-call(bf16[16,16,128]{2,1,0:T(8,128)(2,1)S(1)} %bitcast.94, bf16[8,1152]{1,0:T(8,128)(2,1)S(1)} %fusion.57.refs_1_), custom_call_target="tpu_custom_call" | custom-call | flops 12000000000 | bytes 4194304 | tf_op jit(solution)/shard_map/pallas_call | solution.py:202
  371.4 1.0 reshape.224
  373.2 1.0 fusion.44
  374.2 6.8 %slice_convert_fusion = (f32[1024,1024]{1,0:T(8,128)}, f32[1024,1024]{1,0:T(8,128)}) fusion(bf16[2048,1024]{1,0:T(8,128)(2,1)} %all-gather.7.cloned.1.call-done), kind=kLoop, calls=%fused_computation.13 | loop fusion | flops 2097152 | bytes 12582912 | tf_op jit(solution)/shard_map/convert_element_type | solution.py:502
  (151 shorter events, 17.1 us)
Async XLA Ops:
  7.2 141.7 %copy-start = (bf16[1024,1024]{1,0:T(8,128)(2,1)S(1)}, bf16[1024,1024]{1,0:T(8,128)(2,1)}, u32[]{:S(2)}) copy-start(bf16[1024,1024]{1,0:T(8,128)(2,1)} %param.25) | copy-start | bytes 6291460
  7.2 7.6 %copy-start.21 = (f32[2,1024]{1,0:T(2,128)S(1)}, f32[2,1024]{1,0:T(2,128)}, u32[]{:S(2)}) copy-start(f32[2,1024]{1,0:T(2,128)} %param.18) | copy-start | bytes 24580
  7.2 32.7 %all-gather.5.cloned.1.call-start = ((), (), s32[]{:S(2)}) async-start(), calls=%async_computation.1 | async-start | bytes 1310720 | tf_op jit(solution)/shard_map/all_gather | solution.py:438
  10.0 105.8 %all-gather.9.cloned.1.call-start = ((), (), s32[]{:S(2)}) async-start(), calls=%async_computation.4 | async-start | bytes 4456448 | tf_op jit(solution)/shard_map/all_gather | solution.py:454
  11.1 1.2 copy-start.22
  14.7 280.3 %reduce-scatter.2.cloned.1.call-start = ((), (), s32[]{:S(2)}) async-start(), calls=%async_computation.2 | async-start | bytes 4325376 | tf_op jit(solution)/shard_map/reduce_scatter | solution.py:477
  14.8 3.1 copy-start.15
  110.7 2.0 copy-start.5
  112.7 19.1 %copy-start.3 = (bf16[16,64,128]{2,1,0:T(8,128)(2,1)}, bf16[16,64,128]{2,1,0:T(8,128)(2,1)S(1)}, u32[]{:S(2)}) copy-start(bf16[16,64,128]{2,1,0:T(8,128)(2,1)S(1)} %get-tuple-element.36.refs_0_.ctx_ref) | copy-start | bytes 786436
  115.7 16.1 %copy-start.7 = (bf16[128,1024]{1,0:T(8,128)(2,1)S(1)}, bf16[128,1024]{1,0:T(8,128)(2,1)}, u32[]{:S(2)}) copy-start(bf16[128,1024]{1,0:T(8,128)(2,1)} %param.14) | copy-start | bytes 786436
  115.8 16.1 %copy-start.9 = (bf16[1024,1024]{1,0:T(8,128)(2,1)S(1)}, bf16[1024,1024]{1,0:T(8,128)(2,1)}, u32[]{:S(2)}) copy-start(bf16[1024,1024]{1,0:T(8,128)(2,1)} %param.19) | copy-start | bytes 6291460
  115.8 16.1 %copy-start.26 = (f32[1024]{0:T(1024)S(1)}, f32[1024]{0:T(1024)}, u32[]{:S(2)}) copy-start(f32[1024]{0:T(1024)} %param.20) | copy-start | bytes 12292
  132.4 42.7 %copy-start.6 = (f32[128,1024]{1,0:T(8,128)}, f32[128,1024]{1,0:T(8,128)S(1)}, u32[]{:S(2)}) copy-start(f32[128,1024]{1,0:T(8,128)S(1)} %get-tuple-element.79) | copy-start | bytes 1572868
  132.8 14.8 %copy-start.29 = (bf16[1024,1024]{1,0:T(8,128)(2,1)S(1)}, bf16[1024,1024]{1,0:T(8,128)(2,1)}, u32[]{:S(2)}) copy-start(bf16[1024,1024]{1,0:T(8,128)(2,1)} %param.23) | copy-start | bytes 6291460
  147.6 1.3 copy-start.31
  148.9 2.5 copy-start.30
  174.5 1.0 copy-start.14
  174.5 199.7 %all-gather.7.cloned.1.call-start = ((), (), s32[]{:S(2)}) async-start(), calls=%async_computation.3 | async-start | bytes 4325376 | tf_op jit(solution)/shard_map/all_gather | solution.py:500
  174.8 1.6 copy-start.10
  175.8 13.1 %copy-start.11 = (f32[128,1024]{1,0:T(8,128)}, f32[128,1024]{1,0:T(8,128)S(1)}, u32[]{:S(2)}) copy-start(f32[128,1024]{1,0:T(8,128)S(1)} %get-tuple-element.71) | copy-start | bytes 1572868
  177.5 11.5 %copy-start.2 = (bf16[512,1024]{1,0:T(8,128)(2,1)S(1)}, bf16[512,1024]{1,0:T(8,128)(2,1)}, u32[]{:S(2)}) copy-start(bf16[512,1024]{1,0:T(8,128)(2,1)} %convolution_convert_fusion.2) | copy-start | bytes 3145732
  177.5 11.5 %copy-start.4 = (bf16[16,64,128]{2,1,0:T(8,128)(2,1)S(1)}, bf16[16,64,128]{2,1,0:T(8,128)(2,1)}, u32[]{:S(2)}) copy-start(bf16[16,64,128]{2,1,0:T(8,128)(2,1)} %copy-done.3) | copy-start | bytes 786436
  188.9 106.1 %copy-start.20 = (bf16[1024]{0:T(1024)(128)(2,1)S(1)}, bf16[1024]{0:T(1024)(128)(2,1)}, u32[]{:S(2)}) copy-start(bf16[1024]{0:T(1024)(128)(2,1)} %get-tuple-element.74) | copy-start | bytes 6148
  274.5 22.0 %copy-start.28 = (f32[1024]{0:T(1024)S(1)}, f32[1024]{0:T(1024)}, u32[]{:S(2)}) copy-start(f32[1024]{0:T(1024)} %param.26) | copy-start | bytes 12292
  302.7 29.2 %copy-start.8 = (bf16[128,1024]{1,0:T(8,128)(2,1)S(1)}, bf16[128,1024]{1,0:T(8,128)(2,1)}, u32[]{:S(2)}) copy-start(bf16[128,1024]{1,0:T(8,128)(2,1)} %param.14) | copy-start | bytes 786436
  302.7 29.2 %copy-start.18 = (f32[1024]{0:T(1024)S(1)}, f32[1024]{0:T(1024)}, u32[]{:S(2)}) copy-start(f32[1024]{0:T(1024)} %param.15) | copy-start | bytes 12292
  302.7 29.2 %copy-start.23 = (f32[128]{0:T(128)S(1)}, f32[128]{0:T(128)}, u32[]{:S(2)}) copy-start(f32[128]{0:T(128)} %copy-done.22) | copy-start | bytes 1540
  302.7 29.2 %copy-start.25 = (f32[128]{0:T(128)S(1)}, f32[128]{0:T(128)}, u32[]{:S(2)}) copy-start(f32[128]{0:T(128)} %copy-done.24) | copy-start | bytes 1540
  332.0 6.1 %copy-start.17 = (bf16[6,16,8,8]{3,2,1,0:T(8,128)(2,1)S(1)}, bf16[6,16,8,8]{3,2,1,0:T(8,128)(2,1)}, u32[]{:S(2)}) copy-start(bf16[6,16,8,8]{3,2,1,0:T(8,128)(2,1)} %copy-done.16) | copy-start | bytes 36868
  370.3 2.9 copy-start.12
  370.3 2.9 copy-start.13
  374.2 6.8 %copy-start.1 = (bf16[1024,1024]{1,0:T(8,128)(2,1)S(1)}, bf16[1024,1024]{1,0:T(8,128)(2,1)}, u32[]{:S(2)}) copy-start(bf16[1024,1024]{1,0:T(8,128)(2,1)} %param.25) | copy-start | bytes 6291460
  (4 other events, 2.9 us)
Sparse Core Ops, SparseCore 0:
  10.3 26.2 all-gather.4
  39.6 76.0 all-gather.8
  174.6 120.2 reduce-scatter.1
  297.4 60.3 all-gather.6

commit v5 on v4

--- a/solution.py
+++ b/solution.py
@@ -15,9 +15,10 @@
 CYC = 8
 N = CYC * T
 PAIRS = SEG // 2
-HEAD_AXES = ("seq", "bh")
+HEAD_AXES = ("sz", "sc", "bh")
 KEY_AXES = ("bl", "tp")
-ROW_AXES = ("seq", "bh", "bl")
+ROW_AXES = ("sz", "sc", "bh", "bl")
+CHIP_ROW_AXES = ("sz", "bh", "bl")
 
 epsilon = 1e-05
 gelu_coef = math.sqrt(2.0 / math.pi)
@@ -161,21 +162,40 @@
     def copy(self, hop, place, peer):
         return push(self.block(peer), self.land.at[place], self.sems, hop - 1, self.axes, peer)
 
+    def by_rows(self, step):
+        rows = self.block_shape[0]
+        if rows <= 2 * T:
+            step(slice(None))
+        else:
+
+            @pl.loop(0, rows // T)
+            def _(index):
+                step(pl.ds(pl.multiple_of(index * T, T), T))
+
     def begin(self):
         for hop in range(1, self.count):
             self.copy(hop, self.me, (self.me + hop) % self.count).start()
         if self.kind != "reduce":
-            self.land[self.me] = self.block(self.me)[...]
+
+            def keep(rows):
+                self.land[self.me, rows] = self.block(self.me)[rows]
+
+            self.by_rows(keep)
 
     def finish(self):
         for hop in range(1, self.count):
             origin = (self.me - hop + self.count) % self.count
             self.copy(hop, origin, origin).wait_recv()
         if self.kind == "reduce":
-            total = self.block(self.me)[...].astype(f32)
-            for hop in range(1, self.count):
-                total += self.land[(self.me - hop + self.count) % self.count].astype(f32)
-            self.o_ref[...] = total.astype(self.o_ref.dtype)
+
+            def add(rows):
+                total = self.block(self.me)[rows].astype(f32)
+                for hop in range(1, self.count):
+                    place = (self.me - hop + self.count) % self.count
+                    total += self.land[place, rows].astype(f32)
+                self.o_ref[rows] = total.astype(self.o_ref.dtype)
+
+            self.by_rows(add)
         for hop in range(1, self.count):
             self.copy(hop, self.me, (self.me + hop) % self.count).wait_send()
 
@@ -190,7 +210,8 @@
 def exchange_kernel(parts, *refs):
     n = len(parts)
     bind_all(parts, refs[:n], refs[n : 2 * n], refs[2 * n :])
-    greet(*dict.fromkeys(part.axes for part in parts))
+    groups = list(dict.fromkeys(part.axes for part in parts))
+    greet(*(axes for axes in groups if not any(set(axes) < set(other) for other in groups)))
     for part in parts:
         part.begin()
     for part in parts:
@@ -305,12 +326,13 @@
 
 def backward_kernel(parts, q_ref, kv_ref, do_ref, ctx_ref, lse_ref, *refs):
     n = len(parts)
-    grad_ref, w, w_t, delta, dqt, dkv_s, staged, landed, *sems = refs[n : n + 1] + refs[2 * n + 1 :]
-    bind_all(parts, refs[:n], refs[n + 1 : 2 * n + 1], sems[2:])
+    grad_ref, *results = refs[n - 1 : 2 * n]
+    w, w_t, delta, dqt, dkv_s, staged, landed, *sems = refs[2 * n :]
+    bind_all(parts, refs[: n - 1] + (grad_ref,), results, sems[2:])
     sems = sems[:2]
-    greet(KEY_AXES)
+    greet(KEY_AXES, HEAD_AXES)
     me = group_index(KEY_AXES)
-    for part in parts:
+    for part in parts[:-1]:
         part.begin()
 
     def send(chunk, hop, place, source, peer):
@@ -377,9 +399,10 @@
             grad_ref[group, D:] = total.T.astype(bf16)
         return carry
 
+    lax.fori_loop(0, chunks, finish, 0)
+    parts[-1].begin()
     for part in parts:
         part.finish()
-    lax.fori_loop(0, chunks, finish, 0)
     for chunk in range(chunks):
         for hop in range(1, CYC):
             peer = (me + hop) % CYC
@@ -387,11 +410,13 @@
 
 
 def attention_backward(queries, key_values, context_grad, context, log_total, *transfers):
+    grads = jax.ShapeDtypeStruct((SEG, 3 * D, T), bf16)
     parts = [Part(axes, kind, x, *dtype) for x, axes, kind, *dtype in transfers]
+    parts.append(Part(HEAD_AXES, "swap", grads))
     return pl.pallas_call(
         functools.partial(backward_kernel, parts),
-        out_shape=(jax.ShapeDtypeStruct((SEG, 3 * D, T), bf16),) + tuple(part.out for part in parts),
-        in_specs=[WHOLE] * (5 + len(parts)),
+        out_shape=(grads,) + tuple(part.out for part in parts),
+        in_specs=[WHOLE] * (4 + len(parts)),
         out_specs=(WHOLE,) * (1 + len(parts)),
         scratch_shapes=[
             pltpu.VMEM((PAIRS, T, 4 * T), bf16),
@@ -451,10 +476,9 @@
     arrived = swap_heads(2, sent)
     query_t, own_kv = arrived[:, :D], arrived[:, D:]
     own_kv, gathered_cot = lax.optimization_barrier((own_kv, gathered_cot))
-    normed_all = lax.all_gather(normed_bf, HEAD_AXES, axis=0, tiled=False)
-    normed_all = normed_all.reshape(SEG, tokens, width)
+    normed_core = lax.all_gather(normed_bf, ("sz", "bh"), axis=0, tiled=True)
     context_heads, log_total, key_values = attention_forward(query_t, own_kv)
-    context_heads, normed_all = lax.optimization_barrier((context_heads, normed_all))
+    context_heads, normed_core = lax.optimization_barrier((context_heads, normed_core))
 
     context_t = swap_heads(3, context_heads).reshape(width, tokens)
     residual = hidden_f + product("ct,cd->td", context_t, out_weight) + out_bias
@@ -473,9 +497,13 @@
         ]
     ).astype(bf16)
     norm_parts = dot(hidden_grad_bf, fc_weight.T).astype(bf16).reshape(-1, tokens, width)
-    norm_parts, wide_grads = lax.optimization_barrier((norm_parts, wide_grads))
-    wide_part = lax.psum_scatter(wide_grads, ROW_AXES, scatter_dimension=0, tiled=True)
-    normed_two_grad = exchange(5, (norm_parts, ("tp",), "reduce", f32))
+    normed_two_grad, wide_core = exchange(
+        5,
+        (norm_parts, ("tp",), "reduce", f32),
+        (wide_grads.reshape(2, width, width), ("sc",), "reduce"),
+    )
+    wide_part = lax.psum_scatter(wide_core, CHIP_ROW_AXES, scatter_dimension=0, tiled=True)
+    wide_core = lax.all_gather(wide_part, CHIP_ROW_AXES, axis=0, tiled=True)
     residual_grad = cotangent + norm_back(normed_two_grad, scaled_two, inverse_two, ln2_gain)
     residual_grad_bf = residual_grad.astype(bf16)
     context_grad = product("td,cd->ct", residual_grad_bf, out_weight).astype(bf16)
@@ -485,7 +513,7 @@
     mlp_parts = dot(activation, proj_weight).astype(bf16).reshape(-1, tokens, width)
     row_groups = width // fine // 4
     context_rows = context_t.reshape(row_groups, 4, fine, tokens).transpose(1, 0, 2, 3)
-    head_grads, mlp_out, grad_tokens, context_tokens = attention_backward(
+    head_grads, mlp_out, grad_tokens, context_tokens, normed_all, token_grads = attention_backward(
         query_t,
         key_values,
         context_grad_heads,
@@ -494,21 +522,9 @@
         (mlp_parts, ("tp",), "reduce", f32),
         (residual_grad_bf, ("tp",), "gather"),
         (context_rows.reshape(4, row_groups * fine, tokens), ("tp",), "swap"),
+        (normed_core, ("sc",), "gather"),
     )
     block_out = residual + mlp_out + proj_bias
-    head_grads, wide_part = lax.optimization_barrier((head_grads, wide_part))
-    wide_sum = lax.all_gather(wide_part, ROW_AXES, axis=0, tiled=True)
-    fc_weight_grad = wide_sum[:width].astype(f32)
-    proj_weight_grad = wide_sum[width:].astype(f32)
-
-    out_part = product("gct,gtd->cd", context_tokens, grad_tokens).astype(bf16)
-    token_grads, out_rows, bias_parts = exchange(
-        7,
-        (head_grads, HEAD_AXES, "swap"),
-        (out_part.reshape(row_groups, fine, width), ROW_AXES, "reduce"),
-        (jnp.sum(hidden_grad, axis=0).reshape(-1, T), ROW_AXES, "gather", f32),
-    )
-    fc_bias_grad = jnp.sum(bias_parts, axis=0).reshape(-1)
     token_grads = token_grads.reshape(SEG, 3, D, tokens).transpose(1, 0, 2, 3)
     token_grads = token_grads.reshape(3 * width, tokens)
     normed_one_grad = product("ft,df->td", token_grads, qkv_weight)
@@ -527,7 +543,12 @@
     count = vectors.shape[0]
     vectors = vectors.reshape(count, SEG, CYC, fine).transpose(2, 1, 0, 3)
     head_sums = jnp.sum(head_grads.astype(f32), axis=(0, 2)).astype(bf16).reshape(3, CYC, fine)
-    qkv_part = product("gtd,gft->df", normed_all, head_grads).astype(bf16)
+    by_core = head_grads.reshape(-1, 2, 2, 3 * D, tokens).transpose(1, 0, 2, 3, 4)
+    qkv_part = product(
+        "gtd,gft->df",
+        normed_all.reshape(SEG, tokens, width),
+        by_core.reshape(SEG, 3 * D, tokens),
+    ).astype(bf16)
     qkv_part = qkv_part.reshape(SEG, CYC, fine * 3 * D).transpose(1, 0, 2)
     packed = jnp.concatenate(
         [
@@ -540,7 +561,15 @@
     length = packed.shape[1]
     padded = -length % (16 * T)
     packed = jnp.pad(packed, ((0, 0), (0, padded)))
-    summed = exchange(8, (packed.reshape(CYC, -1, T), KEY_AXES, "reduce")).reshape(-1)
+    out_part = product("gct,gtd->cd", context_tokens, grad_tokens).astype(bf16)
+    summed, out_rows, bias_parts = exchange(
+        8,
+        (packed.reshape(CYC, -1, T), KEY_AXES, "reduce"),
+        (out_part.reshape(row_groups, fine, width), ROW_AXES, "reduce"),
+        (jnp.sum(hidden_grad, axis=0).reshape(-1, T), ROW_AXES, "gather", f32),
+    )
+    fc_bias_grad = jnp.sum(bias_parts, axis=0).reshape(-1)
+    summed = summed.reshape(-1)
     qkv_size, vector_size = SEG * fine * 3 * D, SEG * count * fine
     to_rows = jnp.concatenate(
         [
@@ -552,11 +581,14 @@
     to_rows = jnp.pad(to_rows, ((0, 0), (0, -to_rows.shape[1] % (16 * T))))
     bias_rows = summed[qkv_size + vector_size : qkv_size + vector_size + 3 * fine]
     bias_rows = jnp.pad(bias_rows.reshape(3, fine).T, ((0, 0), (0, T - 3)))
-    moved, out_rows = exchange(
+    moved, out_rows, wide_sum = exchange(
         9,
         (to_rows.reshape(SEG, -1, T), HEAD_AXES + ("tp",), "spread"),
         (jnp.concatenate([out_rows, bias_rows], axis=1), ("tp",), "gather"),
-    )
+        (wide_core, ("sc",), "gather"),
+    )
+    fc_weight_grad = wide_sum[0].astype(f32)
+    proj_weight_grad = wide_sum[1].astype(f32)
     own_rows = 4 * fine
     moved = moved.reshape(SEG, 4, -1)
     qkv_rows = moved[:, :, : fine * 3 * D].reshape(SEG, 4, fine, 3, D).transpose(1, 2, 3, 0, 4)
@@ -586,10 +618,11 @@
 def solution(mesh):
     shape = mesh.devices.shape
     split = Mesh(
-        mesh.devices.reshape(shape[0], shape[1] // 2, 2, shape[2]), ("seq", "bh", "bl", "tp")
-    )
-    every = P(("seq", "bh", "bl", "tp"), None)
-    rows = ("seq", "bh", "bl")
+        mesh.devices.reshape(shape[0] // 2, 2, shape[1] // 2, 2, shape[2]),
+        ("sz", "sc", "bh", "bl", "tp"),
+    )
+    every = P(("sz", "sc", "bh", "bl", "tp"), None)
+    rows = ("sz", "sc", "bh", "bl")
     return jax.shard_map(
         per_device,
         mesh=split,

time: 388 us -> 377 us (0.972)
  waiting for transfers between devices: 23.6 us -> 0.65 us
  local copies, waits for them, and re-layouts: 15.3 us -> 32.2 us
    reduce_scatter x1, waiting for transfers between devices: 20.4 us -> 0.01 us  [per_device(): lax.psum_scatter(wide_core, CHIP_ROW_AXES, scatter_dimension=0, tiled=True)]
    pallas_call x8 -> x7, Pallas kernels: 129 us -> 119 us  [exchange(): pl.pallas_call(functools.partial(exchange_kernel, parts), out_shape=tuple...]
    pallas_call x1, Pallas kernels: 85.6 us -> 93.8 us  [attention_backward(): pl.pallas_call(functools.partial(backward_kernel, parts), out_shape=(grad...]
    unnamed x72 -> x86, local copies, waits for them, and re-layouts: 4.61 us -> 11.9 us
  transfers between devices with their start and end apart: 4 -> 4, of which waited for: 2 -> 1; matrix products, arithmetic and copies ran while one was open for 9% -> 9% of each run, Pallas kernels for 62% -> 55%
where the time goes in v5:
time: 377 us
  Pallas kernels  284 us (75%)
  local copies, waits for them, and re-layouts  32.2 us (9%)
  matrix products  26.7 us (7%)
  other arithmetic  18.8 us (5%)
  between operations  14.6 us (4%)
    pallas_call x7, Pallas kernels, exchange(): pl.pallas_call(functools.partial(exchange_kernel, parts), out_shape=tuple...  119 us
    pallas_call x1, Pallas kernels, attention_backward(): pl.pallas_call(functools.partial(backward_kernel, parts), out_shape=(grad...  93.8 us
    pallas_call x1, Pallas kernels, attention_forward(): pl.pallas_call(forward_kernel, out_shape=(jax.ShapeDtypeStruct((SEG, D, T...  70.9 us
    dot_general x8, matrix products, product(): return jnp.einsum(spec, a, b, preferred_element_type=f32)  16.2 us
    unnamed x86, local copies, waits for them, and re-layouts  11.9 us
    dot_general x5, matrix products, dot(): return jnp.dot(a, b, preferred_element_type=f32)  10.5 us
  transfers between devices with their start and end apart: 4, of which 1 were waited for; matrix products, arithmetic and copies ran while one was open for 9% of the time, Pallas kernels for 55%

profile of v5, /device:TPU:1, one launch (start us, length us, event | category | flops | bytes accessed | tf_op | source)
XLA Modules:
  0.0 376.6 jit_solution(5886045883519199900)
XLA Ops:
  7.3 2.1 fusion.59
  10.5 1.2 fusion.46
  11.7 1.9 fusion.40
  13.7 3.0 fusion.5
  17.7 2.0 fusion.26
  20.0 19.1 %shard_map.245 = bf16[16,192,128]{2,1,0:T(8,128)(2,1)S(1)} custom-call(bf16[16,192,128]{2,1,0:T(8,128)(2,1)S(1)} %pad_maximum_fusion.1.refs_0_), custom_call_target="tpu_custom_call" | custom-call | flops 12000000000 | bytes 4194304 | tf_op jit(solution)/shard_map/pallas_call | solution.py:223
  39.9 70.9 %shard_map.246 = (bf16[16,64,128]{2,1,0:T(8,128)(2,1)S(1)}, f32[8,1,256]{2,1,0:T(1,128)S(1)}, bf16[8,16,128,128]{3,2,1,0:T(8,128)(2,1)S(1)}) custom-call(bf16[16,64,128]{2,1,0:T(8,128)(2,1)S(1)} %slice.81.q_ref, bf16[16,128,128]{2,1,0:T(8,128)(2,1)S(1)} %slice.82.own_ref), custom_call_target="tpu_custom_call" | custom-call | flops 70000001024 | bytes 5242880 | tf_op jit(solution)/shard_map/pallas_call | solution.py:302
  110.8 2.0 copy-done.14
  113.4 18.3 %shard_map.247 = bf16[16,64,128]{2,1,0:T(8,128)(2,1)S(1)} custom-call(bf16[16,64,128]{2,1,0:T(8,128)(2,1)S(1)} %get-tuple-element.37.refs_0_.ctx_ref), custom_call_target="tpu_custom_call" | custom-call | flops 12000000000 | bytes 4194304 | tf_op jit(solution)/shard_map/pallas_call | solution.py:223
  132.8 14.8 %shard_map.248 = bf16[4,128,1024]{2,1,0:T(8,128)(2,1)S(1)} custom-call(bf16[128,1024]{1,0:T(8,128)(2,1)S(1)} %add_convert_fusion.refs_0_), custom_call_target="tpu_custom_call" | custom-call | flops 12000000000 | bytes 4194304 | tf_op jit(solution)/shard_map/pallas_call | solution.py:223
  147.6 1.3 fusion.63
  148.9 1.7 convolution_convert_fusion
  150.6 2.4 fusion.62
  153.0 1.3 convolution_convert_fusion.1
  154.3 1.3 convolution_convert_fusion.3
  155.6 2.5 convolution_convert_fusion.2
  158.6 16.1 %shard_map.249 = (f32[128,1024]{1,0:T(8,128)S(1)}, bf16[1024,1024]{1,0:T(8,128)(2,1)}) custom-call(bf16[4,128,1024]{2,1,0:T(8,128)(2,1)S(1)} %bitcast.109, bf16[2,1024,1024]{2,1,0:T(8,128)(2,1)S(1)} %bitcast.99), custom_call_target="tpu_custom_call" | custom-call | flops 12000000000 | bytes 4194304 | tf_op jit(solution)/shard_map/pallas_call | solution.py:223
  176.2 11.4 %shard_map.250.do_ref = bf16[16,64,128]{2,1,0:T(8,128)(2,1)S(1)} custom-call(bf16[16,64,128]{2,1,0:T(8,128)(2,1)S(1)} %bitcast.106), custom_call_target="tpu_custom_call" | custom-call | flops 12000000000 | bytes 4194304 | tf_op jit(solution)/shard_map/pallas_call | solution.py:223
  190.4 1.2 copy-done.9
  193.5 93.8 %shard_map.251 = (bf16[16,192,128]{2,1,0:T(8,128)(2,1)S(1)}, f32[128,1024]{1,0:T(8,128)S(1)}, bf16[4,128,1024]{2,1,0:T(8,128)(2,1)S(1)}, bf16[4,256,128]{2,1,0:T...) custom-call(bf16[16,64,128]{2,1,0:T(8,128)(2,1)S(1)} %copy-done.6, ...), custom_call_target="tpu_custom_call" | custom-call | flops 80000000000 | bytes 10485760 | tf_op jit(solution)/shard_map/pallas_call | solution.py:416
  289.1 4.2 %fusion.17 = bf16[1024,192]{0,1:T(8,128)(2,1)} fusion(bf16[16,192,128]{2,1,0:T(8,128)(2,1)} %bitcast.119, bf16[16,128,1024]{2,1,0:T(8,128)(2,1)} %bitcast.129), kind=kOutput, calls=%fused_computation.25 | convolution fusion | flops 805502976 | bytes 5373952 | tf_op jit(solution)/shard_map/gtd,gft->df/dot_general | solution.py:62
  293.2 2.0 copy.55
  295.3 2.3 reshape.230
  298.0 5.2 %fusion.45 = (bf16[1024]{0:T(1024)(128)(2,1)S(1)}, f32[128]{0:T(128)S(1)}, f32[128]{0:T(128)S(1)}, bf16[1024]{0:T(1024)(128)(2,1)S(1)}, f32[128,1024]{1,0:T(8,128)S(1)}) fusion(bf16[128,1024]{1,0:T(8,128)(2,1)S(1)} %copy-done.18, f32[128]{0:T(128)S(1)} %copy-done.32, f32[128]{0:T(128)S(1)} %copy-done.30, f32[1024]{0:T(1024)S(1)} %copy-done.26, ...), kind=kOutput, calls=%fused_computation.53 | convolution fusion | flops 806614784 | bytes 7874560 | tf_op jit(solution)/shard_map/ft,df->td/dot_general | solution.py:62
  305.9 22.7 %shard_map.252 = (bf16[208,128]{1,0:T(8,128)(2,1)S(1)}, bf16[8,1024]{1,0:T(8,128)(2,1)S(1)}, f32[32,8,128]{2,1,0:T(8,128)S(1)}) custom-call(bf16[8,208,128]{2,1,0:T(8,128)(2,1)S(1)} %bitcast.104, bf16[32,8,1024]{2,1,0:T(8,128)(2,1)S(1)} %fusion.18.refs_1_, f32[8,128]{1,0:T(8,128)S(1)} %bitcast.112), custom_call_target="tpu_custom_call" | custom-call | flops 12000000000 | bytes 4194304 | tf_op jit(solution)/shard_map/pallas_call | solution.py:223
  328.6 1.9 slice.85
  334.0 1.6 copy-done.8
  335.6 16.4 %shard_map.253 = (bf16[64,16,128]{2,1,0:T(8,128)(2,1)S(1)}, bf16[4,8,1152]{2,1,0:T(8,128)(2,1)S(1)}, bf16[2,1024,1024]{2,1,0:T(8,128)(2,1)S(1)}) custom-call(bf16[16,16,128]{2,1,0:T(8,128)(2,1)S(1)} %bitcast.107, bf16[8,1152]{1,0:T(8,128)(2,1)S(1)} %fusion.57.refs_1_, bf16[1024,1024]{1,0:T(8,128)(2,1)S(1)} %copy-done.8), custom_call_target="tpu_custom_call" | custom-call | flops 12000000000 | bytes 4194304 | tf_op jit(solution)/shard_map/pallas_call | solution.py:223
  352.1 1.9 copy-done.2
  355.0 6.7 %bitcast_convert_fusion = (f32[1024,1024]{1,0:T(8,128)}, f32[1024,1024]{1,0:T(8,128)}) fusion(bf16[2,1024,1024]{2,1,0:T(8,128)(2,1)} %copy-done.2), kind=kLoop, calls=%fused_computation.13 | loop fusion | flops 2097152 | bytes 12582912 | tf_op jit(solution)/shard_map/convert_element_type | solution.py:591
  362.4 1.3 copy.60
  363.7 2.1 reshape.243
  (165 shorter events, 25.4 us)
Async XLA Ops:
  7.2 143.4 %copy-start = (bf16[1024,1024]{1,0:T(8,128)(2,1)S(1)}, bf16[1024,1024]{1,0:T(8,128)(2,1)}, u32[]{:S(2)}) copy-start(bf16[1024,1024]{1,0:T(8,128)(2,1)} %param.25) | copy-start | bytes 6291460
  7.2 6.5 %copy-start.28 = (f32[2,1024]{1,0:T(2,128)S(1)}, f32[2,1024]{1,0:T(2,128)}, u32[]{:S(2)}) copy-start(f32[2,1024]{1,0:T(2,128)} %param.18) | copy-start | bytes 24580
  7.2 32.7 %all-gather.4.cloned.1.call-start = ((), (), s32[]{:S(2)}) async-start(), calls=%async_computation.1 | async-start | bytes 1310720 | tf_op jit(solution)/shard_map/all_gather | solution.py:463
  9.4 104.0 %all-gather.6.cloned.1.call-start = ((), (), s32[]{:S(2)}) async-start(), calls=%async_computation.2 | async-start | bytes 2359296 | tf_op jit(solution)/shard_map/all_gather | solution.py:479
  10.5 3.2 copy-start.29
  11.7 2.0 copy-start.31
  13.6 275.4 %reduce-scatter.2.cloned.1.call-start = ((), (), s32[]{:S(2)}) async-start(), calls=%async_computation.3 | async-start | bytes 2228224 | tf_op jit(solution)/shard_map/reduce_scatter | solution.py:505
  39.2 71.6 %copy-start.5 = (bf16[16,64,128]{2,1,0:T(8,128)(2,1)}, bf16[16,64,128]{2,1,0:T(8,128)(2,1)S(1)}, u32[]{:S(2)}) copy-start(bf16[16,64,128]{2,1,0:T(8,128)(2,1)S(1)} %slice.81.q_ref) | copy-start | bytes 786436
  110.8 2.0 copy-start.14
  112.8 18.9 %copy-start.10 = (bf16[16,64,128]{2,1,0:T(8,128)(2,1)}, bf16[16,64,128]{2,1,0:T(8,128)(2,1)S(1)}, u32[]{:S(2)}) copy-start(bf16[16,64,128]{2,1,0:T(8,128)(2,1)S(1)} %get-tuple-element.37.refs_0_.ctx_ref) | copy-start | bytes 786436
  113.4 18.4 %copy-start.17 = (bf16[128,1024]{1,0:T(8,128)(2,1)S(1)}, bf16[128,1024]{1,0:T(8,128)(2,1)}, u32[]{:S(2)}) copy-start(bf16[128,1024]{1,0:T(8,128)(2,1)} %param.14) | copy-start | bytes 786436
  113.4 18.4 %copy-start.20 = (bf16[1024,1024]{1,0:T(8,128)(2,1)S(1)}, bf16[1024,1024]{1,0:T(8,128)(2,1)}, u32[]{:S(2)}) copy-start(bf16[1024,1024]{1,0:T(8,128)(2,1)} %param.19) | copy-start | bytes 6291460
  113.4 18.4 %copy-start.33 = (f32[1024]{0:T(1024)S(1)}, f32[1024]{0:T(1024)}, u32[]{:S(2)}) copy-start(f32[1024]{0:T(1024)} %param.20) | copy-start | bytes 12292
  132.4 42.6 %copy-start.15 = (f32[128,1024]{1,0:T(8,128)}, f32[128,1024]{1,0:T(8,128)S(1)}, u32[]{:S(2)}) copy-start(f32[128,1024]{1,0:T(8,128)S(1)} %get-tuple-element.81) | copy-start | bytes 1572868
  132.8 14.8 %copy-start.36 = (bf16[1024,1024]{1,0:T(8,128)(2,1)S(1)}, bf16[1024,1024]{1,0:T(8,128)(2,1)}, u32[]{:S(2)}) copy-start(bf16[1024,1024]{1,0:T(8,128)(2,1)} %param.23) | copy-start | bytes 6291460
  147.6 1.3 copy-start.37
  158.5 16.4 %copy-start.23 = (f32[128,1024]{1,0:T(8,128)S(1)}, f32[128,1024]{1,0:T(8,128)}, u32[]{:S(2)}) copy-start(f32[128,1024]{1,0:T(8,128)} %param.27) | copy-start | bytes 1572868
  175.2 12.5 %copy-start.21 = (f32[128,1024]{1,0:T(8,128)}, f32[128,1024]{1,0:T(8,128)S(1)}, u32[]{:S(2)}) copy-start(f32[128,1024]{1,0:T(8,128)S(1)} %get-tuple-element.73) | copy-start | bytes 1572868
  188.5 145.6 %all-gather.8.cloned.1.call-start = ((), (), s32[]{:S(2)}) async-start(), calls=%async_computation.4 | async-start | bytes 2228224 | tf_op jit(solution)/shard_map/all_gather | solution.py:506
  293.2 4.7 %copy-start.18 = (bf16[128,1024]{1,0:T(8,128)(2,1)S(1)}, bf16[128,1024]{1,0:T(8,128)(2,1)}, u32[]{:S(2)}) copy-start(bf16[128,1024]{1,0:T(8,128)(2,1)} %param.14) | copy-start | bytes 786436
  293.2 4.7 %copy-start.26 = (f32[1024]{0:T(1024)S(1)}, f32[1024]{0:T(1024)}, u32[]{:S(2)}) copy-start(f32[1024]{0:T(1024)} %param.15) | copy-start | bytes 12292
  293.2 4.7 %copy-start.30 = (f32[128]{0:T(128)S(1)}, f32[128]{0:T(128)}, u32[]{:S(2)}) copy-start(f32[128]{0:T(128)} %copy-done.29) | copy-start | bytes 1540
  293.2 4.7 %copy-start.32 = (f32[128]{0:T(128)S(1)}, f32[128]{0:T(128)}, u32[]{:S(2)}) copy-start(f32[128]{0:T(128)} %copy-done.31) | copy-start | bytes 1540
  297.9 5.5 %copy-start.25 = (bf16[1,16,8,8]{3,2,1,0:T(8,128)(2,1)S(1)}, bf16[1,16,8,8]{3,2,1,0:T(8,128)(2,1)}, u32[]{:S(2)}) copy-start(bf16[1,16,8,8]{3,2,1,0:T(8,128)(2,1)} %stack.27) | copy-start | bytes 6148
  303.2 2.2 copy-start.4
  305.8 26.2 %copy-start.16 = (f32[128,1024]{1,0:T(8,128)S(1)}, f32[128,1024]{1,0:T(8,128)}, u32[]{:S(2)}) copy-start(f32[128,1024]{1,0:T(8,128)} %copy-done.15) | copy-start | bytes 1572868
  305.8 26.2 %copy-start.35 = (f32[1024]{0:T(1024)S(1)}, f32[1024]{0:T(1024)}, u32[]{:S(2)}) copy-start(f32[1024]{0:T(1024)} %param.26) | copy-start | bytes 12292
  328.5 4.4 %copy-start.19 = (bf16[128,1024]{1,0:T(8,128)(2,1)S(1)}, bf16[128,1024]{1,0:T(8,128)(2,1)}, u32[]{:S(2)}) copy-start(bf16[128,1024]{1,0:T(8,128)(2,1)} %param.14) | copy-start | bytes 786436
  328.6 4.4 %copy-start.22 = (f32[128,1024]{1,0:T(8,128)S(1)}, f32[128,1024]{1,0:T(8,128)}, u32[]{:S(2)}) copy-start(f32[128,1024]{1,0:T(8,128)} %copy-done.21) | copy-start | bytes 1572868
  334.0 1.6 copy-start.8
  352.0 1.9 copy-start.2
  361.7 8.4 %copy-start.1 = (bf16[1024,1024]{1,0:T(8,128)(2,1)S(1)}, bf16[1024,1024]{1,0:T(8,128)(2,1)}, u32[]{:S(2)}) copy-start(bf16[1024,1024]{1,0:T(8,128)(2,1)} %param.25) | copy-start | bytes 6291460
  (11 other events, 10.5 us)
Sparse Core Ops, SparseCore 0:
  10.3 26.2 all-gather.3
  39.5 73.8 all-gather.5
  188.6 86.9 reduce-scatter.1
  289.2 44.0 all-gather.7

commit v6 on v5

--- a/solution.py
+++ b/solution.py
@@ -236,8 +236,10 @@
     return result[0] if len(transfers) == 1 else result
 
 
-FWD_CHUNK = 4
+FWD_CHUNK = 1
+FWD_AHEAD = 3
 BWD_CHUNK = 2
+BWD_OTHERS = 2
 
 
 def forward_kernel(q_ref, own_ref, ctx_ref, lse_ref, kv_ref, qb, m_s, l_s, acc, *sems):
@@ -250,9 +252,14 @@
             own_ref.at[rows], kv_ref.at[place, rows], sems, (chunk, hop - 1), KEY_AXES, peer
         )
 
-    for chunk in range(SEG // FWD_CHUNK):
+    chunks = SEG // FWD_CHUNK
+
+    def send_all(chunk):
         for hop in range(1, CYC):
             send(chunk, hop, me, (me + hop) % CYC).start()
+
+    for chunk in range(FWD_AHEAD):
+        send_all(chunk)
     kv_ref[me] = own_ref[...]
     for pair in range(PAIRS):
         q = pair_of(q_ref, pair).astype(f32) * score_scale
@@ -281,19 +288,25 @@
         return carry
 
     def chunk_step(chunk, carry):
+        @pl.when(chunk + FWD_AHEAD < chunks)
+        def _():
+            send_all(chunk + FWD_AHEAD)
+
         for hop in range(1, CYC):
             origin = (me - hop + CYC) % CYC
             send(chunk, hop, origin, origin).wait_recv()
         return lax.fori_loop(chunk * FWD_CHUNK, (chunk + 1) * FWD_CHUNK, key_step, carry)
 
-    lax.fori_loop(0, SEG // FWD_CHUNK, chunk_step, 0)
+    lax.fori_loop(0, chunks, chunk_step, 0)
     for pair in range(PAIRS):
         row_sum = l_s[pair]
         o = (acc[pair] / row_sum).astype(bf16)
         ctx_ref[2 * pair] = o[:, :T]
         ctx_ref[2 * pair + 1] = o[:, T:]
         lse_ref[pair] = m_s[pair] + jnp.log(row_sum)
-    for chunk in range(SEG // FWD_CHUNK):
+
+    @pl.loop(0, chunks)
+    def _(chunk):
         for hop in range(1, CYC):
             send(chunk, hop, me, (me + hop) % CYC).wait_send()
 
@@ -332,8 +345,6 @@
     sems = sems[:2]
     greet(KEY_AXES, HEAD_AXES)
     me = group_index(KEY_AXES)
-    for part in parts[:-1]:
-        part.begin()
 
     def send(chunk, hop, place, source, peer):
         rows = pl.ds(chunk * BWD_CHUNK, BWD_CHUNK)
@@ -378,6 +389,12 @@
         for hop in range(1, CYC):
             peer = (me + hop) % CYC
             send(chunks - 1 - step, hop, me, peer, peer).start()
+
+        @pl.when(step == BWD_OTHERS)
+        def _():
+            for part in parts[:-1]:
+                part.begin()
+
         return carry
 
     lax.fori_loop(0, chunks, chunk_step, 0)
@@ -403,7 +420,9 @@
     parts[-1].begin()
     for part in parts:
         part.finish()
-    for chunk in range(chunks):
+
+    @pl.loop(0, chunks)
+    def _(chunk):
         for hop in range(1, CYC):
             peer = (me + hop) % CYC
             send(chunk, hop, me, peer, peer).wait_send()
@@ -497,10 +516,11 @@
         ]
     ).astype(bf16)
     norm_parts = dot(hidden_grad_bf, fc_weight.T).astype(bf16).reshape(-1, tokens, width)
-    normed_two_grad, wide_core = exchange(
+    normed_two_grad, wide_core, bias_pair = exchange(
         5,
         (norm_parts, ("tp",), "reduce", f32),
         (wide_grads.reshape(2, width, width), ("sc",), "reduce"),
+        (jnp.sum(hidden_grad, axis=0).reshape(-1, T), ("bl",), "gather", f32),
     )
     wide_part = lax.psum_scatter(wide_core, CHIP_ROW_AXES, scatter_dimension=0, tiled=True)
     wide_core = lax.all_gather(wide_part, CHIP_ROW_AXES, axis=0, tiled=True)
@@ -513,7 +533,15 @@
     mlp_parts = dot(activation, proj_weight).astype(bf16).reshape(-1, tokens, width)
     row_groups = width // fine // 4
     context_rows = context_t.reshape(row_groups, 4, fine, tokens).transpose(1, 0, 2, 3)
-    head_grads, mlp_out, grad_tokens, context_tokens, normed_all, token_grads = attention_backward(
+    (
+        head_grads,
+        mlp_out,
+        grad_tokens,
+        context_tokens,
+        normed_all,
+        bias_parts,
+        token_grads,
+    ) = attention_backward(
         query_t,
         key_values,
         context_grad_heads,
@@ -523,6 +551,7 @@
         (residual_grad_bf, ("tp",), "gather"),
         (context_rows.reshape(4, row_groups * fine, tokens), ("tp",), "swap"),
         (normed_core, ("sc",), "gather"),
+        (jnp.sum(bias_pair, axis=0), HEAD_AXES, "gather", f32),
     )
     block_out = residual + mlp_out + proj_bias
     token_grads = token_grads.reshape(SEG, 3, D, tokens).transpose(1, 0, 2, 3)
@@ -540,71 +569,55 @@
             jnp.sum(normed_one_grad, axis=0),
         ]
     ).astype(bf16)
-    count = vectors.shape[0]
-    vectors = vectors.reshape(count, SEG, CYC, fine).transpose(2, 1, 0, 3)
+    vectors = vectors.reshape(-1, SEG, CYC, fine).transpose(2, 1, 0, 3)
     head_sums = jnp.sum(head_grads.astype(f32), axis=(0, 2)).astype(bf16).reshape(3, CYC, fine)
+    own_head = jnp.arange(SEG)[None, :, None, None] == group_index(HEAD_AXES)
+    head_sums = jnp.where(own_head, head_sums.transpose(1, 0, 2)[:, None], 0)
+    narrow = jnp.concatenate([vectors, head_sums], axis=2)
+    count = narrow.shape[2]
+    narrow = narrow.reshape(CYC, SEG, 1, count * fine)
     by_core = head_grads.reshape(-1, 2, 2, 3 * D, tokens).transpose(1, 0, 2, 3, 4)
     qkv_part = product(
         "gtd,gft->df",
         normed_all.reshape(SEG, tokens, width),
         by_core.reshape(SEG, 3 * D, tokens),
     ).astype(bf16)
-    qkv_part = qkv_part.reshape(SEG, CYC, fine * 3 * D).transpose(1, 0, 2)
+    qkv_lines = fine * 3 * D // T
+    qkv_part = qkv_part.reshape(SEG, CYC, qkv_lines, T).transpose(1, 0, 2, 3)
     packed = jnp.concatenate(
-        [
-            qkv_part.reshape(CYC, -1),
-            vectors.reshape(CYC, -1),
-            head_sums.transpose(1, 0, 2).reshape(CYC, -1),
-        ],
-        axis=1,
-    )
-    length = packed.shape[1]
-    padded = -length % (16 * T)
-    packed = jnp.pad(packed, ((0, 0), (0, padded)))
+        [qkv_part, jnp.pad(narrow, ((0, 0), (0, 0), (0, 15 - qkv_lines), (0, T - count * fine)))],
+        axis=2,
+    )
     out_part = product("gct,gtd->cd", context_tokens, grad_tokens).astype(bf16)
-    summed, out_rows, bias_parts = exchange(
+    summed, out_rows = exchange(
+        7,
+        (packed, KEY_AXES, "reduce"),
+        (out_part.reshape(row_groups, fine, width), ROW_AXES, "reduce"),
+    )
+    fc_bias_grad = jnp.sum(bias_parts, axis=0).reshape(-1)
+    moved, out_rows, wide_sum = exchange(
         8,
-        (packed.reshape(CYC, -1, T), KEY_AXES, "reduce"),
-        (out_part.reshape(row_groups, fine, width), ROW_AXES, "reduce"),
-        (jnp.sum(hidden_grad, axis=0).reshape(-1, T), ROW_AXES, "gather", f32),
-    )
-    fc_bias_grad = jnp.sum(bias_parts, axis=0).reshape(-1)
-    summed = summed.reshape(-1)
-    qkv_size, vector_size = SEG * fine * 3 * D, SEG * count * fine
-    to_rows = jnp.concatenate(
-        [
-            summed[:qkv_size].reshape(SEG, -1),
-            summed[qkv_size : qkv_size + vector_size].reshape(SEG, -1),
-        ],
-        axis=1,
-    )
-    to_rows = jnp.pad(to_rows, ((0, 0), (0, -to_rows.shape[1] % (16 * T))))
-    bias_rows = summed[qkv_size + vector_size : qkv_size + vector_size + 3 * fine]
-    bias_rows = jnp.pad(bias_rows.reshape(3, fine).T, ((0, 0), (0, T - 3)))
-    moved, out_rows, wide_sum = exchange(
-        9,
-        (to_rows.reshape(SEG, -1, T), HEAD_AXES + ("tp",), "spread"),
-        (jnp.concatenate([out_rows, bias_rows], axis=1), ("tp",), "gather"),
+        (summed, HEAD_AXES + ("tp",), "spread"),
+        (out_rows, ("tp",), "gather"),
         (wide_core, ("sc",), "gather"),
     )
     fc_weight_grad = wide_sum[0].astype(f32)
     proj_weight_grad = wide_sum[1].astype(f32)
     own_rows = 4 * fine
-    moved = moved.reshape(SEG, 4, -1)
-    qkv_rows = moved[:, :, : fine * 3 * D].reshape(SEG, 4, fine, 3, D).transpose(1, 2, 3, 0, 4)
+    moved = moved.reshape(SEG, 4, -1, T)
+    qkv_rows = moved[:, :, :qkv_lines].reshape(SEG, 4, fine, 3, D).transpose(1, 2, 3, 0, 4)
     qkv_rows = qkv_rows.reshape(own_rows, 3 * width).astype(f32)
-    narrow = moved[:, :, fine * 3 * D : fine * 3 * D + count * fine].astype(f32)
-    narrow = jnp.sum(narrow.reshape(SEG, 4, count, fine), axis=0).transpose(1, 0, 2)
-    narrow = narrow.reshape(count, own_rows)
-    out_rows = out_rows.reshape(own_rows, -1).astype(f32)
+    narrow = jnp.sum(moved[:, :, qkv_lines, : count * fine].astype(f32), axis=0)
+    narrow = narrow.reshape(4, count, fine).transpose(1, 0, 2).reshape(count, own_rows)
+    out_rows = out_rows.reshape(own_rows, width).astype(f32)
     return (
         block_out,
         input_grad,
         narrow[4],
         narrow[5],
         qkv_rows,
-        jnp.stack([out_rows[:, width], out_rows[:, width + 2]]),
-        out_rows[:, :width],
+        jnp.stack([narrow[6], narrow[8]]),
+        out_rows,
         narrow[0],
         narrow[1],
         narrow[2],

time: 377 us -> 387 us (1.027)
  waiting for transfers between devices: 0.65 us -> 23.9 us
  Pallas kernels: 284 us -> 272 us
    all_gather x1, waiting for transfers between devices: 0.01 us -> 15.4 us  [per_device(): wide_core = lax.all_gather(wide_part, CHIP_ROW_AXES, axis=0, tiled=True)]
    pallas_call x7, Pallas kernels: 119 us -> 107 us  [exchange(): pl.pallas_call(functools.partial(exchange_kernel, parts), out_shape=tuple...]
    all_gather x1, waiting for transfers between devices: 0.57 us -> 8.45 us  [per_device(): normed_core = lax.all_gather(normed_bf, ('sz', 'bh'), axis=0, tiled=True)]
    unnamed x86 -> x87, local copies, waits for them, and re-layouts: 11.9 us -> 9.84 us
  transfers between devices with their start and end apart: 4 -> 4, of which waited for: 1 -> 2; matrix products, arithmetic and copies ran while one was open for 9% -> 9% of each run, Pallas kernels for 55% -> 52%
where the time goes in v6:
time: 387 us
  Pallas kernels  272 us (70%)
  local copies, waits for them, and re-layouts  30.1 us (8%)
  matrix products  27.3 us (7%)
  waiting for transfers between devices  23.9 us (6%)
  other arithmetic  19.1 us (5%)
  between operations  14.6 us (4%)
    pallas_call x7, Pallas kernels, exchange(): pl.pallas_call(functools.partial(exchange_kernel, parts), out_shape=tuple...  107 us
    pallas_call x1, Pallas kernels, attention_backward(): pl.pallas_call(functools.partial(backward_kernel, parts), out_shape=(grad...  95.6 us
    pallas_call x1, Pallas kernels, attention_forward(): pl.pallas_call(forward_kernel, out_shape=(jax.ShapeDtypeStruct((SEG, D, T...  68.7 us
    dot_general x8, matrix products, product(): return jnp.einsum(spec, a, b, preferred_element_type=f32)  16.8 us
    all_gather x1, waiting for transfers between devices, per_device(): wide_core = lax.all_gather(wide_part, CHIP_ROW_AXES, axis=0, tiled=True)  15.4 us
    dot_general x5, matrix products, dot(): return jnp.dot(a, b, preferred_element_type=f32)  10.5 us
    unnamed x87, local copies, waits for them, and re-layouts  9.84 us
    all_gather x1, waiting for transfers between devices, per_device(): normed_core = lax.all_gather(normed_bf, ('sz', 'bh'), axis=0, tiled=True)  8.45 us
  transfers between devices with their start and end apart: 4, of which 2 were waited for; matrix products, arithmetic and copies ran while one was open for 9% of the time, Pallas kernels for 52%

profile of v6, /device:TPU:1, one launch (start us, length us, event | category | flops | bytes accessed | tf_op | source)
XLA Modules:
  0.0 386.6 jit_solution(13956553705179989757)
XLA Ops:
  7.3 2.1 fusion.50
  11.7 1.9 fusion.38
  13.7 3.0 fusion.5
  17.7 2.0 fusion.26
  20.0 19.1 %shard_map.245 = bf16[16,192,128]{2,1,0:T(8,128)(2,1)S(1)} custom-call(bf16[16,192,128]{2,1,0:T(8,128)(2,1)S(1)} %pad_maximum_fusion.1.refs_0_), custom_call_target="tpu_custom_call" | custom-call | flops 12000000000 | bytes 4194304 | tf_op jit(solution)/shard_map/pallas_call | solution.py:223
  40.4 68.7 %shard_map.246 = (bf16[16,64,128]{2,1,0:T(8,128)(2,1)S(1)}, f32[8,1,256]{2,1,0:T(1,128)S(1)}, bf16[8,16,128,128]{3,2,1,0:T(8,128)(2,1)S(1)}) custom-call(bf16[16,64,128]{2,1,0:T(8,128)(2,1)S(1)} %slice.70.q_ref, bf16[16,128,128]{2,1,0:T(8,128)(2,1)S(1)} %slice.71.own_ref), custom_call_target="tpu_custom_call" | custom-call | flops 70000001024 | bytes 5242880 | tf_op jit(solution)/shard_map/pallas_call | solution.py:315
  109.2 2.0 copy-done.13
  111.2 8.4 %all-gather.6.cloned.1.call-done.refs_3_ = bf16[1024,1024]{1,0:T(8,128)(2,1)} async-done(((bf16[128,1024]{1,0:T(8,128)(2,1)}), bf16[1024,1024]{1,0:T(8,128)(2,1)}) %all-gather.6.cloned.1.call-update) | async-done | bytes 2097168 | tf_op jit(solution)/shard_map/all_gather | solution.py:498
  119.7 9.7 %shard_map.247 = bf16[16,64,128]{2,1,0:T(8,128)(2,1)S(1)} custom-call(bf16[16,64,128]{2,1,0:T(8,128)(2,1)S(1)} %get-tuple-element.38.refs_0_.ctx_ref), custom_call_target="tpu_custom_call" | custom-call | flops 12000000000 | bytes 4194304 | tf_op jit(solution)/shard_map/pallas_call | solution.py:223
  130.5 15.1 %shard_map.248 = bf16[4,128,1024]{2,1,0:T(8,128)(2,1)S(1)} custom-call(bf16[128,1024]{1,0:T(8,128)(2,1)S(1)} %add_convert_fusion.refs_0_), custom_call_target="tpu_custom_call" | custom-call | flops 12000000000 | bytes 4194304 | tf_op jit(solution)/shard_map/pallas_call | solution.py:223
  146.9 1.7 convolution_convert_fusion
  148.5 2.4 fusion.53
  151.0 1.3 convolution_convert_fusion.1
  152.3 1.3 convolution_convert_fusion.3
  153.6 2.5 convolution_convert_fusion.2
  156.5 17.7 %shard_map.249 = (f32[128,1024]{1,0:T(8,128)S(1)}, bf16[1024,1024]{1,0:T(8,128)(2,1)}, f32[2,8,128]{2,1,0:T(8,128)S(1)}) custom-call(bf16[4,128,1024]{2,1,0:T(8,128)(2,1)S(1)} %bitcast.98, bf16[2,1024,1024]{2,1,0:T(8,128)(2,1)S(1)} %bitcast.88, f32[8,128]{1,0:T(8,128)S(1)} %bitcast.101), custom_call_target="tpu_custom_call" | custom-call | flops 12000000000 | bytes 4194304 | tf_op jit(solution)/shard_map/pallas_call | solution.py:223
  175.8 10.4 %shard_map.250.do_ref = bf16[16,64,128]{2,1,0:T(8,128)(2,1)S(1)} custom-call(bf16[16,64,128]{2,1,0:T(8,128)(2,1)S(1)} %bitcast.96), custom_call_target="tpu_custom_call" | custom-call | flops 12000000000 | bytes 4194304 | tf_op jit(solution)/shard_map/pallas_call | solution.py:223
  192.1 95.6 %shard_map.251 = (bf16[16,192,128]{2,1,0:T(8,128)(2,1)S(1)}, f32[128,1024]{1,0:T(8,128)S(1)}, bf16[4,128,1024]{2,1,0:T(8,128)(2,1)S(1)}, bf16[4,256,128]{2,1,0:T...) custom-call(bf16[16,64,128]{2,1,0:T(8,128)(2,1)S(1)} %copy-done.5, ...), custom_call_target="tpu_custom_call" | custom-call | flops 80000000000 | bytes 10485760 | tf_op jit(solution)/shard_map/pallas_call | solution.py:435
  288.5 4.0 %fusion.17 = bf16[1024,192]{0,1:T(8,128)(2,1)} fusion(bf16[16,192,128]{2,1,0:T(8,128)(2,1)S(1)} %bitcast.108, bf16[16,128,1024]{2,1,0:T(8,128)(2,1)} %bitcast.116), kind=kOutput, calls=%fused_computation.25 | convolution fusion | flops 805502976 | bytes 5373952 | tf_op jit(solution)/shard_map/gtd,gft->df/dot_general | solution.py:62
  292.5 2.0 copy.54
  294.5 2.4 reshape.215
  296.9 1.9 copy.61
  300.7 6.0 %fusion.43 = (bf16[1024]{0:T(1024)(128)(2,1)S(1)}, f32[128]{0:T(128)S(1)}, f32[128]{0:T(128)S(1)}, bf16[1024]{0:T(1024)(128)(2,1)S(1)}, f32[128,1024]{1,0:T(8,128)}) fusion(bf16[128,1024]{1,0:T(8,128)(2,1)S(1)} %copy-done.17, f32[128]{0:T(128)} %copy-done.32, f32[128]{0:T(128)S(1)} %copy-done.31, f32[1024]{0:T(1024)S(1)} %copy-done.27, ...), kind=kOutput, calls=%fused_computation.51 | convolution fusion | flops 806614784 | bytes 7874560 | tf_op jit(solution)/shard_map/ft,df->td/dot_general | solution.py:62
  308.5 1.4 fusion.45.refs_0_
  312.3 18.9 %shard_map.252 = (bf16[16,16,128]{2,1,0:T(8,128)(2,1)S(1)}, bf16[8,1024]{1,0:T(8,128)(2,1)S(1)}) custom-call(bf16[8,16,16,128]{3,2,1,0:T(8,128)(2,1)S(1)} %fusion.45.refs_0_, bf16[32,8,1024]{2,1,0:T(8,128)(2,1)S(1)} %fusion.18.refs_1_), custom_call_target="tpu_custom_call" | custom-call | flops 12000000000 | bytes 4194304 | tf_op jit(solution)/shard_map/pallas_call | solution.py:223
  331.3 15.4 %all-gather.8.cloned.1.call-done.refs_2_ = bf16[1024,1024]{1,0:T(8,128)(2,1)} async-done(((bf16[64,1024]{1,0:T(8,128)(2,1)}), bf16[1024,1024]{1,0:T(8,128)(2,1)}) %all-gather.8.cloned.1.call-update) | async-done | bytes 2097168 | tf_op jit(solution)/shard_map/all_gather | solution.py:526
  346.7 1.6 copy-done.7
  348.3 16.2 %shard_map.253 = (bf16[64,16,128]{2,1,0:T(8,128)(2,1)S(1)}, bf16[4,8,1024]{2,1,0:T(8,128)(2,1)S(1)}, bf16[2,1024,1024]{2,1,0:T(8,128)(2,1)S(1)}) custom-call(bf16[16,16,128]{2,1,0:T(8,128)(2,1)S(1)} %get-tuple-element.51.refs_0_, bf16[8,1024]{1,0:T(8,128)(2,1)S(1)} %get-tuple-element.52.refs_1_, bf16[1024,1024]{1,0:T(8,128)(2,1)S(1)} %copy-done.7), custom_call_target="tpu_custom_call" | custom-call | flops 12000000000 | bytes 4194304 | tf_op jit(solution)/shard_map/pallas_call | solution.py:223
  365.4 4.4 %bitcast_convert_fusion = (f32[1024,1024]{1,0:T(8,128)}, f32[1024,1024]{1,0:T(8,128)}) fusion(bf16[2,1024,1024]{2,1,0:T(8,128)(2,1)S(1)} %get-tuple-element.56), kind=kLoop, calls=%fused_computation.13 | loop fusion | flops 2097152 | bytes 12582912 | tf_op jit(solution)/shard_map/convert_element_type | solution.py:605
  370.2 1.7 reshape.226
  371.8 1.3 copy.58
  373.2 2.1 reshape.222
  (159 shorter events, 27.7 us)
Async XLA Ops:
  7.2 141.3 %copy-start = (bf16[1024,1024]{1,0:T(8,128)(2,1)S(1)}, bf16[1024,1024]{1,0:T(8,128)(2,1)}, u32[]{:S(2)}) copy-start(bf16[1024,1024]{1,0:T(8,128)(2,1)} %param.25) | copy-start | bytes 6291460
  7.2 6.5 %copy-start.29 = (f32[2,1024]{1,0:T(2,128)S(1)}, f32[2,1024]{1,0:T(2,128)}, u32[]{:S(2)}) copy-start(f32[2,1024]{1,0:T(2,128)} %param.18) | copy-start | bytes 24580
  7.2 33.2 %all-gather.4.cloned.1.call-start = ((), (), s32[]{:S(2)}) async-start(), calls=%async_computation.1 | async-start | bytes 1310720 | tf_op jit(solution)/shard_map/all_gather | solution.py:482
  9.4 110.3 %all-gather.6.cloned.1.call-start = ((), (), s32[]{:S(2)}) async-start(), calls=%async_computation.2 | async-start | bytes 2359296 | tf_op jit(solution)/shard_map/all_gather | solution.py:498
  10.5 3.2 copy-start.30
  11.7 2.0 copy-start.32
  13.6 287.0 %reduce-scatter.2.cloned.1.call-start = ((), (), s32[]{:S(2)}) async-start(), calls=%async_computation.3 | async-start | bytes 2228224 | tf_op jit(solution)/shard_map/reduce_scatter | solution.py:525
  39.2 70.0 %copy-start.4 = (bf16[16,64,128]{2,1,0:T(8,128)(2,1)}, bf16[16,64,128]{2,1,0:T(8,128)(2,1)S(1)}, u32[]{:S(2)}) copy-start(bf16[16,64,128]{2,1,0:T(8,128)(2,1)S(1)} %slice.70.q_ref) | copy-start | bytes 786436
  109.2 2.0 copy-start.13
  111.2 18.2 %copy-start.9 = (bf16[16,64,128]{2,1,0:T(8,128)(2,1)}, bf16[16,64,128]{2,1,0:T(8,128)(2,1)S(1)}, u32[]{:S(2)}) copy-start(bf16[16,64,128]{2,1,0:T(8,128)(2,1)S(1)} %get-tuple-element.38.refs_0_.ctx_ref) | copy-start | bytes 786436
  119.7 9.8 %copy-start.16 = (bf16[128,1024]{1,0:T(8,128)(2,1)S(1)}, bf16[128,1024]{1,0:T(8,128)(2,1)}, u32[]{:S(2)}) copy-start(bf16[128,1024]{1,0:T(8,128)(2,1)} %param.14) | copy-start | bytes 786436
  119.7 9.8 %copy-start.19 = (bf16[1024,1024]{1,0:T(8,128)(2,1)S(1)}, bf16[1024,1024]{1,0:T(8,128)(2,1)}, u32[]{:S(2)}) copy-start(bf16[1024,1024]{1,0:T(8,128)(2,1)} %param.19) | copy-start | bytes 6291460
  119.7 9.8 %copy-start.34 = (f32[1024]{0:T(1024)S(1)}, f32[1024]{0:T(1024)}, u32[]{:S(2)}) copy-start(f32[1024]{0:T(1024)} %param.20) | copy-start | bytes 12292
  130.0 44.4 %copy-start.14 = (f32[128,1024]{1,0:T(8,128)}, f32[128,1024]{1,0:T(8,128)S(1)}, u32[]{:S(2)}) copy-start(f32[128,1024]{1,0:T(8,128)S(1)} %get-tuple-element.83) | copy-start | bytes 1572868
  130.4 15.1 %copy-start.38 = (bf16[1024,1024]{1,0:T(8,128)(2,1)S(1)}, bf16[1024,1024]{1,0:T(8,128)(2,1)}, u32[]{:S(2)}) copy-start(bf16[1024,1024]{1,0:T(8,128)(2,1)} %param.23) | copy-start | bytes 6291460
  156.5 18.0 %copy-start.23 = (f32[128,1024]{1,0:T(8,128)S(1)}, f32[128,1024]{1,0:T(8,128)}, u32[]{:S(2)}) copy-start(f32[128,1024]{1,0:T(8,128)} %param.27) | copy-start | bytes 1572868
  174.7 11.5 %copy-start.20 = (f32[128,1024]{1,0:T(8,128)}, f32[128,1024]{1,0:T(8,128)S(1)}, u32[]{:S(2)}) copy-start(f32[128,1024]{1,0:T(8,128)S(1)} %get-tuple-element.75) | copy-start | bytes 1572868
  187.0 159.6 %all-gather.8.cloned.1.call-start = ((), (), s32[]{:S(2)}) async-start(), calls=%async_computation.4 | async-start | bytes 2228224 | tf_op jit(solution)/shard_map/all_gather | solution.py:526
  294.5 6.1 %copy-start.17 = (bf16[128,1024]{1,0:T(8,128)(2,1)S(1)}, bf16[128,1024]{1,0:T(8,128)(2,1)}, u32[]{:S(2)}) copy-start(bf16[128,1024]{1,0:T(8,128)(2,1)} %param.14) | copy-start | bytes 786436
  294.5 6.1 %copy-start.27 = (f32[1024]{0:T(1024)S(1)}, f32[1024]{0:T(1024)}, u32[]{:S(2)}) copy-start(f32[1024]{0:T(1024)} %param.15) | copy-start | bytes 12292
  294.5 6.1 %copy-start.31 = (f32[128]{0:T(128)S(1)}, f32[128]{0:T(128)}, u32[]{:S(2)}) copy-start(f32[128]{0:T(128)} %copy-done.30) | copy-start | bytes 1540
  300.6 6.6 %copy-start.26 = (bf16[1,16,8,8]{3,2,1,0:T(8,128)(2,1)S(1)}, bf16[1,16,8,8]{3,2,1,0:T(8,128)(2,1)}, u32[]{:S(2)}) copy-start(bf16[1,16,8,8]{3,2,1,0:T(8,128)(2,1)} %stack.26) | copy-start | bytes 6148
  300.7 6.6 %copy-start.25 = (bf16[1,16,8,8]{3,2,1,0:T(8,128)(2,1)S(1)}, bf16[1,16,8,8]{3,2,1,0:T(8,128)(2,1)}, u32[]{:S(2)}) copy-start(bf16[1,16,8,8]{3,2,1,0:T(8,128)(2,1)} %stack.27) | copy-start | bytes 6148
  300.7 6.6 %copy-start.37 = (pred[16]{0:T(512)(128)(4,1)S(1)}, pred[16]{0:T(512)(128)(4,1)}, u32[]{:S(2)}) copy-start(pred[16]{0:T(512)(128)(4,1)} %iota_compare_fusion.1) | copy-start | bytes 52
  306.7 3.2 copy-start.3
  307.4 3.0 copy-start.15
  307.4 3.0 copy-start.36
  308.5 2.8 copy-start.18
  308.5 2.8 copy-start.21
  308.5 2.8 copy-start.22
  308.5 2.8 copy-start.33
  370.1 10.0 %copy-start.1 = (bf16[1024,1024]{1,0:T(8,128)(2,1)S(1)}, bf16[1024,1024]{1,0:T(8,128)(2,1)}, u32[]{:S(2)}) copy-start(bf16[1024,1024]{1,0:T(8,128)(2,1)} %param.25) | copy-start | bytes 6291460
  (13 other events, 13.4 us)
Sparse Core Ops, SparseCore 0:
  10.3 26.2 all-gather.3
  39.5 80.1 all-gather.5
  187.2 87.2 reduce-scatter.1
  300.7 45.9 all-gather.7

commit v7 on v6

--- a/solution.py
+++ b/solution.py
@@ -497,10 +497,10 @@
     own_kv, gathered_cot = lax.optimization_barrier((own_kv, gathered_cot))
     normed_core = lax.all_gather(normed_bf, ("sz", "bh"), axis=0, tiled=True)
     context_heads, log_total, key_values = attention_forward(query_t, own_kv)
-    context_heads, normed_core = lax.optimization_barrier((context_heads, normed_core))
 
     context_t = swap_heads(3, context_heads).reshape(width, tokens)
     residual = hidden_f + product("ct,cd->td", context_t, out_weight) + out_bias
+    residual, normed_core = lax.optimization_barrier((residual, normed_core))
     scaled_two, inverse_two, normed_two = normalize(residual, ln2_gain, ln2_bias)
     gathered_norm = exchange(4, (normed_two.astype(bf16), ("tp",), "gather"))
     gathered_norm = gathered_norm.reshape(-1, width)
@@ -516,6 +516,9 @@
         ]
     ).astype(bf16)
     norm_parts = dot(hidden_grad_bf, fc_weight.T).astype(bf16).reshape(-1, tokens, width)
+    mlp_parts = dot(activation, proj_weight).astype(bf16)
+    mlp_parts, norm_parts = lax.optimization_barrier((mlp_parts, norm_parts))
+    mlp_out = lax.psum_scatter(mlp_parts, "tp", scatter_dimension=0, tiled=True)
     normed_two_grad, wide_core, bias_pair = exchange(
         5,
         (norm_parts, ("tp",), "reduce", f32),
@@ -523,19 +526,16 @@
         (jnp.sum(hidden_grad, axis=0).reshape(-1, T), ("bl",), "gather", f32),
     )
     wide_part = lax.psum_scatter(wide_core, CHIP_ROW_AXES, scatter_dimension=0, tiled=True)
-    wide_core = lax.all_gather(wide_part, CHIP_ROW_AXES, axis=0, tiled=True)
     residual_grad = cotangent + norm_back(normed_two_grad, scaled_two, inverse_two, ln2_gain)
     residual_grad_bf = residual_grad.astype(bf16)
     context_grad = product("td,cd->ct", residual_grad_bf, out_weight).astype(bf16)
     context_grad_heads = swap_heads(6, context_grad.reshape(SEG, D, tokens))
 
     fine = D // CYC
-    mlp_parts = dot(activation, proj_weight).astype(bf16).reshape(-1, tokens, width)
     row_groups = width // fine // 4
     context_rows = context_t.reshape(row_groups, 4, fine, tokens).transpose(1, 0, 2, 3)
     (
         head_grads,
-        mlp_out,
         grad_tokens,
         context_tokens,
         normed_all,
@@ -547,13 +547,17 @@
         context_grad_heads,
         context_heads,
         log_total,
-        (mlp_parts, ("tp",), "reduce", f32),
         (residual_grad_bf, ("tp",), "gather"),
         (context_rows.reshape(4, row_groups * fine, tokens), ("tp",), "swap"),
         (normed_core, ("sc",), "gather"),
         (jnp.sum(bias_pair, axis=0), HEAD_AXES, "gather", f32),
     )
-    block_out = residual + mlp_out + proj_bias
+    head_grads, normed_all, token_grads, wide_part, mlp_out = lax.optimization_barrier(
+        (head_grads, normed_all, token_grads, wide_part, mlp_out)
+    )
+    block_out = residual + mlp_out.astype(f32) + proj_bias
+    wide_sum = lax.all_gather(wide_part, ROW_AXES, axis=0, tiled=True)
+    wide_sum = wide_sum.reshape(-1, 2, width // 4, width)
     token_grads = token_grads.reshape(SEG, 3, D, tokens).transpose(1, 0, 2, 3)
     token_grads = token_grads.reshape(3 * width, tokens)
     normed_one_grad = product("ft,df->td", token_grads, qkv_weight)
@@ -595,14 +599,13 @@
         (out_part.reshape(row_groups, fine, width), ROW_AXES, "reduce"),
     )
     fc_bias_grad = jnp.sum(bias_parts, axis=0).reshape(-1)
-    moved, out_rows, wide_sum = exchange(
+    moved, out_rows = exchange(
         8,
         (summed, HEAD_AXES + ("tp",), "spread"),
         (out_rows, ("tp",), "gather"),
-        (wide_core, ("sc",), "gather"),
-    )
-    fc_weight_grad = wide_sum[0].astype(f32)
-    proj_weight_grad = wide_sum[1].astype(f32)
+    )
+    fc_weight_grad = wide_sum[:, 0].reshape(width, width).astype(f32)
+    proj_weight_grad = wide_sum[:, 1].reshape(width, width).astype(f32)
     own_rows = 4 * fine
     moved = moved.reshape(SEG, 4, -1, T)
     qkv_rows = moved[:, :, :qkv_lines].reshape(SEG, 4, fine, 3, D).transpose(1, 2, 3, 0, 4)

time: 387 us -> 361 us (0.933)
  waiting for transfers between devices: 23.9 us -> 0.46 us
  local copies, waits for them, and re-layouts: 30.1 us -> 17.4 us
  matrix products: 27.3 us -> 32.1 us
    all_gather x1, waiting for transfers between devices: 15.4 us -> 0.01 us  [per_device(): wide_sum = lax.all_gather(wide_part, ROW_AXES, axis=0, tiled=True)]
    pallas_call x7, Pallas kernels: 107 us -> 118 us  [exchange(): pl.pallas_call(functools.partial(exchange_kernel, parts), out_shape=tuple...]
    all_gather x1, waiting for transfers between devices: 8.45 us -> 0.29 us  [per_device(): normed_core = lax.all_gather(normed_bf, ('sz', 'bh'), axis=0, tiled=True)]
    pallas_call x1, Pallas kernels: 95.6 us -> 87.8 us  [attention_backward(): pl.pallas_call(functools.partial(backward_kernel, parts), out_shape=(grad...]
    unnamed x87, local copies, waits for them, and re-layouts: 9.84 us -> 5.94 us
  transfers between devices with their start and end apart: 4 -> 5, of which waited for: 2 -> 2; matrix products, arithmetic and copies ran while one was open for 9% -> 11% of each run, Pallas kernels for 52% -> 72%
where the time goes in v7:
time: 361 us
  Pallas kernels  274 us (76%)
  matrix products  32.1 us (9%)
  other arithmetic  21.5 us (6%)
  local copies, waits for them, and re-layouts  17.4 us (5%)
  between operations  14.6 us (4%)
    pallas_call x7, Pallas kernels, exchange(): pl.pallas_call(functools.partial(exchange_kernel, parts), out_shape=tuple...  118 us
    pallas_call x1, Pallas kernels, attention_backward(): pl.pallas_call(functools.partial(backward_kernel, parts), out_shape=(grad...  87.8 us
    pallas_call x1, Pallas kernels, attention_forward(): pl.pallas_call(forward_kernel, out_shape=(jax.ShapeDtypeStruct((SEG, D, T...  68.9 us
    dot_general x8, matrix products, product(): return jnp.einsum(spec, a, b, preferred_element_type=f32)  19.7 us
    dot_general x5, matrix products, dot(): return jnp.dot(a, b, preferred_element_type=f32)  12.5 us
  transfers between devices with their start and end apart: 5, of which 2 were waited for; matrix products, arithmetic and copies ran while one was open for 11% of the time, Pallas kernels for 72%

profile of v7, /device:TPU:1, one launch (start us, length us, event | category | flops | bytes accessed | tf_op | source)
XLA Modules:
  0.0 361.0 jit_solution(8370559210791717000)
XLA Ops:
  7.3 2.7 fusion.51
  10.0 1.1 convert_reduce_fusion
  11.1 1.2 fusion.44
  12.8 1.9 fusion.38
  14.8 2.1 fusion.26
  17.1 2.9 fusion.5
  20.7 19.1 %shard_map.245 = bf16[16,192,128]{2,1,0:T(8,128)(2,1)S(1)} custom-call(bf16[16,192,128]{2,1,0:T(8,128)(2,1)S(1)} %pad_maximum_fusion.1.refs_0_), custom_call_target="tpu_custom_call" | custom-call | flops 12000000000 | bytes 4194304 | tf_op jit(solution)/shard_map/pallas_call | solution.py:223
  40.0 68.9 %shard_map.246 = (bf16[16,64,128]{2,1,0:T(8,128)(2,1)S(1)}, f32[8,1,256]{2,1,0:T(1,128)S(1)}, bf16[8,16,128,128]{3,2,1,0:T(8,128)(2,1)S(1)}) custom-call(bf16[16,64,128]{2,1,0:T(8,128)(2,1)S(1)} %slice.70.q_ref, bf16[16,128,128]{2,1,0:T(8,128)(2,1)S(1)} %slice.71.own_ref), custom_call_target="tpu_custom_call" | custom-call | flops 70000001024 | bytes 5242880 | tf_op jit(solution)/shard_map/pallas_call | solution.py:315
  109.0 12.2 %shard_map.247 = bf16[16,64,128]{2,1,0:T(8,128)(2,1)S(1)} custom-call(bf16[16,64,128]{2,1,0:T(8,128)(2,1)S(1)} %get-tuple-element.42.refs_0_.ctx_ref), custom_call_target="tpu_custom_call" | custom-call | flops 12000000000 | bytes 4194304 | tf_op jit(solution)/shard_map/pallas_call | solution.py:223
  122.7 15.3 %shard_map.248 = bf16[4,128,1024]{2,1,0:T(8,128)(2,1)S(1)} custom-call(bf16[128,1024]{1,0:T(8,128)(2,1)S(1)} %add_convert_fusion.refs_0_), custom_call_target="tpu_custom_call" | custom-call | flops 12000000000 | bytes 4194304 | tf_op jit(solution)/shard_map/pallas_call | solution.py:223
  138.0 1.3 fusion.54
  139.3 1.3 copy-done.39
  140.6 2.6 convolution_convert_fusion.3
  143.2 4.4 %fusion.53 = (f32[1024]{0:T(1024)S(1)}, bf16[512,1024]{1,0:T(8,128)(2,1)S(1)}) fusion(f32[512,1024]{1,0:T(8,128)} %copy-done.39, f32[1024]{0:T(1024)S(1)} %copy-done.38, bf16[512,1024]{1,0:T(8,128)(2,1)} %all-gather.4.cloned.1.call-done, bf16[1024,1024]{1,0:T(8,128)(2,1)S(1)} %copy-done), kind=kOutput, calls=%fused_computation.101 | convolution fusion | flops 1084750848 | bytes 6299648 | tf_op jit(solution)/shard_map/dot_general | solution.py:58
  147.6 3.0 convolution_convert_fusion
  150.6 2.7 convolution_convert_fusion.1
  153.3 1.3 convolution_convert_fusion.2
  154.9 2.7 pad_maximum_fusion
  157.5 24.8 %shard_map.249 = (f32[128,1024]{1,0:T(8,128)S(1)}, bf16[1024,1024]{1,0:T(8,128)(2,1)}, f32[2,8,128]{2,1,0:T(8,128)S(1)}) custom-call(bf16[4,128,1024]{2,1,0:T(8,128)(2,1)S(1)} %bitcast.97, bf16[2,1024,1024]{2,1,0:T(8,128)(2,1)S(1)} %bitcast.88, f32[8,128]{1,0:T(8,128)S(1)} %bitcast.100), custom_call_target="tpu_custom_call" | custom-call | flops 12000000000 | bytes 4194304 | tf_op jit(solution)/shard_map/pallas_call | solution.py:223
  182.7 1.5 fusion.49
  185.2 11.2 %shard_map.250.do_ref = bf16[16,64,128]{2,1,0:T(8,128)(2,1)S(1)} custom-call(bf16[16,64,128]{2,1,0:T(8,128)(2,1)S(1)} %bitcast.96), custom_call_target="tpu_custom_call" | custom-call | flops 12000000000 | bytes 4194304 | tf_op jit(solution)/shard_map/pallas_call | solution.py:223
  199.1 87.8 %shard_map.251 = (bf16[16,192,128]{2,1,0:T(8,128)(2,1)S(1)}, bf16[4,128,1024]{2,1,0:T(8,128)(2,1)S(1)}, bf16[4,256,128]{2,1,0:T(8,128)(2,1)S(1)}, bf16[2,1024,10...) custom-call(bf16[16,64,128]{2,1,0:T(8,128)(2,1)S(1)} %slice.70.q_ref, ...), custom_call_target="tpu_custom_call" | custom-call | flops 80000000000 | bytes 10485760 | tf_op jit(solution)/shard_map/pallas_call | solution.py:435
  289.4 1.4 fusion.18.refs_1_
  291.3 5.9 %fusion.43 = (bf16[1024]{0:T(1024)(128)(2,1)S(1)}, f32[128]{0:T(128)S(1)}, f32[128]{0:T(128)S(1)}, bf16[1024]{0:T(1024)(128)(2,1)S(1)}, f32[128,1024]{1,0:T(8,128)}) fusion(bf16[128,1024]{1,0:T(8,128)(2,1)S(1)} %copy-done.13, f32[128]{0:T(128)S(1)} %copy-done.31, f32[128]{0:T(128)S(1)} %copy-done.29, f32[1024]{0:T(1024)S(1)} %copy-done.24, ...), kind=kOutput, calls=%fused_computation.51 | convolution fusion | flops 806614784 | bytes 7874560 | tf_op jit(solution)/shard_map/ft,df->td/dot_general | solution.py:62
  298.0 3.3 fusion.17
  302.3 20.0 %shard_map.252 = (bf16[16,16,128]{2,1,0:T(8,128)(2,1)S(1)}, bf16[8,1024]{1,0:T(8,128)(2,1)S(1)}) custom-call(bf16[8,16,16,128]{3,2,1,0:T(8,128)(2,1)S(1)} %fusion.45.refs_0_, bf16[32,8,1024]{2,1,0:T(8,128)(2,1)S(1)} %fusion.18.refs_1_), custom_call_target="tpu_custom_call" | custom-call | flops 12000000000 | bytes 4194304 | tf_op jit(solution)/shard_map/pallas_call | solution.py:223
  322.3 15.1 %shard_map.253 = (bf16[64,16,128]{2,1,0:T(8,128)(2,1)S(1)}, bf16[4,8,1024]{2,1,0:T(8,128)(2,1)S(1)}) custom-call(bf16[16,16,128]{2,1,0:T(8,128)(2,1)S(1)} %get-tuple-element.62.refs_0_, bf16[8,1024]{1,0:T(8,128)(2,1)S(1)} %get-tuple-element.63.refs_1_), custom_call_target="tpu_custom_call" | custom-call | flops 12000000000 | bytes 4194304 | tf_op jit(solution)/shard_map/pallas_call | solution.py:223
  342.4 1.0 reshape.222
  345.5 1.0 fusion.42
  346.5 2.7 fusion.50
  349.2 2.6 bitcast_convert_fusion
  351.8 2.6 bitcast_convert_fusion.1
  (165 shorter events, 18.9 us)
Async XLA Ops:
  7.2 133.4 %copy-start = (bf16[1024,1024]{1,0:T(8,128)(2,1)S(1)}, bf16[1024,1024]{1,0:T(8,128)(2,1)}, u32[]{:S(2)}) copy-start(bf16[1024,1024]{1,0:T(8,128)(2,1)} %param.25) | copy-start | bytes 6291460
  7.2 7.6 %copy-start.27 = (f32[2,1024]{1,0:T(2,128)S(1)}, f32[2,1024]{1,0:T(2,128)}, u32[]{:S(2)}) copy-start(f32[2,1024]{1,0:T(2,128)} %param.18) | copy-start | bytes 24580
  7.2 32.7 %all-gather.4.cloned.1.call-start = ((), (), s32[]{:S(2)}) async-start(), calls=%async_computation.2 | async-start | bytes 1310720 | tf_op jit(solution)/shard_map/all_gather | solution.py:482
  10.0 112.2 %all-gather.6.cloned.1.call-start = ((), (), s32[]{:S(2)}) async-start(), calls=%async_computation.3 | async-start | bytes 2359296 | tf_op jit(solution)/shard_map/all_gather | solution.py:498
  14.7 2.4 copy-start.20
  14.7 272.9 %reduce-scatter.5.cloned.1.call-start = ((), (), s32[]{:S(2)}) async-start(), calls=%async_computation.5 | async-start | bytes 1310720 | tf_op jit(solution)/shard_map/reduce_scatter | solution.py:521
  108.9 12.3 %copy-start.5 = (bf16[16,64,128]{2,1,0:T(8,128)(2,1)}, bf16[16,64,128]{2,1,0:T(8,128)(2,1)S(1)}, u32[]{:S(2)}) copy-start(bf16[16,64,128]{2,1,0:T(8,128)(2,1)S(1)} %get-tuple-element.42.refs_0_.ctx_ref) | copy-start | bytes 786436
  108.9 12.3 %copy-start.9 = (bf16[8,16,128,128]{3,2,1,0:T(8,128)(2,1)}, bf16[8,16,128,128]{3,2,1,0:T(8,128)(2,1)S(1)}, u32[]{:S(2)}) copy-start(bf16[8,16,128,128]{3,2,1,0:T(8,128)(2,1)S(1)} %get-tuple-element.44.kv_ref) | copy-start | bytes 12582916
  108.9 12.3 %copy-start.12 = (bf16[128,1024]{1,0:T(8,128)(2,1)S(1)}, bf16[128,1024]{1,0:T(8,128)(2,1)}, u32[]{:S(2)}) copy-start(bf16[128,1024]{1,0:T(8,128)(2,1)} %param.14) | copy-start | bytes 786436
  108.9 12.3 %copy-start.15 = (bf16[1024,1024]{1,0:T(8,128)(2,1)S(1)}, bf16[1024,1024]{1,0:T(8,128)(2,1)}, u32[]{:S(2)}) copy-start(bf16[1024,1024]{1,0:T(8,128)(2,1)} %param.19) | copy-start | bytes 6291460
  108.9 12.3 %copy-start.32 = (f32[1024]{0:T(1024)S(1)}, f32[1024]{0:T(1024)}, u32[]{:S(2)}) copy-start(f32[1024]{0:T(1024)} %param.20) | copy-start | bytes 12292
  121.8 60.9 %copy-start.10 = (f32[128,1024]{1,0:T(8,128)}, f32[128,1024]{1,0:T(8,128)S(1)}, u32[]{:S(2)}) copy-start(f32[128,1024]{1,0:T(8,128)S(1)} %fusion.22) | copy-start | bytes 1572868
  122.6 15.3 %copy-start.35 = (bf16[1024,1024]{1,0:T(8,128)(2,1)S(1)}, bf16[1024,1024]{1,0:T(8,128)(2,1)}, u32[]{:S(2)}) copy-start(bf16[1024,1024]{1,0:T(8,128)(2,1)} %param.23) | copy-start | bytes 6291460
  138.0 2.6 copy-start.38
  143.2 4.5 %copy-start.37 = (bf16[512,1024]{1,0:T(8,128)(2,1)S(1)}, bf16[512,1024]{1,0:T(8,128)(2,1)}, u32[]{:S(2)}) copy-start(bf16[512,1024]{1,0:T(8,128)(2,1)} %all-gather.4.cloned.1.call-done) | copy-start | bytes 3145732
  143.2 4.5 %copy-start.40 = (f32[512,1024]{1,0:T(8,128)S(1)}, f32[512,1024]{1,0:T(8,128)}, u32[]{:S(2)}) copy-start(f32[512,1024]{1,0:T(8,128)} %copy-done.39) | copy-start | bytes 6291460
  147.6 3.0 copy-start.4
  150.6 2.7 copy-start.36
  154.6 133.0 %reduce-scatter.3.cloned.1.call-start = ((), (), s32[]{:S(2)}) async-start(), calls=%async_computation.4 | async-start | bytes 2228224 | tf_op jit(solution)/shard_map/reduce_scatter | solution.py:528
  182.4 1.8 copy-start.16
  184.1 12.3 %copy-start.17 = (f32[128,1024]{1,0:T(8,128)}, f32[128,1024]{1,0:T(8,128)S(1)}, u32[]{:S(2)}) copy-start(f32[128,1024]{1,0:T(8,128)S(1)} %get-tuple-element.85) | copy-start | bytes 1572868
  196.5 150.0 %all-gather.8.cloned.1.call-start = ((), (), s32[]{:S(2)}) async-start(), calls=%async_computation.6 | async-start | bytes 4325376 | tf_op jit(solution)/shard_map/all_gather | solution.py:559
  199.1 88.6 %copy-start.26 = (bf16[1024]{0:T(1024)(128)(2,1)S(1)}, bf16[1024]{0:T(1024)(128)(2,1)}, u32[]{:S(2)}) copy-start(bf16[1024]{0:T(1024)(128)(2,1)} %get-tuple-element.88) | copy-start | bytes 6148
  289.4 1.8 copy-start.31
  291.3 6.1 %copy-start.22 = (bf16[6,16,8,8]{3,2,1,0:T(8,128)(2,1)S(1)}, bf16[6,16,8,8]{3,2,1,0:T(8,128)(2,1)}, u32[]{:S(2)}) copy-start(bf16[6,16,8,8]{3,2,1,0:T(8,128)(2,1)} %copy-done.21) | copy-start | bytes 36868
  341.4 3.2 copy-start.11
  341.4 3.2 copy-start.23
  341.4 3.2 copy-start.34
  341.8 3.6 %copy-start.14 = (bf16[128,1024]{1,0:T(8,128)(2,1)S(1)}, bf16[128,1024]{1,0:T(8,128)(2,1)}, u32[]{:S(2)}) copy-start(bf16[128,1024]{1,0:T(8,128)(2,1)} %param.14) | copy-start | bytes 786436
  341.9 3.6 %copy-start.18 = (f32[128,1024]{1,0:T(8,128)S(1)}, f32[128,1024]{1,0:T(8,128)}, u32[]{:S(2)}) copy-start(f32[128,1024]{1,0:T(8,128)} %copy-done.17) | copy-start | bytes 1572868
  342.3 3.1 copy-start.19
  351.8 2.6 copy-start.1
  (14 other events, 16.1 us)
Sparse Core Ops, SparseCore 0:
  10.3 26.2 all-gather.3
  39.5 82.5 all-gather.5
  154.7 29.0 reduce-scatter.4
  196.6 90.9 reduce-scatter.2
  289.8 53.1 all-gather.7

commit v8 on v7

--- a/solution.py
+++ b/solution.py
@@ -516,9 +516,6 @@
         ]
     ).astype(bf16)
     norm_parts = dot(hidden_grad_bf, fc_weight.T).astype(bf16).reshape(-1, tokens, width)
-    mlp_parts = dot(activation, proj_weight).astype(bf16)
-    mlp_parts, norm_parts = lax.optimization_barrier((mlp_parts, norm_parts))
-    mlp_out = lax.psum_scatter(mlp_parts, "tp", scatter_dimension=0, tiled=True)
     normed_two_grad, wide_core, bias_pair = exchange(
         5,
         (norm_parts, ("tp",), "reduce", f32),
@@ -552,10 +549,9 @@
         (normed_core, ("sc",), "gather"),
         (jnp.sum(bias_pair, axis=0), HEAD_AXES, "gather", f32),
     )
-    head_grads, normed_all, token_grads, wide_part, mlp_out = lax.optimization_barrier(
-        (head_grads, normed_all, token_grads, wide_part, mlp_out)
-    )
-    block_out = residual + mlp_out.astype(f32) + proj_bias
+    head_grads, normed_all, token_grads, wide_part, activation = lax.optimization_barrier(
+        (head_grads, normed_all, token_grads, wide_part, activation)
+    )
     wide_sum = lax.all_gather(wide_part, ROW_AXES, axis=0, tiled=True)
     wide_sum = wide_sum.reshape(-1, 2, width // 4, width)
     token_grads = token_grads.reshape(SEG, 3, D, tokens).transpose(1, 0, 2, 3)
@@ -593,11 +589,14 @@
         axis=2,
     )
     out_part = product("gct,gtd->cd", context_tokens, grad_tokens).astype(bf16)
-    summed, out_rows = exchange(
+    mlp_parts = dot(activation, proj_weight).astype(bf16).reshape(-1, tokens, width)
+    summed, out_rows, mlp_out = exchange(
         7,
         (packed, KEY_AXES, "reduce"),
         (out_part.reshape(row_groups, fine, width), ROW_AXES, "reduce"),
-    )
+        (mlp_parts, ("tp",), "reduce", f32),
+    )
+    block_out = residual + mlp_out + proj_bias
     fc_bias_grad = jnp.sum(bias_parts, axis=0).reshape(-1)
     moved, out_rows = exchange(
         8,

time: 361 us -> 350 us (0.970)
  matrix products: 32.1 us -> 27.5 us
  Pallas kernels: 274 us -> 270 us
  transfers between devices with their start and end apart: 5 -> 4, of which waited for: 2 -> 1; matrix products, arithmetic and copies ran while one was open for 11% -> 11% of each run, Pallas kernels for 72% -> 68%
where the time goes in v8:
time: 350 us; the launch traced here: 349 us
  Pallas kernels  270 us (77%)
  matrix products  27.5 us (8%)
  local copies, waits for them, and re-layouts  18.2 us (5%)
  other arithmetic  18.1 us (5%)
  between operations  14.7 us (4%)
    pallas_call x7, Pallas kernels, exchange(): pl.pallas_call(functools.partial(exchange_kernel, parts), out_shape=tuple...  114 us
    pallas_call x1, Pallas kernels, attention_backward(): pl.pallas_call(functools.partial(backward_kernel, parts), out_shape=(grad...  87 us
    pallas_call x1, Pallas kernels, attention_forward(): pl.pallas_call(forward_kernel, out_shape=(jax.ShapeDtypeStruct((SEG, D, T...  68.9 us
    dot_general x8, matrix products, product(): return jnp.einsum(spec, a, b, preferred_element_type=f32)  16.6 us
    dot_general x5, matrix products, dot(): return jnp.dot(a, b, preferred_element_type=f32)  10.8 us
  transfers between devices with their start and end apart: 4, of which 1 were waited for; matrix products, arithmetic and copies ran while one was open for 11% of the time, Pallas kernels for 68%

profile of v8, /device:TPU:1, one launch (start us, length us, event | category | flops | bytes accessed | tf_op | source)
XLA Modules:
  0.0 349.2 jit_solution(2060640964322684712)
XLA Ops:
  7.3 2.7 fusion.51
  10.0 1.1 convert_reduce_fusion
  11.1 1.2 fusion.44
  12.8 1.9 fusion.38
  14.8 2.1 fusion.26
  17.1 2.9 fusion.5
  20.7 19.1 %shard_map.245 = bf16[16,192,128]{2,1,0:T(8,128)(2,1)S(1)} custom-call(bf16[16,192,128]{2,1,0:T(8,128)(2,1)S(1)} %pad_maximum_fusion.1.refs_0_), custom_call_target="tpu_custom_call" | custom-call | flops 12000000000 | bytes 4194304 | tf_op jit(solution)/shard_map/pallas_call | solution.py:223
  40.0 68.9 %shard_map.246 = (bf16[16,64,128]{2,1,0:T(8,128)(2,1)S(1)}, f32[8,1,256]{2,1,0:T(1,128)S(1)}, bf16[8,16,128,128]{3,2,1,0:T(8,128)(2,1)S(1)}) custom-call(bf16[16,64,128]{2,1,0:T(8,128)(2,1)S(1)} %slice.70.q_ref, bf16[16,128,128]{2,1,0:T(8,128)(2,1)S(1)} %slice.71.own_ref), custom_call_target="tpu_custom_call" | custom-call | flops 70000001024 | bytes 5242880 | tf_op jit(solution)/shard_map/pallas_call | solution.py:315
  109.0 12.2 %shard_map.247 = bf16[16,64,128]{2,1,0:T(8,128)(2,1)S(1)} custom-call(bf16[16,64,128]{2,1,0:T(8,128)(2,1)S(1)} %get-tuple-element.41.refs_0_.ctx_ref), custom_call_target="tpu_custom_call" | custom-call | flops 12000000000 | bytes 4194304 | tf_op jit(solution)/shard_map/pallas_call | solution.py:223
  122.7 15.3 %shard_map.248 = bf16[4,128,1024]{2,1,0:T(8,128)(2,1)S(1)} custom-call(bf16[128,1024]{1,0:T(8,128)(2,1)S(1)} %add_convert_fusion.refs_0_), custom_call_target="tpu_custom_call" | custom-call | flops 12000000000 | bytes 4194304 | tf_op jit(solution)/shard_map/pallas_call | solution.py:223
  138.0 1.7 multiply_convert_fusion
  139.8 2.4 fusion.53
  142.3 1.3 convolution_convert_fusion.1
  143.6 1.3 convolution_convert_fusion.3
  144.8 1.3 convolution_convert_fusion
  146.6 17.5 %shard_map.249 = (f32[128,1024]{1,0:T(8,128)S(1)}, bf16[1024,1024]{1,0:T(8,128)(2,1)}, f32[2,8,128]{2,1,0:T(8,128)S(1)}) custom-call(bf16[4,128,1024]{2,1,0:T(8,128)(2,1)S(1)} %bitcast.100, bf16[2,1024,1024]{2,1,0:T(8,128)(2,1)S(1)} %bitcast.91, f32[8,128]{1,0:T(8,128)S(1)} %bitcast.104), custom_call_target="tpu_custom_call" | custom-call | flops 12000000000 | bytes 4194304 | tf_op jit(solution)/shard_map/pallas_call | solution.py:223
  167.1 10.7 %shard_map.250.do_ref = bf16[16,64,128]{2,1,0:T(8,128)(2,1)S(1)} custom-call(bf16[16,64,128]{2,1,0:T(8,128)(2,1)S(1)} %bitcast.99), custom_call_target="tpu_custom_call" | custom-call | flops 12000000000 | bytes 4194304 | tf_op jit(solution)/shard_map/pallas_call | solution.py:223
  177.8 87.0 %shard_map.251 = (bf16[16,192,128]{2,1,0:T(8,128)(2,1)S(1)}, bf16[4,128,1024]{2,1,0:T(8,128)(2,1)S(1)}, bf16[4,256,128]{2,1,0:T(8,128)(2,1)S(1)}, bf16[2,1024,10...) custom-call(bf16[16,64,128]{2,1,0:T(8,128)(2,1)S(1)} %slice.70.q_ref, ...), custom_call_target="tpu_custom_call" | custom-call | flops 80000000000 | bytes 10485760 | tf_op jit(solution)/shard_map/pallas_call | solution.py:435
  267.3 1.4 fusion.18.refs_1_
  269.2 6.0 %fusion.40 = (f32[128]{0:T(128)S(1)}, bf16[1024]{0:T(1024)(128)(2,1)S(1)}, f32[128]{0:T(128)S(1)}, bf16[1024]{0:T(1024)(128)(2,1)S(1)}, f32[128,1024]{1,0:T(8,128)}) fusion(bf16[128,1024]{1,0:T(8,128)(2,1)S(1)} %copy-done.9, f32[1024]{0:T(1024)S(1)} %copy-done.20, f32[128]{0:T(128)S(1)} %copy-done.27, f32[128]{0:T(128)S(1)} %copy-done.25, ...), kind=kOutput, calls=%fused_computation.48 | convolution fusion | flops 806614784 | bytes 7874560 | tf_op jit(solution)/shard_map/ft,df->td/dot_general | solution.py:62
  276.0 3.2 fusion.17
  280.2 1.3 copy-done.32
  281.5 2.5 convolution_convert_fusion.2
  284.0 24.7 %shard_map.252 = (bf16[16,16,128]{2,1,0:T(8,128)(2,1)S(1)}, bf16[8,1024]{1,0:T(8,128)(2,1)S(1)}, f32[128,1024]{1,0:T(8,128)S(1)}) custom-call(bf16[8,16,16,128]{3,2,1,0:T(8,128)(2,1)S(1)} %fusion.45.refs_0_, bf16[32,8,1024]{2,1,0:T(8,128)(2,1)S(1)} %fusion.18.refs_1_, bf16[4,128,1024]{2,1,0:T(8,128)(2,1)S(1)} %bitcast.103), custom_call_target="tpu_custom_call" | custom-call | flops 12000000000 | bytes 4194304 | tf_op jit(solution)/shard_map/pallas_call | solution.py:223
  308.7 14.6 %shard_map.253 = (bf16[64,16,128]{2,1,0:T(8,128)(2,1)S(1)}, bf16[4,8,1024]{2,1,0:T(8,128)(2,1)S(1)}) custom-call(bf16[16,16,128]{2,1,0:T(8,128)(2,1)S(1)} %get-tuple-element.60.refs_0_, bf16[8,1024]{1,0:T(8,128)(2,1)S(1)} %get-tuple-element.61.refs_1_), custom_call_target="tpu_custom_call" | custom-call | flops 12000000000 | bytes 4194304 | tf_op jit(solution)/shard_map/pallas_call | solution.py:223
  328.1 1.3 copy.58
  329.5 2.1 reshape.226
  332.8 0.9 add_add_fusion
  333.7 1.0 fusion.43
  334.8 2.7 fusion.50
  337.5 2.6 bitcast_convert_fusion
  340.1 2.6 bitcast_convert_fusion.1
  (152 shorter events, 17.0 us)
Async XLA Ops:
  7.2 130.8 %copy-start = (bf16[1024,1024]{1,0:T(8,128)(2,1)S(1)}, bf16[1024,1024]{1,0:T(8,128)(2,1)}, u32[]{:S(2)}) copy-start(bf16[1024,1024]{1,0:T(8,128)(2,1)} %param.23) | copy-start | bytes 6291460
  7.2 7.6 %copy-start.23 = (f32[2,1024]{1,0:T(2,128)S(1)}, f32[2,1024]{1,0:T(2,128)}, u32[]{:S(2)}) copy-start(f32[2,1024]{1,0:T(2,128)} %param.18) | copy-start | bytes 24580
  7.2 32.7 %all-gather.4.cloned.1.call-start = ((), (), s32[]{:S(2)}) async-start(), calls=%async_computation.1 | async-start | bytes 1310720 | tf_op jit(solution)/shard_map/all_gather | solution.py:482
  10.0 112.2 %all-gather.6.cloned.1.call-start = ((), (), s32[]{:S(2)}) async-start(), calls=%async_computation.2 | async-start | bytes 2359296 | tf_op jit(solution)/shard_map/all_gather | solution.py:498
  14.7 2.4 copy-start.17
  14.7 250.8 %reduce-scatter.2.cloned.1.call-start = ((), (), s32[]{:S(2)}) async-start(), calls=%async_computation.3 | async-start | bytes 2228224 | tf_op jit(solution)/shard_map/reduce_scatter | solution.py:525
  108.9 12.3 %copy-start.3 = (bf16[16,64,128]{2,1,0:T(8,128)(2,1)}, bf16[16,64,128]{2,1,0:T(8,128)(2,1)S(1)}, u32[]{:S(2)}) copy-start(bf16[16,64,128]{2,1,0:T(8,128)(2,1)S(1)} %get-tuple-element.41.refs_0_.ctx_ref) | copy-start | bytes 786436
  108.9 12.3 %copy-start.5 = (bf16[8,16,128,128]{3,2,1,0:T(8,128)(2,1)}, bf16[8,16,128,128]{3,2,1,0:T(8,128)(2,1)S(1)}, u32[]{:S(2)}) copy-start(bf16[8,16,128,128]{3,2,1,0:T(8,128)(2,1)S(1)} %get-tuple-element.43.kv_ref) | copy-start | bytes 12582916
  108.9 12.3 %copy-start.8 = (bf16[128,1024]{1,0:T(8,128)(2,1)S(1)}, bf16[128,1024]{1,0:T(8,128)(2,1)}, u32[]{:S(2)}) copy-start(bf16[128,1024]{1,0:T(8,128)(2,1)} %param.14) | copy-start | bytes 786436
  108.9 12.3 %copy-start.11 = (bf16[1024,1024]{1,0:T(8,128)(2,1)S(1)}, bf16[1024,1024]{1,0:T(8,128)(2,1)}, u32[]{:S(2)}) copy-start(bf16[1024,1024]{1,0:T(8,128)(2,1)} %param.19) | copy-start | bytes 6291460
  108.9 12.3 %copy-start.28 = (f32[1024]{0:T(1024)S(1)}, f32[1024]{0:T(1024)}, u32[]{:S(2)}) copy-start(f32[1024]{0:T(1024)} %param.20) | copy-start | bytes 12292
  121.8 42.9 %copy-start.6 = (f32[128,1024]{1,0:T(8,128)}, f32[128,1024]{1,0:T(8,128)S(1)}, u32[]{:S(2)}) copy-start(f32[128,1024]{1,0:T(8,128)S(1)} %fusion.22) | copy-start | bytes 1572868
  122.6 15.3 %copy-start.34 = (f32[1024]{0:T(1024)S(1)}, f32[1024]{0:T(1024)}, u32[]{:S(2)}) copy-start(f32[1024]{0:T(1024)} %param.24) | copy-start | bytes 12292
  138.0 1.8 copy-start.31
  138.0 1.8 copy-start.33
  139.7 5.1 %copy-start.35 = (bf16[512,1024]{1,0:T(8,128)(2,1)}, bf16[512,1024]{1,0:T(8,128)(2,1)S(1)}, u32[]{:S(2)}) copy-start(bf16[512,1024]{1,0:T(8,128)(2,1)S(1)} %get-tuple-element.58) | copy-start | bytes 3145732
  164.1 170.6 %all-gather.8.cloned.1.call-start = ((), (), s32[]{:S(2)}) async-start(), calls=%async_computation.4 | async-start | bytes 4325376 | tf_op jit(solution)/shard_map/all_gather | solution.py:555
  164.4 1.6 copy-start.12
  165.4 12.4 %copy-start.13 = (f32[128,1024]{1,0:T(8,128)}, f32[128,1024]{1,0:T(8,128)S(1)}, u32[]{:S(2)}) copy-start(f32[128,1024]{1,0:T(8,128)S(1)} %get-tuple-element.83) | copy-start | bytes 1572868
  167.1 10.7 %copy-start.4 = (bf16[16,64,128]{2,1,0:T(8,128)(2,1)S(1)}, bf16[16,64,128]{2,1,0:T(8,128)(2,1)}, u32[]{:S(2)}) copy-start(bf16[16,64,128]{2,1,0:T(8,128)(2,1)} %copy-done.3) | copy-start | bytes 786436
  177.8 87.8 %copy-start.22 = (bf16[1024]{0:T(1024)(128)(2,1)S(1)}, bf16[1024]{0:T(1024)(128)(2,1)}, u32[]{:S(2)}) copy-start(bf16[1024]{0:T(1024)(128)(2,1)} %get-tuple-element.86) | copy-start | bytes 6148
  267.3 1.8 copy-start.9
  267.3 1.8 copy-start.20
  267.3 1.8 copy-start.25
  267.3 1.8 copy-start.27
  269.2 6.2 %copy-start.19 = (bf16[6,16,8,8]{3,2,1,0:T(8,128)(2,1)S(1)}, bf16[6,16,8,8]{3,2,1,0:T(8,128)(2,1)}, u32[]{:S(2)}) copy-start(bf16[6,16,8,8]{3,2,1,0:T(8,128)(2,1)} %copy-done.18) | copy-start | bytes 36868
  327.4 5.5 %copy-start.7 = (f32[128,1024]{1,0:T(8,128)S(1)}, f32[128,1024]{1,0:T(8,128)}, u32[]{:S(2)}) copy-start(f32[128,1024]{1,0:T(8,128)} %copy-done.6) | copy-start | bytes 1572868
  327.4 5.5 %copy-start.30 = (f32[1024]{0:T(1024)S(1)}, f32[1024]{0:T(1024)}, u32[]{:S(2)}) copy-start(f32[1024]{0:T(1024)} %param.26) | copy-start | bytes 12292
  328.1 5.6 %copy-start.10 = (bf16[128,1024]{1,0:T(8,128)(2,1)S(1)}, bf16[128,1024]{1,0:T(8,128)(2,1)}, u32[]{:S(2)}) copy-start(bf16[128,1024]{1,0:T(8,128)(2,1)} %param.14) | copy-start | bytes 786436
  328.1 5.6 %copy-start.14 = (f32[128,1024]{1,0:T(8,128)S(1)}, f32[128,1024]{1,0:T(8,128)}, u32[]{:S(2)}) copy-start(f32[128,1024]{1,0:T(8,128)} %copy-done.13) | copy-start | bytes 1572868
  328.1 5.6 %copy-start.15 = (f32[128,1024]{1,0:T(8,128)S(1)}, f32[128,1024]{1,0:T(8,128)}, u32[]{:S(2)}) copy-start(f32[128,1024]{1,0:T(8,128)} %get-tuple-element.94) | copy-start | bytes 1572868
  340.1 2.6 copy-start.1
  (8 other events, 8.1 us)
Sparse Core Ops, SparseCore 0:
  10.3 26.2 all-gather.3
  39.5 82.5 all-gather.5
  164.3 86.2 reduce-scatter.1
  265.7 47.0 all-gather.7
